TPU v7x, 1024 devices: a whole 8x8x8 slice. The times are simulated.
1024 devices in a mesh: grp: 64 (over z, x), mem: 16 (over y, core).
Axes of the slice: x: 8, y: 8, z: 8, core: 2. Of those that a mesh axis runs over, the one named last changes fastest.
Arguments:
- state: float32 [3, 4096, 16, 128], P(None, ('grp', 'mem')), may hold values from -0.18 to 0.18
- direction: float32 [3, 4096, 16, 128], P(None, ('grp', 'mem')), may hold values from -0.6 to 0.6
- rhs: float32 [3, 4096, 16, 128], P(None, ('grp', 'mem')), may hold values from -6 to 6
- clamp: int32 [4096, 16], P(('grp', 'mem')), may hold values 0 or 1
- stiffness: float32 [1024, 4, 32], P(('grp', 'mem')), may hold values from 0.5 to 5
- coarse_owner: int32 [1024, 128], P(('grp', 'mem')), may hold values from 0 to 127, as said below
- coarse_inverse: float32 [1024, 2, 192, 192], P(('grp', 'mem')), may hold values from -0.006 to 0.006
Outputs:
- new_direction: float32 [3, 4096, 16, 128], P(None, ('grp', 'mem'))
- residual: float32 [3, 4096, 16, 128], P(None, ('grp', 'mem'))
- coarse_residual: float32 [3, 1024, 4, 32], P(None, ('grp', 'mem'))
Inputs may be any that keep to these rules, and one draw needn't show every extreme that they name: `coarse_owner`: each layer's row is a permutation of 0 to 127.
All inputs are finite; a program needn't handle non-finite values. No bound on the sum of `clamp` on one device may be relied on, other than what follows from the above.
Results may differ from a plain program's by a relative error of at most 0.0003.
Values sent between devices are 32-bit elements; how exact they have to be, the bound alone decides.
No kernel may reach another device: no remote copies, remote signals or barrier semaphores. Data moves between devices by JAX's collectives and lax.ppermute only.
A program may use at most 32 MiB of HBM per device.

v0:
```python
import jax
import jax.numpy as jnp
import numpy as np
from jax import lax
from jax.sharding import PartitionSpec as P

LAME_FIRST = 1.2
LAME_SHEAR = 0.8
HIGHEST = lax.Precision.HIGHEST


def shifted(block, axis, distance):
    devices = range(lax.axis_size(axis))
    route = [(i - distance, i) for i in devices if i - distance in devices]
    return lax.ppermute(block, axis, route)


def gauss_rule():
    inner = np.sqrt(5.0 - 2.0 * np.sqrt(10.0 / 7.0)) / 3.0
    outer = np.sqrt(5.0 + 2.0 * np.sqrt(10.0 / 7.0)) / 3.0
    inner_weight = (322.0 + 13.0 * np.sqrt(70.0)) / 900.0
    outer_weight = (322.0 - 13.0 * np.sqrt(70.0)) / 900.0
    points = np.array([-outer, -inner, 0.0, inner, outer])
    weights = np.array([outer_weight, inner_weight, 128.0 / 225.0, inner_weight, outer_weight])
    return (points, weights)


def basis_tables():
    gll_points = np.array([-1.0, -np.sqrt(3.0 / 7.0), 0.0, np.sqrt(3.0 / 7.0), 1.0])
    gauss_points, gauss_weights = gauss_rule()
    values = np.zeros((5, 5))
    slopes = np.zeros((5, 5))
    for j in range(5):
        others = [gll_points[k] for k in range(5) if k != j]
        denominator = np.prod([gll_points[j] - o for o in others])
        for q in range(5):
            t = gauss_points[q]
            values[q, j] = np.prod([t - o for o in others]) / denominator
            total = 0.0
            for i in range(4):
                total += np.prod([t - others[k] for k in range(4) if k != i])
            slopes[q, j] = 2.0 * total / denominator
    return (gll_points, gauss_weights, values, slopes)


def banded(table, count):
    banded_matrix = np.zeros((5 * count, 4 * count + 1))
    for e in range(count):
        banded_matrix[5 * e : 5 * e + 5, 4 * e : 4 * e + 5] = table
    return banded_matrix


def restrictor(gll_points, count):
    result = np.zeros((count, 4 * count))
    for e in range(count):
        for j in range(4):
            result[e, 4 * e + j] += (1.0 - gll_points[j]) / 2.0
            if e + 1 < count:
                result[e + 1, 4 * e + j] += (1.0 + gll_points[j]) / 2.0
    return result


def operators(count_y, count_z):
    gll_points, gauss_weights, values, slopes = basis_tables()
    return (
        jnp.asarray(values, jnp.float32),
        jnp.asarray(slopes, jnp.float32),
        jnp.asarray(banded(values, count_y), jnp.float32),
        jnp.asarray(banded(slopes, count_y), jnp.float32),
        jnp.asarray(banded(values, count_z), jnp.float32),
        jnp.asarray(banded(slopes, count_z), jnp.float32),
    )


def gradient(field, mats):
    basis_x, slope_x, basis_y, slope_y, basis_z, slope_z = mats
    along_b = jnp.einsum("cxyz,qz->cxyq", field, basis_z, precision=HIGHEST)
    along_d = jnp.einsum("cxyz,qz->cxyq", field, slope_z, precision=HIGHEST)
    plain_b = jnp.einsum("cxyq,py->cxpq", along_b, basis_y, precision=HIGHEST)
    sloped_b = jnp.einsum("cxyq,py->cxpq", along_b, slope_y, precision=HIGHEST)
    plain_d = jnp.einsum("cxyq,py->cxpq", along_d, basis_y, precision=HIGHEST)
    grad_x = jnp.einsum("cxpq,rx->crpq", plain_b, slope_x, precision=HIGHEST)
    grad_y = jnp.einsum("cxpq,rx->crpq", sloped_b, basis_x, precision=HIGHEST)
    grad_z = jnp.einsum("cxpq,rx->crpq", plain_d, basis_x, precision=HIGHEST)
    return (grad_x, grad_y, grad_z)


def divergence(fluxes, mats):
    basis_x, slope_x, basis_y, slope_y, basis_z, slope_z = mats
    part_x = jnp.einsum("crpq,rx->cxpq", fluxes[0], slope_x, precision=HIGHEST)
    part_y = jnp.einsum("crpq,rx->cxpq", fluxes[1], basis_x, precision=HIGHEST)
    part_z = jnp.einsum("crpq,rx->cxpq", fluxes[2], basis_x, precision=HIGHEST)
    side_b = jnp.einsum("cxpq,py->cxyq", part_x, basis_y, precision=HIGHEST) + jnp.einsum(
        "cxpq,py->cxyq", part_y, slope_y, precision=HIGHEST
    )
    side_d = jnp.einsum("cxpq,py->cxyq", part_z, basis_y, precision=HIGHEST)
    return jnp.einsum("cxyq,qz->cxyz", side_b, basis_z, precision=HIGHEST) + jnp.einsum(
        "cxyq,qz->cxyz", side_d, slope_z, precision=HIGHEST
    )


def state_terms(gradients):
    deform = [[gradients[a][c] + (1.0 if c == a else 0.0) for a in range(3)] for c in range(3)]
    strain = [
        [
            0.5
            * (
                deform[0][a] * deform[0][b]
                + deform[1][a] * deform[1][b]
                + deform[2][a] * deform[2][b]
            )
            - (0.5 if a == b else 0.0)
            for b in range(3)
        ]
        for a in range(3)
    ]
    strain_trace = strain[0][0] + strain[1][1] + strain[2][2]
    stress = [
        [
            2.0 * LAME_SHEAR * strain[a][b] + (LAME_FIRST * strain_trace if a == b else 0.0)
            for b in range(3)
        ]
        for a in range(3)
    ]
    return (deform, stress)


def tangent_flux(gradients, deform, stress, weighting):
    change = [[gradients[a][c] for a in range(3)] for c in range(3)]
    cross_terms = [
        [
            deform[0][a] * change[0][b] + deform[1][a] * change[1][b] + deform[2][a] * change[2][b]
            for b in range(3)
        ]
        for a in range(3)
    ]
    strain_change = [
        [0.5 * (cross_terms[a][b] + cross_terms[b][a]) for b in range(3)] for a in range(3)
    ]
    trace_change = strain_change[0][0] + strain_change[1][1] + strain_change[2][2]
    stress_change = [
        [
            2.0 * LAME_SHEAR * strain_change[a][b] + (LAME_FIRST * trace_change if a == b else 0.0)
            for b in range(3)
        ]
        for a in range(3)
    ]
    fluxes = []
    for a in range(3):
        rows_of = []
        for c in range(3):
            entry = (
                change[c][0] * stress[0][a]
                + change[c][1] * stress[1][a]
                + change[c][2] * stress[2][a]
                + deform[c][0] * stress_change[0][a]
                + deform[c][1] * stress_change[1][a]
                + deform[c][2] * stress_change[2][a]
            )
            rows_of.append(entry * weighting)
        fluxes.append(jnp.stack(rows_of))
    return fluxes


def quad_weighting(element_stiffness, gauss_weights):
    count_y, count_z = element_stiffness.shape
    spread = jnp.repeat(jnp.repeat(element_stiffness, 5, axis=0), 5, axis=1)
    weight_y = np.tile(gauss_weights, count_y)
    weight_z = np.tile(gauss_weights, count_z)
    quadrature = (
        gauss_weights[:, None, None] * weight_y[None, :, None] * weight_z[None, None, :] / 8.0
    )
    return spread[None] * jnp.asarray(quadrature, jnp.float32)


def pad_ends(field):
    return jnp.pad(field, ((0, 0), (0, 0), (0, 1), (0, 1)))


def gradient_of(own_nodes, right_layer, mats):
    return gradient(pad_ends(jnp.concatenate([own_nodes, right_layer[:, None]], axis=1)), mats)


def operate(own_nodes, right_layer, state, right_state, weighting, mats):
    terms = state_terms(gradient_of(state, right_state, mats))
    fluxes = tangent_flux(gradient_of(own_nodes, right_layer, mats), terms[0], terms[1], weighting)
    return divergence(fluxes, mats)[:, :, :-1, :-1]


def settle(image, field, rhs, keep, low_hat, high_hat, hat_y, hat_z):
    partial_value = rhs - keep * image[:, :4] - (1.0 - keep) * field
    coarse_terms = jnp.einsum("cjyz,vy,wz->cjvw", partial_value, hat_y, hat_z, precision=HIGHEST)
    onward = jnp.einsum("cjvw,j->cvw", coarse_terms, high_hat, precision=HIGHEST)
    arrived_layer, arrived_coarse = shifted((image[:, 4], onward), ("grp", "mem"), 1)
    fix_layer = -keep[0] * arrived_layer
    residual = partial_value.at[:, 0].add(fix_layer)
    own_coarse = (
        jnp.einsum("cjvw,j->cvw", coarse_terms, low_hat, precision=HIGHEST)
        + jnp.einsum("cyz,vy,wz->cvw", fix_layer, hat_y, hat_z, precision=HIGHEST)
        + arrived_coarse
    )
    return (residual, own_coarse)


def shards(state, direction, rhs, clamp, stiffness, coarse_owner, coarse_inverse):
    count_y = stiffness.shape[1]
    count_z = stiffness.shape[2]
    mats = operators(count_y, count_z)
    gll_points, gauss_weights, values, slopes = basis_tables()
    low_hat = jnp.asarray((1.0 - gll_points[:4]) / 2.0, jnp.float32)
    high_hat = jnp.asarray((1.0 + gll_points[:4]) / 2.0, jnp.float32)
    hat_y = jnp.asarray(restrictor(gll_points, count_y), jnp.float32)
    hat_z = jnp.asarray(restrictor(gll_points, count_z), jnp.float32)
    bottom = (jnp.arange(4 * count_z) == 0).astype(jnp.float32)
    keep = 1.0 - clamp.astype(jnp.float32)[:, :, None] * bottom[None, None, :]
    masked = keep * direction
    weighting = quad_weighting(stiffness[0], gauss_weights)
    right_direction, right_state, right_keep = shifted(
        (masked[:, 0], state[:, 0], keep[0, :, 0]), ("grp", "mem"), -1
    )
    image = operate(masked, right_direction, state, right_state, weighting, mats)
    first, restricted = settle(image, direction, rhs, keep, low_hat, high_hat, hat_y, hat_z)
    owner_slot = coarse_owner[0]
    flattened = restricted.reshape(3, count_y * count_z)
    outgoing = jnp.zeros_like(flattened).at[:, owner_slot].set(flattened)
    incoming = lax.all_to_all(outgoing, "grp", split_axis=1, concat_axis=1, tiled=True)
    blocks = coarse_inverse.shape[1]
    block_size = coarse_inverse.shape[2] // 3
    stacked = (
        incoming.reshape(3, blocks, block_size).transpose(1, 0, 2).reshape(blocks, 3 * block_size)
    )
    solved = jnp.einsum("kij,kj->ki", coarse_inverse[0], stacked, precision=HIGHEST)
    solved = (
        solved.reshape(blocks, 3, block_size).transpose(1, 0, 2).reshape(3, blocks * block_size)
    )
    returned = lax.all_to_all(solved, "grp", split_axis=1, concat_axis=1, tiled=True)
    correction = returned[:, owner_slot].reshape(3, count_y, count_z)
    right_correction = shifted(correction, ("grp", "mem"), -1)
    spread_own = jnp.einsum("cvw,vy,wz->cyz", correction, hat_y, hat_z, precision=HIGHEST)
    spread_right = jnp.einsum("cvw,vy,wz->cyz", right_correction, hat_y, hat_z, precision=HIGHEST)
    update = keep * (
        low_hat[None, :, None, None] * spread_own[:, None]
        + high_hat[None, :, None, None] * spread_right[:, None]
    )
    new_direction = direction + update
    keep_right = 1.0 - (1.0 - right_keep)[:, None] * bottom[None, :]
    right_new = right_direction + keep_right * spread_right
    image_next = operate(keep * new_direction, right_new, state, right_state, weighting, mats)
    residual, coarse_residual = settle(
        image_next, new_direction, rhs, keep, low_hat, high_hat, hat_y, hat_z
    )
    return (new_direction, residual, coarse_residual[:, None])


def solution(mesh):
    in_specs = (
        P(None, ("grp", "mem"), None, None),
        P(None, ("grp", "mem"), None, None),
        P(None, ("grp", "mem"), None, None),
        P(("grp", "mem"), None),
        P(("grp", "mem"), None, None),
        P(("grp", "mem"), None),
        P(("grp", "mem"), None, None, None),
    )
    out_specs = (
        P(None, ("grp", "mem"), None, None),
        P(None, ("grp", "mem"), None, None),
        P(None, ("grp", "mem"), None, None),
    )
    return jax.shard_map(shards, mesh=mesh, in_specs=in_specs, out_specs=out_specs, check_vma=False)
```

profile of v0, /device:TPU:128, one launch (start us, length us, event | category | flops | bytes accessed | tf_op | source)
XLA Modules:
  0.0 143.9 jit_solution(10511609748581061974)
XLA Ops:
  0.7 0.8 slice_bitcast_fusion.27
  1.5 6.1 %collective-permute-start.1 = (f32[3,16,128]{2,1,0:T(8,128)S(1)}, f32[3,16,128]{2,1,0:T(8,128)S(1)}, u32[]{:S(2)}, u32[]{:S(2)}) collective-permute-start(f32[3,16,128]{2,1,0:T(8,128)S(1)} %slice_bitcast_fusion.27), channel_id=1, source_target_pairs={{1,0},{2,1},{3,2},{4,3},{5,4},{6,5},{7,6},{8,7},{9,8},{10,9},{11,1... | collective-permute-start | bytes 73736 | tf_op jit(solution)/shard_map/ppermute | solution.py:15
  7.6 0.7 convert_element_type.21
  8.4 0.7 slice_reduce_fusion
  9.0 2.6 %collective-permute-start.5 = (f32[16]{0:T(128)}, f32[16]{0:T(128)}, u32[]{:S(2)}, u32[]{:S(2)}) collective-permute-start(f32[16]{0:T(128)} %slice_reduce_fusion), channel_id=1, source_target_pairs={{1,0},{2,1},{3,2},{4,3},{5,4},{6,5},{7,6},{8,7},{9,8},{10,9},{11,1... | collective-permute-start | bytes 200 | tf_op jit(solution)/shard_map/ppermute | solution.py:15
  11.7 2.6 %collective-permute-start = (f32[3,16,128]{2,1,0:T(8,128)S(1)}, f32[3,16,128]{2,1,0:T(8,128)S(1)}, u32[]{:S(2)}, u32[]{:S(2)}) collective-permute-start(f32[3,16,128]{2,1,0:T(8,128)S(1)} %slice_bitcast_fusion.26), channel_id=1, source_target_pairs={{1,0},{2,1},{3,2},{4,3},{5,4},{6,5},{7,6},{8,7},{9,8},{10,9},{11,1... | collective-permute-start | bytes 73736 | tf_op jit(solution)/shard_map/ppermute | solution.py:15
  14.3 0.6 pad_clamp_fusion
  15.2 0.6 collective-permute-done
  22.2 0.6 convolution_bitcast_fusion.9
  22.8 0.6 convolution_bitcast_fusion.11
  23.4 0.6 convolution_bitcast_fusion.12
  24.1 0.6 convolution_bitcast_fusion.13
  24.8 0.6 convolution_bitcast_fusion.14
  25.4 0.6 convolution_bitcast_fusion.10
  26.3 0.5 fusion.88
  28.4 0.6 convolution_bitcast_fusion.6
  29.0 0.5 convolution_bitcast_fusion.19
  29.5 0.8 convolution_bitcast_fusion.8
  30.3 0.5 fusion.64
  30.8 0.6 convolution_bitcast_fusion.7
  31.4 0.5 fusion.1
  33.7 2.6 %collective-permute-start.2 = (f32[3,16,128]{2,1,0:T(8,128)S(1)}, f32[3,16,128]{2,1,0:T(8,128)S(1)}, u32[]{:S(2)}, u32[]{:S(2)}) collective-permute-start(f32[3,16,128]{2,1,0:T(8,128)S(1)} %slice_bitcast_fusion.25), channel_id=1, source_target_pairs={{0,1},{1,2},{2,3},{3,4},{4,5},{5,6},{6,7},{7,8},{8,9},{9,10},{10,1... | collective-permute-start | bytes 73736 | tf_op jit(solution)/shard_map/ppermute | solution.py:15
  38.6 2.2 %collective-permute-start.3 = (f32[3,4,32]{2,1,0:T(4,128)S(1)}, f32[3,4,32]{2,1,0:T(4,128)S(1)}, u32[]{:S(2)}, u32[]{:S(2)}) collective-permute-start(f32[3,4,32]{2,1,0:T(4,128)S(1)} %bitcast.977), channel_id=1, source_target_pairs={{0,1},{1,2},{2,3},{3,4},{4,5},{5,6},{6,7},{7,8},{8,9},{9,10},{10,1... | collective-permute-start | bytes 4616 | tf_op jit(solution)/shard_map/ppermute | solution.py:15
  40.7 2.4 %collective-permute-done.2 = f32[3,16,128]{2,1,0:T(8,128)S(1)} collective-permute-done((f32[3,16,128]{2,1,0:T(8,128)S(1)}, f32[3,16,128]{2,1,0:T(8,128)S(1)}, u32[]{:S(2)}, u32[]{:S(2)}) %collective-permute-start.2) | collective-permute-done | bytes 24608 | tf_op jit(solution)/shard_map/ppermute | solution.py:15
  43.2 4.5 %collective-permute-done.3 = f32[3,4,32]{2,1,0:T(4,128)S(1)} collective-permute-done((f32[3,4,32]{2,1,0:T(4,128)S(1)}, f32[3,4,32]{2,1,0:T(4,128)S(1)}, u32[]{:S(2)}, u32[]{:S(2)}) %collective-permute-start.3) | collective-permute-done | bytes 1568 | tf_op jit(solution)/shard_map/ppermute | solution.py:15
  47.7 0.8 fusion.6
  48.5 1.4 copy.333
  49.9 1.8 %scatter_custom_fusion = f32[3,128]{0,1:T(8,128)} fusion(s32[128]{0:T(128)} %copy-done.34, f32[128,3]{1,0:T(8,128)} %bitcast.968, f32[]{:T(128)} %constant.82.clone.1), kind=kCustom, calls=%fused_computation.234 | custom fusion | bytes 2048 | tf_op jit(solution)/shard_map/scatter | solution.py:225
  51.7 19.7 %all-to-all-start = ((f32[3,64,2]{0,2,1:T(2,128)}), f32[3,64,2]{0,2,1:T(2,128)}, u32[]{:S(2)}, u32[]{:S(2)}) async-start(f32[3,64,2]{0,2,1:T(2,128)} %bitcast.965), calls=%async_computation | async-start | bytes 131072 | tf_op jit(solution)/shard_map/all_to_all | solution.py:226
  71.4 1.2 broadcast_subtract_fusion.1
  72.6 10.0 %all-to-all-done = f32[3,64,2]{0,2,1:T(2,128)} async-done(((f32[3,64,2]{0,2,1:T(2,128)}), f32[3,64,2]{0,2,1:T(2,128)}, u32[]{:S(2)}, u32[]{:S(2)}) %all-to-all-start) | async-done | bytes 1568 | tf_op jit(solution)/shard_map/all_to_all | solution.py:226
  82.6 1.5 %copy.334 = f32[3,2,64]{2,1,0:T(2,128)} copy(f32[3,2,64]{0,2,1:T(8,128)} %bitcast.96) | data formatting | bytes 3072 | tf_op jit(solution)/shard_map/reshape | solution.py:230
  84.0 1.3 copy.260
  85.3 1.3 reshape.205
  86.7 1.1 fusion.50
  87.8 0.6 copy.423
  88.4 1.4 reshape.153
  89.7 1.4 copy.335
  91.1 6.3 %all-to-all-start.1 = ((f32[3,64,2]{0,2,1:T(2,128)}), f32[3,64,2]{0,2,1:T(2,128)}, u32[]{:S(2)}, u32[]{:S(2)}) async-start(f32[3,64,2]{0,2,1:T(2,128)} %bitcast.966), calls=%async_computation.1 | async-start | bytes 131072 | tf_op jit(solution)/shard_map/all_to_all | solution.py:236
  97.4 1.3 multiply_subtract_fusion.1
  98.8 9.9 %all-to-all-done.1 = f32[3,64,2]{0,2,1:T(2,128)} async-done(((f32[3,64,2]{0,2,1:T(2,128)}), f32[3,64,2]{0,2,1:T(2,128)}, u32[]{:S(2)}, u32[]{:S(2)}) %all-to-all-start.1) | async-done | bytes 1568 | tf_op jit(solution)/shard_map/all_to_all | solution.py:236
  108.7 2.2 %gather_fusion = f32[128,3]{1,0:T(8,128)} fusion(f32[3,128]{0,1:T(8,128)} %bitcast.102, s32[1024]{0:T(1024)} %pad_clamp_fusion), kind=kCustom, calls=%fused_computation | custom fusion | bytes 3584 | tf_op jit(solution)/shard_map/gather | solution.py:237
  110.9 1.5 %copy.336 = f32[3,4,32]{2,1,0:T(4,128)} copy(f32[3,4,32]{0,2,1:T(8,128)} %bitcast.967) | data formatting | bytes 3072 | tf_op jit(solution)/shard_map/reshape | solution.py:237
  112.4 0.9 fusion.156
  113.3 1.9 %collective-permute-start.4 = (f32[3,4,32]{2,1,0:T(4,128)S(1)}, f32[3,4,32]{2,1,0:T(4,128)S(1)}, u32[]{:S(2)}, u32[]{:S(2)}) collective-permute-start(f32[3,4,32]{2,1,0:T(4,128)S(1)} %copy-done.18), channel_id=1, source_target_pairs={{1,0},{2,1},{3,2},{4,3},{5,4},{6,5},{7,6},{8,7},{9,8},{10,9},{11,1... | collective-permute-start | bytes 4616 | tf_op jit(solution)/shard_map/ppermute | solution.py:15
  115.5 1.1 collective-permute-done.4
  117.5 0.6 copy-done.17
  121.0 0.6 convolution_bitcast_fusion.3
  121.7 0.6 convolution_bitcast_fusion.5
  122.3 0.6 convolution_bitcast_fusion.4
  124.8 0.6 convolution_bitcast_fusion
  125.4 0.5 convolution_bitcast_fusion.15
  125.9 0.6 convolution_bitcast_fusion.2
  126.5 0.5 fusion.60
  127.0 0.6 convolution_bitcast_fusion.1
  127.6 0.5 fusion
  129.5 0.7 copy-done.22
  131.2 1.9 %collective-permute-start.6 = (f32[3,16,128]{2,1,0:T(8,128)S(1)}, f32[3,16,128]{2,1,0:T(8,128)S(1)}, u32[]{:S(2)}, u32[]{:S(2)}) collective-permute-start(f32[3,16,128]{2,1,0:T(8,128)S(1)} %slice_bitcast_fusion.24), channel_id=1, source_target_pairs={{0,1},{1,2},{2,3},{3,4},{4,5},{5,6},{6,7},{7,8},{8,9},{9,10},{10,1... | collective-permute-start | bytes 73736 | tf_op jit(solution)/shard_map/ppermute | solution.py:15
  133.3 0.6 copy.284
  134.0 1.9 %collective-permute-start.7 = (f32[3,4,32]{2,1,0:T(4,128)S(1)}, f32[3,4,32]{2,1,0:T(4,128)S(1)}, u32[]{:S(2)}, u32[]{:S(2)}) collective-permute-start(f32[3,4,32]{2,1,0:T(4,128)S(1)} %bitcast.976), channel_id=1, source_target_pairs={{0,1},{1,2},{2,3},{3,4},{4,5},{5,6},{6,7},{7,8},{8,9},{9,10},{10,1... | collective-permute-start | bytes 4616 | tf_op jit(solution)/shard_map/ppermute | solution.py:15
  135.9 4.7 %collective-permute-done.6 = f32[3,16,128]{2,1,0:T(8,128)S(1)} collective-permute-done((f32[3,16,128]{2,1,0:T(8,128)S(1)}, f32[3,16,128]{2,1,0:T(8,128)S(1)}, u32[]{:S(2)}, u32[]{:S(2)}) %collective-permute-start.6) | collective-permute-done | bytes 24608 | tf_op jit(solution)/shard_map/ppermute | solution.py:15
  140.7 0.7 copy.285
  141.4 1.8 %collective-permute-done.7 = f32[3,4,32]{2,1,0:T(4,128)S(1)} collective-permute-done((f32[3,4,32]{2,1,0:T(4,128)S(1)}, f32[3,4,32]{2,1,0:T(4,128)S(1)}, u32[]{:S(2)}, u32[]{:S(2)}) %collective-permute-start.7) | collective-permute-done | bytes 1568 | tf_op jit(solution)/shard_map/ppermute | solution.py:15
  143.1 0.8 fusion.4
  (139 shorter events, 21.0 us)
Async XLA Ops:
  0.6 86.0 %copy-start = (f32[1,2,192,192]{3,2,1,0:T(8,128)S(1)}, f32[1,2,192,192]{3,2,1,0:T(8,128)}, u32[]{:S(2)}) copy-start(f32[1,2,192,192]{3,2,1,0:T(8,128)} %param.26) | copy-start | bytes 884740
  0.6 11.0 %copy-start.3 = (f32[3,4,16,128]{3,2,1,0:T(8,128)S(1)}, f32[3,4,16,128]{3,2,1,0:T(8,128)}, u32[]{:S(2)}) copy-start(f32[3,4,16,128]{3,2,1,0:T(8,128)} %param.21) | copy-start | bytes 294916
  1.5 15.9 %collective-permute-start.1 = (f32[3,16,128]{2,1,0:T(8,128)S(1)}, f32[3,16,128]{2,1,0:T(8,128)S(1)}, u32[]{:S(2)}, u32[]{:S(2)}) collective-permute-start(f32[3,16,128]{2,1,0:T(8,128)S(1)} %slice_bitcast_fusion.27), channel_id=1, source_target_pairs={{1,0},{2,1},{3,2},{4,3},{5,4},{6,5},{7,6},{8,7},{9,8},{10,9},{11,1... | collective-permute-start | bytes 73736 | tf_op jit(solution)/shard_map/ppermute | solution.py:15
  7.6 0.7 copy-start.30
  9.0 62.3 %collective-permute-start.5 = (f32[16]{0:T(128)}, f32[16]{0:T(128)}, u32[]{:S(2)}, u32[]{:S(2)}) collective-permute-start(f32[16]{0:T(128)} %slice_reduce_fusion), channel_id=1, source_target_pairs={{1,0},{2,1},{3,2},{4,3},{5,4},{6,5},{7,6},{8,7},{9,8},{10,9},{11,1... | collective-permute-start | bytes 200 | tf_op jit(solution)/shard_map/ppermute | solution.py:15
  11.7 2.6 %copy-start.35 = (s32[1,128]{1,0:T(1,128)S(1)}, s32[1,128]{1,0:T(1,128)}, u32[]{:S(2)}) copy-start(s32[1,128]{1,0:T(1,128)} %param.25) | copy-start | bytes 1540
  11.7 4.1 %collective-permute-start = (f32[3,16,128]{2,1,0:T(8,128)S(1)}, f32[3,16,128]{2,1,0:T(8,128)S(1)}, u32[]{:S(2)}, u32[]{:S(2)}) collective-permute-start(f32[3,16,128]{2,1,0:T(8,128)S(1)} %slice_bitcast_fusion.26), channel_id=1, source_target_pairs={{1,0},{2,1},{3,2},{4,3},{5,4},{6,5},{7,6},{8,7},{9,8},{10,9},{11,1... | collective-permute-start | bytes 73736 | tf_op jit(solution)/shard_map/ppermute | solution.py:15
  14.3 0.6 copy-start.34
  14.3 0.7 copy-start.31
  15.1 0.9 copy-start.11
  15.8 0.7 copy-start.19
  16.0 0.9 copy-start.13
  16.9 0.9 copy-start.25
  18.3 0.7 copy-start.9
  19.0 0.7 copy-start.2
  21.5 0.7 copy-start.6
  23.4 0.7 copy-start.15
  25.4 0.9 copy-start.1
  31.4 0.9 copy-start.5
  32.3 0.9 copy-start.4
  33.2 3.1 %copy-start.7 = (f32[3,4,16,128]{3,2,1,0:T(8,128)S(1)}, f32[3,4,16,128]{3,2,1,0:T(8,128)}, u32[]{:S(2)}) copy-start(f32[3,4,16,128]{3,2,1,0:T(8,128)} %param.22) | copy-start | bytes 294916
  33.7 2.6 %copy-start.21 = (f32[4,16,1,1]{1,0,3,2:T(4,128)S(1)}, f32[4,16,1,1]{1,0,3,2:T(4,128)}, u32[]{:S(2)}) copy-start(f32[4,16,1,1]{1,0,3,2:T(4,128)} %constant.115) | copy-start | bytes 772
  33.7 9.4 %copy-start.23 = (f32[4,16,1]{1,0,2:T(4,128)S(1)}, f32[4,16,1]{1,0,2:T(4,128)}, u32[]{:S(2)}) copy-start(f32[4,16,1]{1,0,2:T(4,128)} %constant.126) | copy-start | bytes 772
  33.7 9.4 %collective-permute-start.2 = (f32[3,16,128]{2,1,0:T(8,128)S(1)}, f32[3,16,128]{2,1,0:T(8,128)S(1)}, u32[]{:S(2)}, u32[]{:S(2)}) collective-permute-start(f32[3,16,128]{2,1,0:T(8,128)S(1)} %slice_bitcast_fusion.25), channel_id=1, source_target_pairs={{0,1},{1,2},{2,3},{3,4},{4,5},{5,6},{6,7},{7,8},{8,9},{9,10},{10,1... | collective-permute-start | bytes 73736 | tf_op jit(solution)/shard_map/ppermute | solution.py:15
  36.3 0.7 copy-start.16
  37.1 0.7 copy-start.28
  37.7 0.7 copy-start.26
  38.6 9.2 %copy-start.10 = (f32[32,128,1]{1,0,2:T(8,128)S(1)}, f32[32,128,1]{1,0,2:T(8,128)}, u32[]{:S(2)}) copy-start(f32[32,128,1]{1,0,2:T(8,128)} %constant.114) | copy-start | bytes 49156
  38.6 9.2 %collective-permute-start.3 = (f32[3,4,32]{2,1,0:T(4,128)S(1)}, f32[3,4,32]{2,1,0:T(4,128)S(1)}, u32[]{:S(2)}, u32[]{:S(2)}) collective-permute-start(f32[3,4,32]{2,1,0:T(4,128)S(1)} %bitcast.977), channel_id=1, source_target_pairs={{0,1},{1,2},{2,3},{3,4},{4,5},{5,6},{6,7},{7,8},{8,9},{9,10},{10,1... | collective-permute-start | bytes 4616 | tf_op jit(solution)/shard_map/ppermute | solution.py:15
  51.7 30.9 %all-to-all-start = ((f32[3,64,2]{0,2,1:T(2,128)}), f32[3,64,2]{0,2,1:T(2,128)}, u32[]{:S(2)}, u32[]{:S(2)}) async-start(f32[3,64,2]{0,2,1:T(2,128)} %bitcast.965), calls=%async_computation | async-start | bytes 131072 | tf_op jit(solution)/shard_map/all_to_all | solution.py:226
  91.1 17.5 %all-to-all-start.1 = ((f32[3,64,2]{0,2,1:T(2,128)}), f32[3,64,2]{0,2,1:T(2,128)}, u32[]{:S(2)}, u32[]{:S(2)}) async-start(f32[3,64,2]{0,2,1:T(2,128)} %bitcast.966), calls=%async_computation.1 | async-start | bytes 131072 | tf_op jit(solution)/shard_map/all_to_all | solution.py:236
  112.4 0.9 copy-start.18
  112.4 2.9 %copy-start.24 = (f32[4,16,1]{1,0,2:T(4,128)S(1)}, f32[4,16,1]{1,0,2:T(4,128)}, u32[]{:S(2)}) copy-start(f32[4,16,1]{1,0,2:T(4,128)} %constant.126) | copy-start | bytes 772
  113.3 3.3 %collective-permute-start.4 = (f32[3,4,32]{2,1,0:T(4,128)S(1)}, f32[3,4,32]{2,1,0:T(4,128)S(1)}, u32[]{:S(2)}, u32[]{:S(2)}) collective-permute-start(f32[3,4,32]{2,1,0:T(4,128)S(1)} %copy-done.18), channel_id=1, source_target_pairs={{1,0},{2,1},{3,2},{4,3},{5,4},{6,5},{7,6},{8,7},{9,8},{10,9},{11,1... | collective-permute-start | bytes 4616 | tf_op jit(solution)/shard_map/ppermute | solution.py:15
  116.7 0.7 copy-start.32
  116.7 0.7 copy-start.33
  117.4 0.7 copy-start.17
  117.4 0.8 copy-start.20
  117.4 0.9 copy-start.12
  118.3 0.9 copy-start.14
  128.6 0.9 copy-start.8
  129.5 0.7 copy-start.22
  130.4 0.7 copy-start.29
  131.0 2.1 %copy-start.27 = (f32[4,1,1,1]{0,1,3,2:T(1,128)S(1)}, f32[4,1,1,1]{0,1,3,2:T(1,128)}, u32[]{:S(2)}) copy-start(f32[4,1,1,1]{0,1,3,2:T(1,128)} %constant.125) | copy-start | bytes 52
  131.2 9.4 %collective-permute-start.6 = (f32[3,16,128]{2,1,0:T(8,128)S(1)}, f32[3,16,128]{2,1,0:T(8,128)S(1)}, u32[]{:S(2)}, u32[]{:S(2)}) collective-permute-start(f32[3,16,128]{2,1,0:T(8,128)S(1)} %slice_bitcast_fusion.24), channel_id=1, source_target_pairs={{0,1},{1,2},{2,3},{3,4},{4,5},{5,6},{6,7},{7,8},{8,9},{9,10},{10,1... | collective-permute-start | bytes 73736 | tf_op jit(solution)/shard_map/ppermute | solution.py:15
  134.0 9.2 %collective-permute-start.7 = (f32[3,4,32]{2,1,0:T(4,128)S(1)}, f32[3,4,32]{2,1,0:T(4,128)S(1)}, u32[]{:S(2)}, u32[]{:S(2)}) collective-permute-start(f32[3,4,32]{2,1,0:T(4,128)S(1)} %bitcast.976), channel_id=1, source_target_pairs={{0,1},{1,2},{2,3},{3,4},{4,5},{5,6},{6,7},{7,8},{8,9},{9,10},{10,1... | collective-permute-start | bytes 4616 | tf_op jit(solution)/shard_map/ppermute | solution.py:15
where the time goes:
time: 145 us; the launch traced here: 144 us
  starting transfers between devices  47.7 us (33%)
  waiting for transfers between devices  34.8 us (24%)
  matrix products  26.8 us (18%)
  local copies, waits for them, and re-layouts  25.3 us (17%)
  other arithmetic  7.89 us (5%)
  between operations  1.49 us (1%)
    ppermute x8, starting transfers between devices, shifted(): return lax.ppermute(block, axis, route)  21.7 us
    all_to_all x1, starting transfers between devices, shards(): lax.all_to_all(outgoing, 'grp', split_axis=1, concat_axis=1, tiled=True)  19.7 us
    ppermute x8, waiting for transfers between devices, shifted(): return lax.ppermute(block, axis, route)  14.9 us
    all_to_all x1, waiting for transfers between devices, shards(): lax.all_to_all(outgoing, 'grp', split_axis=1, concat_axis=1, tiled=True)  9.97 us
    all_to_all x1, waiting for transfers between devices, shards(): lax.all_to_all(solved, 'grp', split_axis=1, concat_axis=1, tiled=True)  9.91 us
    unnamed x74, local copies, waits for them, and re-layouts  9.18 us
    all_to_all x1, starting transfers between devices, shards(): lax.all_to_all(solved, 'grp', split_axis=1, concat_axis=1, tiled=True)  6.27 us
    another operation x18, other arithmetic, tangent_flux(): fluxes.append(jnp.stack(rows_of))  3.84 us
  transfers between devices with their start and end apart: 10, of which 8 were waited for; matrix products, arithmetic and copies ran while one was open for 18% of the time, Pallas kernels for 0%

commit v1 on v0

v1 whole, which is shorter than its diff:
```python
import functools
import jax
import jax.numpy as jnp
import numpy as np
from jax import lax
from jax.experimental import pallas as pl
from jax.experimental.pallas import tpu as pltpu
from jax.sharding import PartitionSpec as P

F32 = jnp.float32
BF16 = jnp.bfloat16
HIGHEST = lax.Precision.HIGHEST
EY = 4
EZ = 32
ROWS = 112
LIVE = 104
WIDE = 256
NODES = 80


def basis_tables():
    gll = np.array([-1.0, -np.sqrt(3.0 / 7.0), 0.0, np.sqrt(3.0 / 7.0), 1.0])
    inner = np.sqrt(5.0 - 2.0 * np.sqrt(10.0 / 7.0)) / 3.0
    outer = np.sqrt(5.0 + 2.0 * np.sqrt(10.0 / 7.0)) / 3.0
    inner_weight = (322.0 + 13.0 * np.sqrt(70.0)) / 900.0
    outer_weight = (322.0 - 13.0 * np.sqrt(70.0)) / 900.0
    points = np.array([-outer, -inner, 0.0, inner, outer])
    weights = np.array([outer_weight, inner_weight, 128.0 / 225.0, inner_weight, outer_weight])
    values = np.zeros((5, 5))
    slopes = np.zeros((5, 5))
    for j in range(5):
        others = [gll[k] for k in range(5) if k != j]
        denominator = np.prod([gll[j] - o for o in others])
        for q in range(5):
            t = points[q]
            values[q, j] = np.prod([t - o for o in others]) / denominator
            total = 0.0
            for i in range(4):
                total += np.prod([t - others[k] for k in range(4) if k != i])
            slopes[q, j] = 2.0 * total / denominator
    return gll, weights, values, slopes


def banded(table, count):
    result = np.zeros((5 * count, 4 * count + 1))
    for e in range(count):
        result[5 * e : 5 * e + 5, 4 * e : 4 * e + 5] = table
    return result[:, :-1]


def restrictor(gll, count):
    result = np.zeros((count, 4 * count))
    for e in range(count):
        for j in range(4):
            result[e, 4 * e + j] += (1.0 - gll[j]) / 2.0
            if e + 1 < count:
                result[e + 1, 4 * e + j] += (1.0 + gll[j]) / 2.0
    return result


def halves(table):
    table = np.asarray(table, np.float32)
    high = table.astype(BF16)
    low = (table - high.astype(np.float32)).astype(BF16)
    return high, low


def stack_left(table):
    high, low = halves(table)
    return np.concatenate([high, high, low], axis=1)


def stack_right(table):
    high, low = halves(table)
    return np.concatenate([high, high, low], axis=0)


@functools.lru_cache(maxsize=None)
def constants():
    gll, weights, values, slopes = basis_tables()
    by, dy = banded(values, EY), banded(slopes, EY)
    bz, dz = banded(values, EZ), banded(slopes, EZ)
    along = np.zeros((4 * EZ, 2 * WIDE))
    along[:, : 5 * EZ] = bz.T
    along[:, WIDE : WIDE + 5 * EZ] = dz.T
    kinds = np.zeros((3, ROWS, NODES))
    for a, (bx, side) in enumerate(((slopes, by), (values, dy), (values, by))):
        kinds[a, :100] = np.kron(bx, side)
    low = (1.0 - gll[:4]) / 2.0
    high = (1.0 + gll[:4]) / 2.0
    hat_y, hat_z = restrictor(gll, EY), restrictor(gll, EZ)
    rest = np.zeros((16, NODES))
    rest[0:4, :64] = np.kron(low[None, :], hat_y)
    rest[4:8, :64] = np.kron(high[None, :], hat_y)
    rest[4:8, 64:] = hat_y
    fold = np.zeros((8, 24))
    for c in range(3):
        for part in range(2):
            for k in range(4):
                fold[part * 4 + c, c * 8 + part * 4 + k] = 1.0
    quad_y = np.zeros((ROWS, EY))
    for r in range(5):
        for p in range(20):
            quad_y[r * 20 + p, p // 5] = weights[r] * weights[p % 5] / 8.0
    quad_z = np.zeros((EZ, WIDE))
    for q in range(5 * EZ):
        quad_z[q // 5, q] = weights[q % 5]
    return dict(
        along=stack_right(along),
        grads=stack_left(kinds.reshape(3 * ROWS, NODES)),
        back_xy=stack_left(np.concatenate([kinds[0].T, kinds[1].T], axis=1)),
        back_z=stack_left(kinds[2].T),
        back_along=stack_right(along.T),
        rest=stack_left(rest),
        tables=np.concatenate(
            [
                np.tile(hat_z.T, (1, 4)),
                np.pad(fold, ((0, 0), (0, 104))),
                np.pad(rest[:8].T, ((0, 0), (0, 120))),
            ],
            axis=0,
        ).astype(np.float32),
        quad_y=np.asarray(quad_y, np.float32),
        quad_z=np.asarray(quad_z, np.float32),
    )


def split(x):
    high = x.astype(BF16)
    return high, (x - high.astype(F32)).astype(BF16)


def dot(a, b):
    return jnp.dot(a, b, preferred_element_type=F32)


def exact(a, b):
    return jnp.dot(a, b, preferred_element_type=F32, precision=HIGHEST)


def under(x):
    high, low = split(x)
    return jnp.concatenate([high, low, high], axis=0)


def beside(x):
    high, low = split(x)
    return jnp.concatenate([high, low, high], axis=1)


def near(x):
    return pltpu.with_memory_space_constraint(x, pltpu.VMEM)


def call(body, outs, *operands, scratch=()):
    vmem = pl.BlockSpec(memory_space=pltpu.VMEM)
    return pl.pallas_call(
        body,
        out_shape=[pltpu.VMEM(s, F32) for s in outs],
        in_specs=[vmem] * len(operands),
        out_specs=[vmem] * len(outs),
        scratch_shapes=list(scratch),
        compiler_params=pltpu.CompilerParams(vmem_limit_bytes=24 * 2**20),
    )(*[near(x) for x in operands])


def prepare_body(count, *refs):
    sources, refs = refs[:count], refs[count:]
    message, keep_rows, rows, weighting = refs[:4]
    targets, done = refs[4:-1], refs[-1]
    copies = [
        pltpu.make_async_copy(source, target, done.at[i])
        for i, (source, target) in enumerate(zip(sources, targets))
    ]
    for copy in copies:
        copy.start()
    state, direction = targets[0], targets[1]
    clamp, owner, inverse, stiffness, quad_y, quad_z = targets[-6:]
    for i in (0, 1, count - 6, count - 5):
        copies[i].wait()
    eye = lax.broadcasted_iota(jnp.int32, (16, 16), 0) == lax.broadcasted_iota(
        jnp.int32, (16, 16), 1
    )
    lane = lax.broadcasted_iota(jnp.int32, (16, 128), 1)
    for x in range(4):
        row = clamp[x : x + 1, :].astype(F32)
        column = jnp.sum(jnp.where(eye, row, 0.0), axis=1, keepdims=True)
        keep = jnp.where(lane == 0, 1.0 - column, 1.0)
        keep_rows[x * 16 : (x + 1) * 16, :] = keep
        if x == 0:
            message[96:112, :] = keep
            message[112:120, :] = jnp.broadcast_to(owner[...].astype(F32), (8, 128))
            for c in range(3):
                message[c * 16 : (c + 1) * 16, :] = keep * direction[c, 0]
                message[48 + c * 16 : 48 + (c + 1) * 16, :] = state[c, 0]
    for i in range(count - 4, count):
        copies[i].wait()
    row = lax.broadcasted_iota(jnp.int32, (64, 64), 0)
    column = lax.broadcasted_iota(jnp.int32, (64, 64), 1)
    order = (column == (row % 32) * 2 + row // 32).astype(F32)
    for b in range(2):
        for c in range(3):
            sorted_rows = exact(order, inverse[b, c * 64 : (c + 1) * 64, :])
            for q in range(2):
                part = sorted_rows[q * 32 : (q + 1) * 32]
                padded = jnp.concatenate([part, jnp.zeros((32, 64), F32)], axis=1)
                for h in range(2):
                    first = b * 32 * 12 + (q * 3 + c) * 2 + h
                    rows[pl.ds(first, 32, stride=12), :] = padded[:, h * 128 : (h + 1) * 128]
    weighting[...] = exact(exact(quad_y[...], stiffness[...]), quad_z[...])
    for i in range(2, count - 6):
        copies[i].wait()


def prepare(kept, used):
    operands = list(kept) + list(used)
    far = pl.BlockSpec(memory_space=pltpu.HBM)
    vmem = pl.BlockSpec(memory_space=pltpu.VMEM)
    made = [(120, 128), (64, 128), (768, 128), (ROWS, WIDE)]
    outs = [pltpu.VMEM(s, F32) for s in made] + [pltpu.VMEM(x.shape, x.dtype) for x in kept]
    return pl.pallas_call(
        functools.partial(prepare_body, len(operands)),
        out_shape=outs,
        in_specs=[far] * len(operands),
        out_specs=[vmem] * len(outs),
        scratch_shapes=[pltpu.VMEM(x.shape, x.dtype) for x in used]
        + [pltpu.SemaphoreType.DMA((len(operands),))],
        compiler_params=pltpu.CompilerParams(vmem_limit_bytes=24 * 2**20),
    )(*[pltpu.with_memory_space_constraint(x, pltpu.HBM) for x in operands])


def gradients(fields, along, grads, refs):
    lines = jnp.concatenate([f for field in fields for f in field], axis=0)
    flat = dot(beside(lines), along[...])
    for i, ref in enumerate(refs):
        parts = [flat[(3 * i + c) * NODES : (3 * i + c + 1) * NODES] for c in range(3)]
        plain = jnp.concatenate([p[:, :WIDE] for p in parts], axis=1)
        sloped = jnp.concatenate([p[:, WIDE:] for p in parts], axis=1)
        ref[0 : 2 * ROWS, :] = dot(grads[0 : 2 * ROWS, :], under(plain))
        ref[2 * ROWS :, :] = dot(grads[2 * ROWS :, :], under(sloped))


def physics(state_grad, grad, weighting, flux):
    pairs = ((0, 0), (1, 1), (2, 2), (0, 1), (0, 2), (1, 2))
    for start in range(0, LIVE, 8):
        here = slice(start, start + 8)
        w = weighting[here, :]

        def piece(ref, c, a):
            return ref[a * ROWS + start : a * ROWS + start + 8, c * WIDE : (c + 1) * WIDE]

        deform = [
            [piece(state_grad, c, a) + (1.0 if a == c else 0.0) for a in range(3)]
            for c in range(3)
        ]
        change = [[piece(grad, c, a) for a in range(3)] for c in range(3)]
        square = {
            (a, b): deform[0][a] * deform[0][b]
            + deform[1][a] * deform[1][b]
            + deform[2][a] * deform[2][b]
            for a, b in pairs
        }
        shift = 0.6 * (square[0, 0] + square[1, 1] + square[2, 2] - 3.0)
        held = {
            (a, b): w * (0.8 * (square[a, b] - 1.0) + shift) if a == b else (0.8 * w) * square[a, b]
            for a, b in pairs
        }
        cross = [
            [
                deform[0][a] * change[0][b] + deform[1][a] * change[1][b] + deform[2][a] * change[2][b]
                for b in range(3)
            ]
            for a in range(3)
        ]
        trace = (1.2 * w) * (cross[0][0] + cross[1][1] + cross[2][2])
        moved = {}
        for a, b in pairs:
            if a == b:
                moved[a, b] = (1.6 * w) * cross[a][b] + trace
            else:
                moved[a, b] = (0.8 * w) * (cross[a][b] + cross[b][a])
        for a in range(3):
            for c in range(3):
                entry = None
                for b in range(3):
                    key = (min(a, b), max(a, b))
                    term = change[c][b] * held[key] + deform[c][b] * moved[key]
                    entry = term if entry is None else entry + term
                flux[a * ROWS + start : a * ROWS + start + 8, c * WIDE : (c + 1) * WIDE] = entry
    for a in range(3):
        flux[a * ROWS + LIVE : (a + 1) * ROWS, :] = jnp.zeros((ROWS - LIVE, 3 * WIDE), F32)


def images(flux, back_xy, back_z, back_along):
    side_b = dot(back_xy[...], under(flux[0 : 2 * ROWS, :]))
    side_d = dot(back_z[...], under(flux[2 * ROWS :, :]))
    lines = jnp.concatenate(
        [
            jnp.concatenate(
                [side_b[:, c * WIDE : (c + 1) * WIDE], side_d[:, c * WIDE : (c + 1) * WIDE]], axis=1
            )
            for c in range(3)
        ],
        axis=0,
    )
    return dot(beside(lines), back_along[...])


def coarse_rows(extended, rest):
    levels = dot(rest[...], under(jnp.concatenate(extended, axis=1)))
    return jnp.concatenate([levels[:8, c * 128 : (c + 1) * 128] for c in range(3)], axis=0)


def own_rows(ref, c):
    return ref[c].reshape(64, 128)


def first_body(
    state, direction, rhs, keep_rows, halo, weighting, along, grads, back_xy, back_z, back_along,
    rest, tables, owner, state_grad, sums, grad, flux,
):
    keep = keep_rows[...]
    fields = [
        [jnp.concatenate([own_rows(state, c), halo[48 + c * 16 : 64 + c * 16, :]], axis=0) for c in range(3)],
        [
            jnp.concatenate([keep * own_rows(direction, c), halo[c * 16 : 16 + c * 16, :]], axis=0)
            for c in range(3)
        ],
    ]
    gradients(fields, along, grads, (state_grad, grad))
    physics(state_grad, grad, weighting, flux)
    image = images(flux, back_xy, back_z, back_along)
    keep_right = halo[96:112, :]
    extended = []
    for c in range(3):
        part = image[c * NODES : (c + 1) * NODES]
        own = own_rows(rhs, c) - keep * part[:64] - (1.0 - keep) * own_rows(direction, c)
        extended.append(jnp.concatenate([own, -keep_right * part[64:]], axis=0))
    levels = exact(coarse_rows(extended, rest), tables[0:128, :])
    row = lax.broadcasted_iota(jnp.int32, (24, 128), 0)
    lane = lax.broadcasted_iota(jnp.int32, (24, 128), 1)
    levels = jnp.where(lane // EZ == row % EY, levels, 0.0)
    levels = exact(tables[128:136, 0:24], levels)
    sums[0:4, :] = placed(levels, owner[...])[0:4]
    sums[4:8, :] = placed(levels, halo[112:113, :].astype(jnp.int32))[4:8]


def slots(owner):
    place = (owner % 2) * 64 + owner // 2
    return (lax.broadcasted_iota(jnp.int32, (128, 128), 0) == place).astype(BF16)


def placed(rows, owner):
    where = slots(owner)
    nt = (((1,), (1,)), ((), ()))
    return sum(lax.dot_general(part, where, nt, preferred_element_type=F32) for part in split(rows))


def solve_body(gathered, rows, owner, correction):
    tn = (((0,), (0,)), ((), ()))
    values = gathered[...]
    row = lax.broadcasted_iota(jnp.int32, (128, 256), 0)
    lane = lax.broadcasted_iota(jnp.int32, (128, 256), 1)
    match = (row // 4 == lane % 64 // 2) & (row % 4 == lane // 64) & (lane < 192)
    need = None
    for q in range(2):
        pick = (match & (lane % 2 == q)).astype(BF16)
        for part in split(values[:, q * 64 : (q + 1) * 64]):
            term = lax.dot_general(part, pick, tn, preferred_element_type=F32)
            need = term if need is None else need + term
    products = []
    for k in range(6):
        product = None
        for h in range(2):
            term = rows[pl.ds(2 * k + h, 64, stride=12), :] * need[:, h * 128 : (h + 1) * 128]
            product = term if product is None else product + term
        products.append(product)
    ones = jnp.ones((128, 128), BF16)
    sums = sum(dot(part, ones) for part in split(jnp.concatenate(products, axis=0)))
    lane = lax.broadcasted_iota(jnp.int32, (64, 128), 1)
    stacked = []
    for q in range(2):
        first, second, third = [sums[(q * 3 + c) * 64 : (q * 3 + c + 1) * 64] for c in range(3)]
        stacked.append(jnp.where(lane == 0, first, jnp.where(lane == 1, second, third)))
    stacked = jnp.concatenate(stacked, axis=0)[:, 0:8]
    where = slots(owner[...])
    correction[...] = sum(
        lax.dot_general(part, where, tn, preferred_element_type=F32) for part in split(stacked)
    )


def second_body(
    correction, right, state_grad, direction, rhs, keep_rows, halo, weighting, along, grads,
    back_xy, back_z, back_along, rest, tables, new, partial, message, own_coarse, grad, flux,
):
    keep = keep_rows[...]
    keep_right = halo[96:112, :]
    rows = jnp.concatenate(
        [
            jnp.broadcast_to(ref[c : c + 1, :], (4, 128))
            for c in range(3)
            for ref in (correction, right)
        ],
        axis=0,
    )
    row = lax.broadcasted_iota(jnp.int32, (24, 128), 0)
    lane = lax.broadcasted_iota(jnp.int32, (24, 128), 1)
    levels = lax.dot_general(
        jnp.where(lane // EZ == row % EY, rows, 0.0), tables[0:128, :], (((1,), (1,)), ((), ())),
        preferred_element_type=F32, precision=HIGHEST,
    )
    levels = jnp.concatenate([levels[c * 8 : (c + 1) * 8] for c in range(3)], axis=1)
    update = exact(tables[136:216, 0:8], levels)
    field = []
    fresh = []
    for c in range(3):
        piece = update[:, c * 128 : (c + 1) * 128]
        own = own_rows(direction, c) + keep * piece[:64]
        new[c] = own.reshape(4, 16, 128)
        fresh.append(own)
        field.append(
            jnp.concatenate(
                [keep * own, halo[c * 16 : 16 + c * 16, :] + keep_right * piece[64:]], axis=0
            )
        )
    gradients([field], along, grads, (grad,))
    physics(state_grad, grad, weighting, flux)
    image = images(flux, back_xy, back_z, back_along)
    extended = []
    for c in range(3):
        part = image[c * NODES : (c + 1) * NODES]
        own = own_rows(rhs, c) - keep * part[:64] - (1.0 - keep) * fresh[c]
        last = -keep_right * part[64:]
        partial[c] = own.reshape(4, 16, 128)
        message[c * 16 : (c + 1) * 16, :] = last
        extended.append(jnp.concatenate([own, last], axis=0))
    levels = exact(coarse_rows(extended, rest), tables[0:128, :])
    message[48:72, :] = levels
    for c in range(3):
        own_coarse[c] = levels[c * 8 : c * 8 + 4, :EZ]


def finish_body(partial, arrived, own_coarse, residual, coarse):
    for c in range(3):
        residual[c, 0] = partial[c, 0] + arrived[c * 16 : (c + 1) * 16, :]
        residual[c, 1:4] = partial[c, 1:4]
        coarse[c] = own_coarse[c] + arrived[52 + c * 8 : 56 + c * 8, :EZ]


def finish(partial, arrived, own_coarse):
    vmem = pl.BlockSpec(memory_space=pltpu.VMEM)
    return pl.pallas_call(
        finish_body,
        out_shape=[
            jax.ShapeDtypeStruct((3, 4, 16, 128), F32),
            jax.ShapeDtypeStruct((3, EY, EZ), F32),
        ],
        in_specs=[vmem] * 3,
        out_specs=[vmem] * 2,
        compiler_params=pltpu.CompilerParams(vmem_limit_bytes=24 * 2**20),
    )(near(partial), near(arrived), near(own_coarse))


def shifted(block, distance):
    axes = ("grp", "mem")
    count = lax.axis_size(axes)
    route = [(i - distance, i) for i in range(count) if 0 <= i - distance < count]
    return lax.ppermute(block, axes, route)


def shards(state, direction, rhs, clamp, stiffness, coarse_owner, coarse_inverse):
    k = constants()
    names = ("along", "grads", "back_xy", "back_z", "back_along", "rest", "tables")
    kept = [state, direction, rhs] + [jnp.asarray(k[name]) for name in names] + [coarse_owner]
    used = [
        clamp, coarse_owner, coarse_inverse[0], stiffness[0],
        jnp.asarray(k["quad_y"]), jnp.asarray(k["quad_z"]),
    ]
    message, keep_rows, rows, weighting, state, direction, rhs, *shared, owner = prepare(kept, used)
    halo = shifted(message, -1)
    rows = lax.all_to_all(
        rows.reshape(192, 4, 128), "grp", split_axis=0, concat_axis=0, tiled=True
    ).reshape(768, 128)
    big = (3 * ROWS, 3 * WIDE)
    scratch = (pltpu.VMEM(big, F32), pltpu.VMEM(big, F32))
    state_grad, sums = call(
        first_body,
        [big, (8, 128)],
        state, direction, rhs, keep_rows, halo, weighting, *shared, owner,
        scratch=scratch,
    )
    arrived = shifted(sums, 1)
    total = jnp.broadcast_to((sums[0:4] + arrived[4:8])[None], (32, 4, 128)).reshape(128, 128)
    total, rows = lax.optimization_barrier((total, rows))
    sides = [list(range(32)), list(range(32, 64))]
    gathered = lax.all_to_all(
        total, "grp", split_axis=0, concat_axis=0, tiled=True, axis_index_groups=sides
    )
    (correction,) = call(solve_body, [(8, 128)], gathered, rows, owner)
    right = shifted(correction, -1)
    field = (3, 4, 16, 128)
    new, partial, last, own_coarse = call(
        second_body,
        [field, field, (72, 128), (3, EY, EZ)],
        correction, right, state_grad, direction, rhs, keep_rows, halo, weighting, *shared,
        scratch=scratch,
    )
    residual, coarse = finish(partial, shifted(last, 1), own_coarse)
    return new, residual, coarse[:, None]


def solution(mesh):
    along = ("grp", "mem")
    field = P(None, along, None, None)
    in_specs = (
        field, field, field, P(along, None), P(along, None, None), P(along, None),
        P(along, None, None, None),
    )
    return jax.shard_map(
        shards, mesh=mesh, in_specs=in_specs, out_specs=(field, field, field), check_vma=False
    )
```

time: 145 us -> 81.3 us (0.56)
  matrix products: 26.8 us -> 0 us
  local copies, waits for them, and re-layouts: 25.3 us -> 0.65 us
  blocking collectives: 0 us -> 17.4 us
  waiting for transfers between devices: 34.8 us -> 18.1 us
  starting transfers between devices: 47.7 us -> 33.9 us
  Pallas kernels: 0 us -> 10.2 us
  other arithmetic: 7.89 us -> 0.01 us
    dot_general x57 -> x0, matrix products: 26.8 us -> none  [the longest x3 1.89 us: gradient(): grad_y = jnp.einsum('cxpq,rx->crpq', sloped_b, basis_x, precision=HIGHEST)]
    all_to_all x2 -> x1, waiting for transfers between devices: 19.9 us -> 0.01 us  [shards(): lax.all_to_all(rows.reshape(192, 4, 128), 'grp', split_axis=0, concat_axi...]
    all_to_all x0 -> x1, blocking collectives: none -> 17.4 us  [shards(): lax.all_to_all(total, 'grp', split_axis=0, concat_axis=0, tiled=True, axi...]
    pallas_call x0 -> x5, Pallas kernels: none -> 10.2 us  [the longest x3 6.31 us: call(): pl.pallas_call(body, out_shape=[pltpu.VMEM(s, F32) for s in outs], in_spe...]
    ppermute x8 -> x4, starting transfers between devices: 21.7 us -> 12.9 us  [shifted(): return lax.ppermute(block, axes, route)]
    unnamed x74 -> x1, local copies, waits for them, and re-layouts: 9.18 us -> 0.64 us
    reshape x7 -> x0, local copies, waits for them, and re-layouts: 7.23 us -> none  [the longest x2 2.84 us: shards(): incoming.reshape(3, blocks, block_size).transpose(1, 0, 2)]
    all_to_all x2 -> x1, starting transfers between devices: 25.9 us -> 20.9 us  [shards(): lax.all_to_all(rows.reshape(192, 4, 128), 'grp', split_axis=0, concat_axi...]
  transfers between devices with their start and end apart: 10 -> 5, of which waited for: 8 -> 4; matrix products, arithmetic and copies ran while one was open for 18% -> 1% of each run, Pallas kernels for 0% -> 3%
where the time goes in v1:
time: 81.3 us; the launch traced here: 80.9 us
  starting transfers between devices  33.9 us (42%)
  waiting for transfers between devices  18.1 us (22%)
  blocking collectives  17.4 us (21%)
  Pallas kernels  10.2 us (13%)
    all_to_all x1, starting transfers between devices, shards(): lax.all_to_all(rows.reshape(192, 4, 128), 'grp', split_axis=0, concat_axi...  20.9 us
    ppermute x4, waiting for transfers between devices, shifted(): return lax.ppermute(block, axes, route)  18.1 us
    all_to_all x1, blocking collectives, shards(): lax.all_to_all(total, 'grp', split_axis=0, concat_axis=0, tiled=True, axi...  17.4 us
    ppermute x4, starting transfers between devices, shifted(): return lax.ppermute(block, axes, route)  12.9 us
    pallas_call x3, Pallas kernels, call(): pl.pallas_call(body, out_shape=[pltpu.VMEM(s, F32) for s in outs], in_spe...  6.31 us
    pallas_call x1, Pallas kernels, prepare(): pl.pallas_call(functools.partial(prepare_body, len(operands)), out_shape=...  3.27 us
  transfers between devices with their start and end apart: 5, of which 4 were waited for; matrix products, arithmetic and copies ran while one was open for 1% of the time, Pallas kernels for 3%

profile of v1, /device:TPU:128, one launch (start us, length us, event | category | flops | bytes accessed | tf_op | source)
XLA Modules:
  0.0 80.9 jit_solution(5712172410592319197)
XLA Ops:
  0.6 3.3 %shard_map.175 = (f32[120,128]{1,0:T(8,128)S(1)}, f32[64,128]{1,0:T(8,128)S(1)}, f32[768,128]{1,0:T(8,128)}, f32[112,256]{1,0:T(8,128)S(1)}, f32[3,4,16,128]{3,2...) custom-call(f32[3,4,16,128]{3,2,1,0:T(8,128)} %refs_0_.1, ...), custom_call_target="tpu_custom_call" | custom-call | tf_op jit(solution)/shard_map/pallas_call | solution.py:221
  3.9 20.9 %all-to-all-start = ((f32[192,4,128]{2,1,0:T(4,128)}), f32[192,4,128]{2,1,0:T(4,128)S(1)}, u32[]{:S(2)}, u32[]{:S(2)}) async-start(f32[192,4,128]{2,1,0:T(4,128)} %bitcast.3), calls=%async_computation | async-start | bytes 786432 | tf_op jit(solution)/shard_map/all_to_all | solution.py:481
  24.8 7.2 %collective-permute-start = (f32[120,128]{1,0:T(8,128)S(1)}, f32[120,128]{1,0:T(8,128)S(1)}, u32[]{:S(2)}, u32[]{:S(2)}) collective-permute-start(f32[120,128]{1,0:T(8,128)S(1)} %get-tuple-element.32), channel_id=1, source_target_pairs={{1,0},{2,1},{3,2},{4,3},{5,4},{6,5},{7,6},{8,7},{9,8},{10,9},{11,1... | collective-permute-start | bytes 184328 | tf_op jit(solution)/shard_map/ppermute | solution.py:468
  32.0 2.2 %collective-permute-done.halo = f32[120,128]{1,0:T(8,128)S(1)} collective-permute-done((f32[120,128]{1,0:T(8,128)S(1)}, f32[120,128]{1,0:T(8,128)S(1)}, u32[]{:S(2)}, u32[]{:S(2)}) %collective-permute-start) | collective-permute-done | bytes 61472 | tf_op jit(solution)/shard_map/ppermute | solution.py:468
  34.2 2.8 %shard_map.176 = (f32[336,768]{1,0:T(8,128)S(1)}, f32[8,128]{1,0:T(8,128)S(1)}) custom-call(f32[3,4,16,128]{3,2,1,0:T(8,128)S(1)} %get-tuple-element.28.state, f32[3,4,16,128]{3,2,1,0:T(8,128)S(1)} %get-tuple-element.29.direction, f32[3,4,16,128]{3,2,1,0:T(8,128)S(1)} %get-tuple-element.30.rhs, f32[64,128]{1,0:T(8,128)S(1)} %get-tuple-element.31.keep_rows, ...), custom_call_target="tpu_custom_call" | custom-call | tf_op jit(solution)/shard_map/pallas_call | solution.py:157
  37.0 1.9 %collective-permute-start.1 = (f32[8,128]{1,0:T(8,128)S(1)}, f32[8,128]{1,0:T(8,128)S(1)}, u32[]{:S(2)}, u32[]{:S(2)}) collective-permute-start(f32[8,128]{1,0:T(8,128)S(1)} %get-tuple-element.42), channel_id=1, source_target_pairs={{0,1},{1,2},{2,3},{3,4},{4,5},{5,6},{6,7},{7,8},{8,9},{9,10},{10,1... | collective-permute-start | bytes 12296 | tf_op jit(solution)/shard_map/ppermute | solution.py:468
  38.9 7.7 %collective-permute-done.1 = f32[8,128]{1,0:T(8,128)S(1)} collective-permute-done((f32[8,128]{1,0:T(8,128)S(1)}, f32[8,128]{1,0:T(8,128)S(1)}, u32[]{:S(2)}, u32[]{:S(2)}) %collective-permute-start.1) | collective-permute-done | bytes 4128 | tf_op jit(solution)/shard_map/ppermute | solution.py:468
  46.7 0.0 all-to-all-done
  46.7 17.4 %all_to_all.16 = f32[32,4,128]{2,1,0:T(4,128)S(1)} all-to-all(f32[32,4,128]{2,1,0:T(4,128)S(1)} %broadcast_in_dim.4), channel_id=1, replica_groups={{0,16,32,48,64,80,96,112,128,144,160,176,192,208,224,240,256,272,288,30..., dimensions={0} | all-to-all | bytes 131072 | tf_op jit(solution)/shard_map/all_to_all | solution.py:496
  64.1 0.7 shard_map.177.correction
  64.7 1.9 %collective-permute-start.2 = (f32[8,128]{1,0:T(8,128)S(1)}, f32[8,128]{1,0:T(8,128)S(1)}, u32[]{:S(2)}, u32[]{:S(2)}) collective-permute-start(f32[8,128]{1,0:T(8,128)S(1)} %shard_map.177.correction), channel_id=1, source_target_pairs={{1,0},{2,1},{3,2},{4,3},{5,4},{6,5},{7,6},{8,7},{9,8},{10,9},{11,1... | collective-permute-start | bytes 12296 | tf_op jit(solution)/shard_map/ppermute | solution.py:468
  66.6 1.3 %collective-permute-done.2.right = f32[8,128]{1,0:T(8,128)S(1)} collective-permute-done((f32[8,128]{1,0:T(8,128)S(1)}, f32[8,128]{1,0:T(8,128)S(1)}, u32[]{:S(2)}, u32[]{:S(2)}) %collective-permute-start.2) | collective-permute-done | bytes 4128 | tf_op jit(solution)/shard_map/ppermute | solution.py:468
  67.9 2.8 %shard_map.178 = (f32[3,4,16,128]{3,2,1,0:T(8,128)S(1)}, f32[3,4,16,128]{3,2,1,0:T(8,128)S(1)}, f32[72,128]{1,0:T(8,128)S(1)}, f32[3,4,32]{2,1,0:T(4,128)S(1)}) custom-call(f32[8,128]{1,0:T(8,128)S(1)} %shard_map.177.correction, f32[8,128]{1,0:T(8,128)S(1)} %collective-permute-done.2.right, f32[336,768]{1,0:T(8,128)S(1)} %get-tuple-element.46.state_grad, ...), custom_call_target="tpu_custom_call" | custom-call | tf_op jit(solution)/shard_map/pallas_call | solution.py:157
  70.8 1.9 %collective-permute-start.3 = (f32[72,128]{1,0:T(8,128)S(1)}, f32[72,128]{1,0:T(8,128)S(1)}, u32[]{:S(2)}, u32[]{:S(2)}) collective-permute-start(f32[72,128]{1,0:T(8,128)S(1)} %get-tuple-element.49), channel_id=1, source_target_pairs={{0,1},{1,2},{2,3},{3,4},{4,5},{5,6},{6,7},{7,8},{8,9},{9,10},{10,1... | collective-permute-start | bytes 110600 | tf_op jit(solution)/shard_map/ppermute | solution.py:468
  72.7 0.6 copy.20
  73.4 6.9 %collective-permute-done.3.arrived = f32[72,128]{1,0:T(8,128)S(1)} collective-permute-done((f32[72,128]{1,0:T(8,128)S(1)}, f32[72,128]{1,0:T(8,128)S(1)}, u32[]{:S(2)}, u32[]{:S(2)}) %collective-permute-start.3) | collective-permute-done | bytes 36896 | tf_op jit(solution)/shard_map/ppermute | solution.py:468
  80.3 0.7 shard_map.179
  (2 shorter events, 0.0 us)
Async XLA Ops:
  3.9 42.7 %all-to-all-start = ((f32[192,4,128]{2,1,0:T(4,128)}), f32[192,4,128]{2,1,0:T(4,128)S(1)}, u32[]{:S(2)}, u32[]{:S(2)}) async-start(f32[192,4,128]{2,1,0:T(4,128)} %bitcast.3), calls=%async_computation | async-start | bytes 786432 | tf_op jit(solution)/shard_map/all_to_all | solution.py:481
  24.8 9.3 %collective-permute-start = (f32[120,128]{1,0:T(8,128)S(1)}, f32[120,128]{1,0:T(8,128)S(1)}, u32[]{:S(2)}, u32[]{:S(2)}) collective-permute-start(f32[120,128]{1,0:T(8,128)S(1)} %get-tuple-element.32), channel_id=1, source_target_pairs={{1,0},{2,1},{3,2},{4,3},{5,4},{6,5},{7,6},{8,7},{9,8},{10,9},{11,1... | collective-permute-start | bytes 184328 | tf_op jit(solution)/shard_map/ppermute | solution.py:468
  37.0 9.7 %collective-permute-start.1 = (f32[8,128]{1,0:T(8,128)S(1)}, f32[8,128]{1,0:T(8,128)S(1)}, u32[]{:S(2)}, u32[]{:S(2)}) collective-permute-start(f32[8,128]{1,0:T(8,128)S(1)} %get-tuple-element.42), channel_id=1, source_target_pairs={{0,1},{1,2},{2,3},{3,4},{4,5},{5,6},{6,7},{7,8},{8,9},{9,10},{10,1... | collective-permute-start | bytes 12296 | tf_op jit(solution)/shard_map/ppermute | solution.py:468
  64.7 3.2 %collective-permute-start.2 = (f32[8,128]{1,0:T(8,128)S(1)}, f32[8,128]{1,0:T(8,128)S(1)}, u32[]{:S(2)}, u32[]{:S(2)}) collective-permute-start(f32[8,128]{1,0:T(8,128)S(1)} %shard_map.177.correction), channel_id=1, source_target_pairs={{1,0},{2,1},{3,2},{4,3},{5,4},{6,5},{7,6},{8,7},{9,8},{10,9},{11,1... | collective-permute-start | bytes 12296 | tf_op jit(solution)/shard_map/ppermute | solution.py:468
  70.8 9.5 %collective-permute-start.3 = (f32[72,128]{1,0:T(8,128)S(1)}, f32[72,128]{1,0:T(8,128)S(1)}, u32[]{:S(2)}, u32[]{:S(2)}) collective-permute-start(f32[72,128]{1,0:T(8,128)S(1)} %get-tuple-element.49), channel_id=1, source_target_pairs={{0,1},{1,2},{2,3},{3,4},{4,5},{5,6},{6,7},{7,8},{8,9},{9,10},{10,1... | collective-permute-start | bytes 110600 | tf_op jit(solution)/shard_map/ppermute | solution.py:468

commit v2 on v1

--- a/solution.py
+++ b/solution.py
@@ -152,7 +152,7 @@
     return pltpu.with_memory_space_constraint(x, pltpu.VMEM)
 
 
-def call(body, outs, *operands, scratch=()):
+def call(body, outs, *operands, scratch=(), cost=None):
     vmem = pl.BlockSpec(memory_space=pltpu.VMEM)
     return pl.pallas_call(
         body,
@@ -160,6 +160,7 @@
         in_specs=[vmem] * len(operands),
         out_specs=[vmem] * len(outs),
         scratch_shapes=list(scratch),
+        cost_estimate=cost,
         compiler_params=pltpu.CompilerParams(vmem_limit_bytes=24 * 2**20),
     )(*[near(x) for x in operands])
 
@@ -167,7 +168,7 @@
 def prepare_body(count, *refs):
     sources, refs = refs[:count], refs[count:]
     message, keep_rows, rows, weighting = refs[:4]
-    targets, done = refs[4:-1], refs[-1]
+    targets, (halves_of, done) = refs[4:-2], refs[-2:]
     copies = [
         pltpu.make_async_copy(source, target, done.at[i])
         for i, (source, target) in enumerate(zip(sources, targets))
@@ -195,18 +196,15 @@
                 message[48 + c * 16 : 48 + (c + 1) * 16, :] = state[c, 0]
     for i in range(count - 4, count):
         copies[i].wait()
-    row = lax.broadcasted_iota(jnp.int32, (64, 64), 0)
-    column = lax.broadcasted_iota(jnp.int32, (64, 64), 1)
-    order = (column == (row % 32) * 2 + row // 32).astype(F32)
+    halves_of[0] = inverse[:, 0:128]
+    halves_of[1] = jnp.concatenate([inverse[:, 128:192], jnp.zeros((384, 64), F32)], axis=1)
     for b in range(2):
         for c in range(3):
-            sorted_rows = exact(order, inverse[b, c * 64 : (c + 1) * 64, :])
             for q in range(2):
-                part = sorted_rows[q * 32 : (q + 1) * 32]
-                padded = jnp.concatenate([part, jnp.zeros((32, 64), F32)], axis=1)
+                source = pl.ds(b * 192 + c * 64 + q, 32, stride=2)
+                first = b * 32 * 12 + (q * 3 + c) * 2
                 for h in range(2):
-                    first = b * 32 * 12 + (q * 3 + c) * 2 + h
-                    rows[pl.ds(first, 32, stride=12), :] = padded[:, h * 128 : (h + 1) * 128]
+                    rows[pl.ds(first + h, 32, stride=12), :] = halves_of[h, source, :]
     weighting[...] = exact(exact(quad_y[...], stiffness[...]), quad_z[...])
     for i in range(2, count - 6):
         copies[i].wait()
@@ -224,6 +222,7 @@
         in_specs=[far] * len(operands),
         out_specs=[vmem] * len(outs),
         scratch_shapes=[pltpu.VMEM(x.shape, x.dtype) for x in used]
+        + [pltpu.VMEM((2, 384, 128), F32)]
         + [pltpu.SemaphoreType.DMA((len(operands),))],
         compiler_params=pltpu.CompilerParams(vmem_limit_bytes=24 * 2**20),
     )(*[pltpu.with_memory_space_constraint(x, pltpu.HBM) for x in operands])
@@ -472,8 +471,9 @@
     k = constants()
     names = ("along", "grads", "back_xy", "back_z", "back_along", "rest", "tables")
     kept = [state, direction, rhs] + [jnp.asarray(k[name]) for name in names] + [coarse_owner]
+    inverse = coarse_inverse.reshape(384, 192)
     used = [
-        clamp, coarse_owner, coarse_inverse[0], stiffness[0],
+        clamp, coarse_owner, inverse, stiffness[0],
         jnp.asarray(k["quad_y"]), jnp.asarray(k["quad_z"]),
     ]
     message, keep_rows, rows, weighting, state, direction, rhs, *shared, owner = prepare(kept, used)
@@ -487,7 +487,7 @@
         first_body,
         [big, (8, 128)],
         state, direction, rhs, keep_rows, halo, weighting, *shared, owner,
-        scratch=scratch,
+        scratch=scratch, cost=pl.CostEstimate(flops=20000000000, bytes_accessed=4 * 10**6, transcendentals=0),
     )
     arrived = shifted(sums, 1)
     total = jnp.broadcast_to((sums[0:4] + arrived[4:8])[None], (32, 4, 128)).reshape(128, 128)

time: 81.3 us -> 77.6 us (0.954)
  the two profiles are of different devices: /device:TPU:128 before, /device:TPU:2 now
where the time goes in v2:
time: 77.6 us; the launch traced here: 77.2 us
  starting transfers between devices  34.1 us (44%)
  blocking collectives  16.2 us (21%)
  waiting for transfers between devices  15.5 us (20%)
  Pallas kernels  9.98 us (13%)
    all_to_all x1, starting transfers between devices, shards(): lax.all_to_all(rows.reshape(192, 4, 128), 'grp', split_axis=0, concat_axi...  22.7 us
    all_to_all x1, blocking collectives, shards(): lax.all_to_all(total, 'grp', split_axis=0, concat_axis=0, tiled=True, axi...  16.2 us
    ppermute x4, starting transfers between devices, shifted(): return lax.ppermute(block, axes, route)  11.4 us
    ppermute x4, waiting for transfers between devices, shifted(): return lax.ppermute(block, axes, route)  11.3 us
    pallas_call x3, Pallas kernels, call(): pl.pallas_call(body, out_shape=[pltpu.VMEM(s, F32) for s in outs], in_spe...  6.32 us
    all_to_all x1, waiting for transfers between devices, shards(): lax.all_to_all(rows.reshape(192, 4, 128), 'grp', split_axis=0, concat_axi...  4.24 us
    pallas_call x1, Pallas kernels, prepare(): pl.pallas_call(functools.partial(prepare_body, len(operands)), out_shape=...  3.01 us
  transfers between devices with their start and end apart: 5, of which 4 were waited for; matrix products, arithmetic and copies ran while one was open for 1% of the time, Pallas kernels for 4%

profile of v2, /device:TPU:2, one launch (start us, length us, event | category | flops | bytes accessed | tf_op | source)
XLA Modules:
  0.0 77.2 jit_solution(12948508995589876882)
XLA Ops:
  0.6 3.0 %shard_map.175 = (f32[120,128]{1,0:T(8,128)S(1)}, f32[64,128]{1,0:T(8,128)S(1)}, f32[768,128]{1,0:T(8,128)}, f32[112,256]{1,0:T(8,128)S(1)}, f32[3,4,16,128]{3,2...) custom-call(f32[3,4,16,128]{3,2,1,0:T(8,128)} %refs_0_.1, ...), custom_call_target="tpu_custom_call" | custom-call | tf_op jit(solution)/shard_map/pallas_call | solution.py:219
  3.7 5.6 %collective-permute-start = (f32[120,128]{1,0:T(8,128)S(1)}, f32[120,128]{1,0:T(8,128)S(1)}, u32[]{:S(2)}, u32[]{:S(2)}) collective-permute-start(f32[120,128]{1,0:T(8,128)S(1)} %get-tuple-element.32), channel_id=1, source_target_pairs={{1,0},{2,1},{3,2},{4,3},{5,4},{6,5},{7,6},{8,7},{9,8},{10,9},{11,1... | collective-permute-start | bytes 184328 | tf_op jit(solution)/shard_map/ppermute | solution.py:467
  9.2 22.7 %all-to-all-start = ((f32[192,4,128]{2,1,0:T(4,128)}), f32[192,4,128]{2,1,0:T(4,128)S(1)}, u32[]{:S(2)}, u32[]{:S(2)}) async-start(f32[192,4,128]{2,1,0:T(4,128)} %bitcast.3), calls=%async_computation | async-start | bytes 786432 | tf_op jit(solution)/shard_map/all_to_all | solution.py:481
  32.0 0.0 collective-permute-done.halo
  32.0 2.8 %shard_map.176 = (f32[336,768]{1,0:T(8,128)S(1)}, f32[8,128]{1,0:T(8,128)S(1)}) custom-call(f32[3,4,16,128]{3,2,1,0:T(8,128)S(1)} %get-tuple-element.28.state, f32[3,4,16,128]{3,2,1,0:T(8,128)S(1)} %get-tuple-element.29.direction, f32[3,4,16,128]{3,2,1,0:T(8,128)S(1)} %get-tuple-element.30.rhs, f32[64,128]{1,0:T(8,128)S(1)} %get-tuple-element.31.keep_rows, ...), custom_call_target="tpu_custom_call" | custom-call | flops 20000000000 | bytes 4000000 | tf_op jit(solution)/shard_map/pallas_call | solution.py:157
  34.8 1.9 %collective-permute-start.1 = (f32[8,128]{1,0:T(8,128)S(1)}, f32[8,128]{1,0:T(8,128)S(1)}, u32[]{:S(2)}, u32[]{:S(2)}) collective-permute-start(f32[8,128]{1,0:T(8,128)S(1)} %get-tuple-element.42), channel_id=1, source_target_pairs={{0,1},{1,2},{2,3},{3,4},{4,5},{5,6},{6,7},{7,8},{8,9},{9,10},{10,1... | collective-permute-start | bytes 12296 | tf_op jit(solution)/shard_map/ppermute | solution.py:467
  36.8 5.1 %collective-permute-done.1 = f32[8,128]{1,0:T(8,128)S(1)} collective-permute-done((f32[8,128]{1,0:T(8,128)S(1)}, f32[8,128]{1,0:T(8,128)S(1)}, u32[]{:S(2)}, u32[]{:S(2)}) %collective-permute-start.1) | collective-permute-done | bytes 4128 | tf_op jit(solution)/shard_map/ppermute | solution.py:467
  41.9 4.2 %all-to-all-done = f32[192,4,128]{2,1,0:T(4,128)S(1)} async-done(((f32[192,4,128]{2,1,0:T(4,128)}), f32[192,4,128]{2,1,0:T(4,128)S(1)}, u32[]{:S(2)}, u32[]{:S(2)}) %all-to-all-start) | async-done | bytes 393248 | tf_op jit(solution)/shard_map/all_to_all | solution.py:481
  46.2 16.2 %all_to_all.16 = f32[32,4,128]{2,1,0:T(4,128)S(1)} all-to-all(f32[32,4,128]{2,1,0:T(4,128)S(1)} %broadcast_in_dim.4), channel_id=1, replica_groups={{0,16,32,48,64,80,96,112,128,144,160,176,192,208,224,240,256,272,288,30..., dimensions={0} | all-to-all | bytes 131072 | tf_op jit(solution)/shard_map/all_to_all | solution.py:496
  62.4 0.7 shard_map.177.correction
  63.1 1.9 %collective-permute-start.2 = (f32[8,128]{1,0:T(8,128)S(1)}, f32[8,128]{1,0:T(8,128)S(1)}, u32[]{:S(2)}, u32[]{:S(2)}) collective-permute-start(f32[8,128]{1,0:T(8,128)S(1)} %shard_map.177.correction), channel_id=1, source_target_pairs={{1,0},{2,1},{3,2},{4,3},{5,4},{6,5},{7,6},{8,7},{9,8},{10,9},{11,1... | collective-permute-start | bytes 12296 | tf_op jit(solution)/shard_map/ppermute | solution.py:467
  65.0 1.3 %collective-permute-done.2.right = f32[8,128]{1,0:T(8,128)S(1)} collective-permute-done((f32[8,128]{1,0:T(8,128)S(1)}, f32[8,128]{1,0:T(8,128)S(1)}, u32[]{:S(2)}, u32[]{:S(2)}) %collective-permute-start.2) | collective-permute-done | bytes 4128 | tf_op jit(solution)/shard_map/ppermute | solution.py:467
  66.3 2.8 %shard_map.178 = (f32[3,4,16,128]{3,2,1,0:T(8,128)S(1)}, f32[3,4,16,128]{3,2,1,0:T(8,128)S(1)}, f32[72,128]{1,0:T(8,128)S(1)}, f32[3,4,32]{2,1,0:T(4,128)S(1)}) custom-call(f32[8,128]{1,0:T(8,128)S(1)} %shard_map.177.correction, f32[8,128]{1,0:T(8,128)S(1)} %collective-permute-done.2.right, f32[336,768]{1,0:T(8,128)S(1)} %get-tuple-element.46.state_grad, ...), custom_call_target="tpu_custom_call" | custom-call | tf_op jit(solution)/shard_map/pallas_call | solution.py:157
  69.1 1.9 %collective-permute-start.3 = (f32[72,128]{1,0:T(8,128)S(1)}, f32[72,128]{1,0:T(8,128)S(1)}, u32[]{:S(2)}, u32[]{:S(2)}) collective-permute-start(f32[72,128]{1,0:T(8,128)S(1)} %get-tuple-element.49), channel_id=1, source_target_pairs={{0,1},{1,2},{2,3},{3,4},{4,5},{5,6},{6,7},{7,8},{8,9},{9,10},{10,1... | collective-permute-start | bytes 110600 | tf_op jit(solution)/shard_map/ppermute | solution.py:467
  71.1 0.6 copy.20
  71.7 4.8 %collective-permute-done.3.arrived = f32[72,128]{1,0:T(8,128)S(1)} collective-permute-done((f32[72,128]{1,0:T(8,128)S(1)}, f32[72,128]{1,0:T(8,128)S(1)}, u32[]{:S(2)}, u32[]{:S(2)}) %collective-permute-start.3) | collective-permute-done | bytes 36896 | tf_op jit(solution)/shard_map/ppermute | solution.py:467
  76.5 0.7 shard_map.179
  (2 shorter events, 0.0 us)
Async XLA Ops:
  3.7 28.3 %collective-permute-start = (f32[120,128]{1,0:T(8,128)S(1)}, f32[120,128]{1,0:T(8,128)S(1)}, u32[]{:S(2)}, u32[]{:S(2)}) collective-permute-start(f32[120,128]{1,0:T(8,128)S(1)} %get-tuple-element.32), channel_id=1, source_target_pairs={{1,0},{2,1},{3,2},{4,3},{5,4},{6,5},{7,6},{8,7},{9,8},{10,9},{11,1... | collective-permute-start | bytes 184328 | tf_op jit(solution)/shard_map/ppermute | solution.py:467
  9.2 36.9 %all-to-all-start = ((f32[192,4,128]{2,1,0:T(4,128)}), f32[192,4,128]{2,1,0:T(4,128)S(1)}, u32[]{:S(2)}, u32[]{:S(2)}) async-start(f32[192,4,128]{2,1,0:T(4,128)} %bitcast.3), calls=%async_computation | async-start | bytes 786432 | tf_op jit(solution)/shard_map/all_to_all | solution.py:481
  34.8 7.1 %collective-permute-start.1 = (f32[8,128]{1,0:T(8,128)S(1)}, f32[8,128]{1,0:T(8,128)S(1)}, u32[]{:S(2)}, u32[]{:S(2)}) collective-permute-start(f32[8,128]{1,0:T(8,128)S(1)} %get-tuple-element.42), channel_id=1, source_target_pairs={{0,1},{1,2},{2,3},{3,4},{4,5},{5,6},{6,7},{7,8},{8,9},{9,10},{10,1... | collective-permute-start | bytes 12296 | tf_op jit(solution)/shard_map/ppermute | solution.py:467
  63.1 3.2 %collective-permute-start.2 = (f32[8,128]{1,0:T(8,128)S(1)}, f32[8,128]{1,0:T(8,128)S(1)}, u32[]{:S(2)}, u32[]{:S(2)}) collective-permute-start(f32[8,128]{1,0:T(8,128)S(1)} %shard_map.177.correction), channel_id=1, source_target_pairs={{1,0},{2,1},{3,2},{4,3},{5,4},{6,5},{7,6},{8,7},{9,8},{10,9},{11,1... | collective-permute-start | bytes 12296 | tf_op jit(solution)/shard_map/ppermute | solution.py:467
  69.1 7.4 %collective-permute-start.3 = (f32[72,128]{1,0:T(8,128)S(1)}, f32[72,128]{1,0:T(8,128)S(1)}, u32[]{:S(2)}, u32[]{:S(2)}) collective-permute-start(f32[72,128]{1,0:T(8,128)S(1)} %get-tuple-element.49), channel_id=1, source_target_pairs={{0,1},{1,2},{2,3},{3,4},{4,5},{5,6},{6,7},{7,8},{8,9},{9,10},{10,1... | collective-permute-start | bytes 110600 | tf_op jit(solution)/shard_map/ppermute | solution.py:467

commit v3 on v2

--- a/solution.py
+++ b/solution.py
@@ -173,8 +173,9 @@
         pltpu.make_async_copy(source, target, done.at[i])
         for i, (source, target) in enumerate(zip(sources, targets))
     ]
-    for copy in copies:
-        copy.start()
+    urgent = (0, 1, count - 6, count - 5, count - 4)
+    for i in urgent + tuple(i for i in range(count) if i not in urgent):
+        copies[i].start()
     state, direction = targets[0], targets[1]
     clamp, owner, inverse, stiffness, quad_y, quad_z = targets[-6:]
     for i in (0, 1, count - 6, count - 5):
@@ -197,14 +198,18 @@
     for i in range(count - 4, count):
         copies[i].wait()
     halves_of[0] = inverse[:, 0:128]
-    halves_of[1] = jnp.concatenate([inverse[:, 128:192], jnp.zeros((384, 64), F32)], axis=1)
+    halves_of[1] = jnp.concatenate([inverse[:, 128:192]] * 2, axis=1)
+    low = lax.broadcasted_iota(jnp.int32, (32, 128), 1) < 64
     for b in range(2):
         for c in range(3):
-            for q in range(2):
-                source = pl.ds(b * 192 + c * 64 + q, 32, stride=2)
-                first = b * 32 * 12 + (q * 3 + c) * 2
-                for h in range(2):
-                    rows[pl.ds(first + h, 32, stride=12), :] = halves_of[h, source, :]
+            first, second = [pl.ds(b * 192 + c * 64 + q, 32, stride=2) for q in range(2)]
+            values = (
+                halves_of[0, first, :],
+                jnp.where(low, halves_of[1, first, :], halves_of[1, second, :]),
+                halves_of[0, second, :],
+            )
+            for i in range(3):
+                rows[pl.ds(b * 32 * 9 + c * 3 + i, 32, stride=9), :] = values[i]
     weighting[...] = exact(exact(quad_y[...], stiffness[...]), quad_z[...])
     for i in range(2, count - 6):
         copies[i].wait()
@@ -214,7 +219,7 @@
     operands = list(kept) + list(used)
     far = pl.BlockSpec(memory_space=pltpu.HBM)
     vmem = pl.BlockSpec(memory_space=pltpu.VMEM)
-    made = [(120, 128), (64, 128), (768, 128), (ROWS, WIDE)]
+    made = [(120, 128), (64, 128), (576, 128), (ROWS, WIDE)]
     outs = [pltpu.VMEM(s, F32) for s in made] + [pltpu.VMEM(x.shape, x.dtype) for x in kept]
     return pl.pallas_call(
         functools.partial(prepare_body, len(operands)),
@@ -358,22 +363,28 @@
 def solve_body(gathered, rows, owner, correction):
     tn = (((0,), (0,)), ((), ()))
     values = gathered[...]
-    row = lax.broadcasted_iota(jnp.int32, (128, 256), 0)
-    lane = lax.broadcasted_iota(jnp.int32, (128, 256), 1)
-    match = (row // 4 == lane % 64 // 2) & (row % 4 == lane // 64) & (lane < 192)
+    row = lax.broadcasted_iota(jnp.int32, (256, 256), 0)
+    lane = lax.broadcasted_iota(jnp.int32, (256, 256), 1)
+    side = lax.axis_index("grp") // 32
+    holder = row // 8
+    target = jnp.where(row % 8 < 4, holder, holder + 1 - jnp.where(holder % 8 == 7, 8 * side, 0))
+    column = jnp.where(lane < 192, lane, lane - 64)
+    match = (target == column % 64 // 2) & (row % 4 == column // 64)
     need = None
     for q in range(2):
-        pick = (match & (lane % 2 == q)).astype(BF16)
+        pick = (match & (column % 2 == q)).astype(BF16)
         for part in split(values[:, q * 64 : (q + 1) * 64]):
             term = lax.dot_general(part, pick, tn, preferred_element_type=F32)
             need = term if need is None else need + term
-    products = []
-    for k in range(6):
-        product = None
-        for h in range(2):
-            term = rows[pl.ds(2 * k + h, 64, stride=12), :] * need[:, h * 128 : (h + 1) * 128]
-            product = term if product is None else product + term
-        products.append(product)
+    low = lax.broadcasted_iota(jnp.int32, (64, 128), 1) < 64
+    inner, outer = need[:, 0:128], need[:, 128:256]
+    products = [[], []]
+    for c in range(3):
+        shared = rows[pl.ds(c * 3 + 1, 64, stride=9), :] * outer
+        for q in range(2):
+            own = rows[pl.ds(c * 3 + 2 * q, 64, stride=9), :] * inner
+            products[q].append(own + jnp.where(low == (q == 0), shared, 0.0))
+    products = products[0] + products[1]
     ones = jnp.ones((128, 128), BF16)
     sums = sum(dot(part, ones) for part in split(jnp.concatenate(products, axis=0)))
     lane = lax.broadcasted_iota(jnp.int32, (64, 128), 1)
@@ -467,6 +478,18 @@
     return lax.ppermute(block, axes, route)
 
 
+def ring():
+    groups, members = lax.axis_size("grp"), lax.axis_size("mem")
+    route = []
+    for g in range(groups):
+        route += [(g * members + m, g * members + m + 1) for m in range(members - 1)]
+        last = g >= groups // 2 - 1 and g % 8 == 7
+        to = g + 8 if last else g
+        if to < groups:
+            route.append((g * members + members - 1, to * members))
+    return route
+
+
 def shards(state, direction, rhs, clamp, stiffness, coarse_owner, coarse_inverse):
     k = constants()
     names = ("along", "grads", "back_xy", "back_z", "back_along", "rest", "tables")
@@ -479,8 +502,8 @@
     message, keep_rows, rows, weighting, state, direction, rhs, *shared, owner = prepare(kept, used)
     halo = shifted(message, -1)
     rows = lax.all_to_all(
-        rows.reshape(192, 4, 128), "grp", split_axis=0, concat_axis=0, tiled=True
-    ).reshape(768, 128)
+        rows.reshape(576, 1, 128), "grp", split_axis=0, concat_axis=0, tiled=True
+    ).reshape(576, 128)
     big = (3 * ROWS, 3 * WIDE)
     scratch = (pltpu.VMEM(big, F32), pltpu.VMEM(big, F32))
     state_grad, sums = call(
@@ -489,8 +512,12 @@
         state, direction, rhs, keep_rows, halo, weighting, *shared, owner,
         scratch=scratch, cost=pl.CostEstimate(flops=20000000000, bytes_accessed=4 * 10**6, transcendentals=0),
     )
-    arrived = shifted(sums, 1)
-    total = jnp.broadcast_to((sums[0:4] + arrived[4:8])[None], (32, 4, 128)).reshape(128, 128)
+    arrived = lax.ppermute(sums, ("grp", "mem"), ring())[4:8]
+    wraps = lax.axis_index("mem") == 0
+    total = jnp.concatenate(
+        [sums[0:4] + jnp.where(wraps, 0.0, arrived), jnp.where(wraps, arrived, 0.0)], axis=0
+    )
+    total = jnp.broadcast_to(total[None], (32, 8, 128)).reshape(256, 128)
     total, rows = lax.optimization_barrier((total, rows))
     sides = [list(range(32)), list(range(32, 64))]
     gathered = lax.all_to_all(

time: 77.6 us -> 75.9 us (0.978)
  waiting for transfers between devices: 15.5 us -> 14.6 us
    ppermute x4 -> x3, waiting for transfers between devices: 11.3 us -> 6.12 us  [shifted(): return lax.ppermute(block, axes, route)]
    ppermute x0 -> x1, waiting for transfers between devices: none -> 4.2 us  [shards(): arrived = lax.ppermute(sums, ('grp', 'mem'), ring())[4:8]]
    ppermute x4 -> x3, starting transfers between devices: 11.4 us -> 9.43 us  [shifted(): return lax.ppermute(block, axes, route)]
    ppermute x0 -> x1, starting transfers between devices: none -> 1.94 us  [shards(): arrived = lax.ppermute(sums, ('grp', 'mem'), ring())[4:8]]
where the time goes in v3:
time: 75.9 us; the launch traced here: 75.6 us
  starting transfers between devices  34.1 us (45%)
  blocking collectives  15.5 us (20%)
  waiting for transfers between devices  14.6 us (19%)
  Pallas kernels  9.94 us (13%)
    all_to_all x1, starting transfers between devices, shards(): lax.all_to_all(rows.reshape(576, 1, 128), 'grp', split_axis=0, concat_axi...  22.7 us
    all_to_all x1, blocking collectives, shards(): lax.all_to_all(total, 'grp', split_axis=0, concat_axis=0, tiled=True, axi...  15.5 us
    ppermute x3, starting transfers between devices, shifted(): return lax.ppermute(block, axes, route)  9.43 us
    pallas_call x3, Pallas kernels, call(): pl.pallas_call(body, out_shape=[pltpu.VMEM(s, F32) for s in outs], in_spe...  6.38 us
    ppermute x3, waiting for transfers between devices, shifted(): return lax.ppermute(block, axes, route)  6.12 us
    all_to_all x1, waiting for transfers between devices, shards(): lax.all_to_all(rows.reshape(576, 1, 128), 'grp', split_axis=0, concat_axi...  4.29 us
    ppermute x1, waiting for transfers between devices, shards(): arrived = lax.ppermute(sums, ('grp', 'mem'), ring())[4:8]  4.2 us
    pallas_call x1, Pallas kernels, prepare(): pl.pallas_call(functools.partial(prepare_body, len(operands)), out_shape=...  2.9 us
  transfers between devices with their start and end apart: 5, of which 4 were waited for; matrix products, arithmetic and copies ran while one was open for 1% of the time, Pallas kernels for 4%

profile of v3, /device:TPU:2, one launch (start us, length us, event | category | flops | bytes accessed | tf_op | source)
XLA Modules:
  0.0 75.6 jit_solution(15123910975373260910)
XLA Ops:
  0.6 2.9 %shard_map.175 = (f32[120,128]{1,0:T(8,128)S(1)}, f32[64,128]{1,0:T(8,128)S(1)}, f32[576,128]{1,0:T(8,128)}, f32[112,256]{1,0:T(8,128)S(1)}, f32[3,4,16,128]{3,2...) custom-call(f32[3,4,16,128]{3,2,1,0:T(8,128)} %refs_0_.1, ...), custom_call_target="tpu_custom_call" | custom-call | tf_op jit(solution)/shard_map/pallas_call | solution.py:224
  3.5 5.6 %collective-permute-start = (f32[120,128]{1,0:T(8,128)S(1)}, f32[120,128]{1,0:T(8,128)S(1)}, u32[]{:S(2)}, u32[]{:S(2)}) collective-permute-start(f32[120,128]{1,0:T(8,128)S(1)} %get-tuple-element.32), channel_id=1, source_target_pairs={{1,0},{2,1},{3,2},{4,3},{5,4},{6,5},{7,6},{8,7},{9,8},{10,9},{11,1... | collective-permute-start | bytes 184328 | tf_op jit(solution)/shard_map/ppermute | solution.py:478
  9.1 22.7 %all-to-all-start = ((f32[576,1,128]{2,1,0:T(1,128)}), f32[576,1,128]{2,1,0:T(1,128)S(1)}, u32[]{:S(2)}, u32[]{:S(2)}) async-start(f32[576,1,128]{2,1,0:T(1,128)} %bitcast.4), calls=%async_computation | async-start | bytes 589824 | tf_op jit(solution)/shard_map/all_to_all | solution.py:504
  31.9 0.0 collective-permute-done.halo
  31.9 2.8 %shard_map.176 = (f32[336,768]{1,0:T(8,128)S(1)}, f32[8,128]{1,0:T(8,128)S(1)}) custom-call(f32[3,4,16,128]{3,2,1,0:T(8,128)S(1)} %get-tuple-element.28.state, f32[3,4,16,128]{3,2,1,0:T(8,128)S(1)} %get-tuple-element.29.direction, f32[3,4,16,128]{3,2,1,0:T(8,128)S(1)} %get-tuple-element.30.rhs, f32[64,128]{1,0:T(8,128)S(1)} %get-tuple-element.31.keep_rows, ...), custom_call_target="tpu_custom_call" | custom-call | flops 20000000000 | bytes 4000000 | tf_op jit(solution)/shard_map/pallas_call | solution.py:157
  34.7 1.9 %collective-permute-start.1 = (f32[8,128]{1,0:T(8,128)S(1)}, f32[8,128]{1,0:T(8,128)S(1)}, u32[]{:S(2)}, u32[]{:S(2)}) collective-permute-start(f32[8,128]{1,0:T(8,128)S(1)} %get-tuple-element.42), channel_id=1, source_target_pairs={{0,1},{1,2},{2,3},{3,4},{4,5},{5,6},{6,7},{7,8},{8,9},{9,10},{10,1... | collective-permute-start | bytes 12296 | tf_op jit(solution)/shard_map/ppermute | solution.py:515
  36.6 4.2 %collective-permute-done.1 = f32[8,128]{1,0:T(8,128)S(1)} collective-permute-done((f32[8,128]{1,0:T(8,128)S(1)}, f32[8,128]{1,0:T(8,128)S(1)}, u32[]{:S(2)}, u32[]{:S(2)}) %collective-permute-start.1) | collective-permute-done | bytes 4128 | tf_op jit(solution)/shard_map/ppermute | solution.py:515
  40.9 4.3 %all-to-all-done = f32[576,1,128]{2,1,0:T(1,128)S(1)} async-done(((f32[576,1,128]{2,1,0:T(1,128)}), f32[576,1,128]{2,1,0:T(1,128)S(1)}, u32[]{:S(2)}, u32[]{:S(2)}) %all-to-all-start) | async-done | bytes 294944 | tf_op jit(solution)/shard_map/all_to_all | solution.py:504
  45.2 15.5 %all_to_all.16 = f32[32,8,128]{2,1,0:T(8,128)S(1)} all-to-all(f32[32,8,128]{2,1,0:T(8,128)S(1)} %bitcast.15), channel_id=1, replica_groups={{0,16,32,48,64,80,96,112,128,144,160,176,192,208,224,240,256,272,288,30..., dimensions={0} | all-to-all | bytes 262144 | tf_op jit(solution)/shard_map/all_to_all | solution.py:523
  60.7 0.7 shard_map.177.correction
  61.5 1.9 %collective-permute-start.2 = (f32[8,128]{1,0:T(8,128)S(1)}, f32[8,128]{1,0:T(8,128)S(1)}, u32[]{:S(2)}, u32[]{:S(2)}) collective-permute-start(f32[8,128]{1,0:T(8,128)S(1)} %shard_map.177.correction), channel_id=1, source_target_pairs={{1,0},{2,1},{3,2},{4,3},{5,4},{6,5},{7,6},{8,7},{9,8},{10,9},{11,1... | collective-permute-start | bytes 12296 | tf_op jit(solution)/shard_map/ppermute | solution.py:478
  63.4 1.3 %collective-permute-done.2.right = f32[8,128]{1,0:T(8,128)S(1)} collective-permute-done((f32[8,128]{1,0:T(8,128)S(1)}, f32[8,128]{1,0:T(8,128)S(1)}, u32[]{:S(2)}, u32[]{:S(2)}) %collective-permute-start.2) | collective-permute-done | bytes 4128 | tf_op jit(solution)/shard_map/ppermute | solution.py:478
  64.7 2.8 %shard_map.178 = (f32[3,4,16,128]{3,2,1,0:T(8,128)S(1)}, f32[3,4,16,128]{3,2,1,0:T(8,128)S(1)}, f32[72,128]{1,0:T(8,128)S(1)}, f32[3,4,32]{2,1,0:T(4,128)S(1)}) custom-call(f32[8,128]{1,0:T(8,128)S(1)} %shard_map.177.correction, f32[8,128]{1,0:T(8,128)S(1)} %collective-permute-done.2.right, f32[336,768]{1,0:T(8,128)S(1)} %get-tuple-element.46.state_grad, ...), custom_call_target="tpu_custom_call" | custom-call | tf_op jit(solution)/shard_map/pallas_call | solution.py:157
  67.5 1.9 %collective-permute-start.3 = (f32[72,128]{1,0:T(8,128)S(1)}, f32[72,128]{1,0:T(8,128)S(1)}, u32[]{:S(2)}, u32[]{:S(2)}) collective-permute-start(f32[72,128]{1,0:T(8,128)S(1)} %get-tuple-element.49), channel_id=1, source_target_pairs={{0,1},{1,2},{2,3},{3,4},{4,5},{5,6},{6,7},{7,8},{8,9},{9,10},{10,1... | collective-permute-start | bytes 110600 | tf_op jit(solution)/shard_map/ppermute | solution.py:478
  69.5 0.6 copy.22
  70.1 4.8 %collective-permute-done.3.arrived = f32[72,128]{1,0:T(8,128)S(1)} collective-permute-done((f32[72,128]{1,0:T(8,128)S(1)}, f32[72,128]{1,0:T(8,128)S(1)}, u32[]{:S(2)}, u32[]{:S(2)}) %collective-permute-start.3) | collective-permute-done | bytes 36896 | tf_op jit(solution)/shard_map/ppermute | solution.py:478
  74.9 0.7 shard_map.179
  (3 shorter events, 0.0 us)
Async XLA Ops:
  3.5 28.3 %collective-permute-start = (f32[120,128]{1,0:T(8,128)S(1)}, f32[120,128]{1,0:T(8,128)S(1)}, u32[]{:S(2)}, u32[]{:S(2)}) collective-permute-start(f32[120,128]{1,0:T(8,128)S(1)} %get-tuple-element.32), channel_id=1, source_target_pairs={{1,0},{2,1},{3,2},{4,3},{5,4},{6,5},{7,6},{8,7},{9,8},{10,9},{11,1... | collective-permute-start | bytes 184328 | tf_op jit(solution)/shard_map/ppermute | solution.py:478
  9.1 36.0 %all-to-all-start = ((f32[576,1,128]{2,1,0:T(1,128)}), f32[576,1,128]{2,1,0:T(1,128)S(1)}, u32[]{:S(2)}, u32[]{:S(2)}) async-start(f32[576,1,128]{2,1,0:T(1,128)} %bitcast.4), calls=%async_computation | async-start | bytes 589824 | tf_op jit(solution)/shard_map/all_to_all | solution.py:504
  34.7 6.2 %collective-permute-start.1 = (f32[8,128]{1,0:T(8,128)S(1)}, f32[8,128]{1,0:T(8,128)S(1)}, u32[]{:S(2)}, u32[]{:S(2)}) collective-permute-start(f32[8,128]{1,0:T(8,128)S(1)} %get-tuple-element.42), channel_id=1, source_target_pairs={{0,1},{1,2},{2,3},{3,4},{4,5},{5,6},{6,7},{7,8},{8,9},{9,10},{10,1... | collective-permute-start | bytes 12296 | tf_op jit(solution)/shard_map/ppermute | solution.py:515
  61.5 3.2 %collective-permute-start.2 = (f32[8,128]{1,0:T(8,128)S(1)}, f32[8,128]{1,0:T(8,128)S(1)}, u32[]{:S(2)}, u32[]{:S(2)}) collective-permute-start(f32[8,128]{1,0:T(8,128)S(1)} %shard_map.177.correction), channel_id=1, source_target_pairs={{1,0},{2,1},{3,2},{4,3},{5,4},{6,5},{7,6},{8,7},{9,8},{10,9},{11,1... | collective-permute-start | bytes 12296 | tf_op jit(solution)/shard_map/ppermute | solution.py:478
  67.5 7.4 %collective-permute-start.3 = (f32[72,128]{1,0:T(8,128)S(1)}, f32[72,128]{1,0:T(8,128)S(1)}, u32[]{:S(2)}, u32[]{:S(2)}) collective-permute-start(f32[72,128]{1,0:T(8,128)S(1)} %get-tuple-element.49), channel_id=1, source_target_pairs={{0,1},{1,2},{2,3},{3,4},{4,5},{5,6},{6,7},{7,8},{8,9},{9,10},{10,1... | collective-permute-start | bytes 110600 | tf_op jit(solution)/shard_map/ppermute | solution.py:478

commit v4 on v3

--- a/solution.py
+++ b/solution.py
@@ -152,7 +152,7 @@
     return pltpu.with_memory_space_constraint(x, pltpu.VMEM)
 
 
-def call(body, outs, *operands, scratch=(), cost=None):
+def call(body, outs, *operands, scratch=()):
     vmem = pl.BlockSpec(memory_space=pltpu.VMEM)
     return pl.pallas_call(
         body,
@@ -160,26 +160,37 @@
         in_specs=[vmem] * len(operands),
         out_specs=[vmem] * len(outs),
         scratch_shapes=list(scratch),
-        cost_estimate=cost,
         compiler_params=pltpu.CompilerParams(vmem_limit_bytes=24 * 2**20),
     )(*[near(x) for x in operands])
 
 
-def prepare_body(count, *refs):
-    sources, refs = refs[:count], refs[count:]
-    message, keep_rows, rows, weighting = refs[:4]
-    targets, (halves_of, done) = refs[4:-2], refs[-2:]
+def loads(pairs, done):
     copies = [
         pltpu.make_async_copy(source, target, done.at[i])
-        for i, (source, target) in enumerate(zip(sources, targets))
+        for i, (source, target) in enumerate(pairs)
     ]
-    urgent = (0, 1, count - 6, count - 5, count - 4)
-    for i in urgent + tuple(i for i in range(count) if i not in urgent):
-        copies[i].start()
-    state, direction = targets[0], targets[1]
-    clamp, owner, inverse, stiffness, quad_y, quad_z = targets[-6:]
-    for i in (0, 1, count - 6, count - 5):
-        copies[i].wait()
+    for copy in copies:
+        copy.start()
+    return copies
+
+
+def prepare_body(
+    state_in, direction_in, clamp_in, owner_in, inverse_in, message, keep_rows, rows, state,
+    direction, owner, clamp, inverse, halves_of, done,
+):
+    copies = loads(
+        (
+            (inverse_in, inverse),
+            (inverse_in.at[:, 0:128], halves_of.at[0]),
+            (clamp_in, clamp),
+            (owner_in, owner),
+            (direction_in, direction),
+            (state_in, state),
+        ),
+        done,
+    )
+    for copy in copies[2:]:
+        copy.wait()
     eye = lax.broadcasted_iota(jnp.int32, (16, 16), 0) == lax.broadcasted_iota(
         jnp.int32, (16, 16), 1
     )
@@ -195,9 +206,8 @@
             for c in range(3):
                 message[c * 16 : (c + 1) * 16, :] = keep * direction[c, 0]
                 message[48 + c * 16 : 48 + (c + 1) * 16, :] = state[c, 0]
-    for i in range(count - 4, count):
-        copies[i].wait()
-    halves_of[0] = inverse[:, 0:128]
+    for copy in copies[:2]:
+        copy.wait()
     halves_of[1] = jnp.concatenate([inverse[:, 128:192]] * 2, axis=1)
     low = lax.broadcasted_iota(jnp.int32, (32, 128), 1) < 64
     for b in range(2):
@@ -210,25 +220,26 @@
             )
             for i in range(3):
                 rows[pl.ds(b * 32 * 9 + c * 3 + i, 32, stride=9), :] = values[i]
-    weighting[...] = exact(exact(quad_y[...], stiffness[...]), quad_z[...])
-    for i in range(2, count - 6):
-        copies[i].wait()
-
-
-def prepare(kept, used):
-    operands = list(kept) + list(used)
+
+
+def prepare(state, direction, clamp, owner, inverse):
+    operands = (state, direction, clamp, owner, inverse)
     far = pl.BlockSpec(memory_space=pltpu.HBM)
     vmem = pl.BlockSpec(memory_space=pltpu.VMEM)
-    made = [(120, 128), (64, 128), (576, 128), (ROWS, WIDE)]
-    outs = [pltpu.VMEM(s, F32) for s in made] + [pltpu.VMEM(x.shape, x.dtype) for x in kept]
+    outs = [pltpu.VMEM(s, F32) for s in ((120, 128), (64, 128), (576, 128))] + [
+        pltpu.VMEM(x.shape, x.dtype) for x in (state, direction, owner)
+    ]
     return pl.pallas_call(
-        functools.partial(prepare_body, len(operands)),
+        prepare_body,
         out_shape=outs,
         in_specs=[far] * len(operands),
         out_specs=[vmem] * len(outs),
-        scratch_shapes=[pltpu.VMEM(x.shape, x.dtype) for x in used]
-        + [pltpu.VMEM((2, 384, 128), F32)]
-        + [pltpu.SemaphoreType.DMA((len(operands),))],
+        scratch_shapes=[
+            pltpu.VMEM(clamp.shape, clamp.dtype),
+            pltpu.VMEM(inverse.shape, F32),
+            pltpu.VMEM((2, 384, 128), F32),
+            pltpu.SemaphoreType.DMA((6,)),
+        ],
         compiler_params=pltpu.CompilerParams(vmem_limit_bytes=24 * 2**20),
     )(*[pltpu.with_memory_space_constraint(x, pltpu.HBM) for x in operands])
 
@@ -315,14 +326,52 @@
     return jnp.concatenate([levels[:8, c * 128 : (c + 1) * 128] for c in range(3)], axis=0)
 
 
+def first_apply(ready, kept, used, scratch):
+    far = pl.BlockSpec(memory_space=pltpu.HBM)
+    vmem = pl.BlockSpec(memory_space=pltpu.VMEM)
+    made = [(3 * ROWS, 3 * WIDE), (8, 128), (ROWS, WIDE)]
+    outs = [pltpu.VMEM(s, F32) for s in made] + [pltpu.VMEM(x.shape, x.dtype) for x in kept]
+    return pl.pallas_call(
+        first_body,
+        out_shape=outs,
+        in_specs=[vmem] * len(ready) + [far] * (len(kept) + len(used)),
+        out_specs=[vmem] * len(outs),
+        scratch_shapes=[pltpu.VMEM(x.shape, x.dtype) for x in used]
+        + scratch
+        + [pltpu.SemaphoreType.DMA((len(kept) + len(used),))],
+        cost_estimate=pl.CostEstimate(flops=2 * 10**10, bytes_accessed=4 * 10**6, transcendentals=0),
+        compiler_params=pltpu.CompilerParams(vmem_limit_bytes=24 * 2**20),
+    )(
+        *[near(x) for x in ready],
+        *[pltpu.with_memory_space_constraint(x, pltpu.HBM) for x in kept + used],
+    )
+
+
 def own_rows(ref, c):
     return ref[c].reshape(64, 128)
 
 
 def first_body(
-    state, direction, rhs, keep_rows, halo, weighting, along, grads, back_xy, back_z, back_along,
-    rest, tables, owner, state_grad, sums, grad, flux,
+    state, direction, keep_rows, halo, owner, rhs_in, along_in, grads_in, xy_in, z_in, back_in,
+    rest_in, tables_in, stiffness_in, quad_y_in, quad_z_in, state_grad, sums, weighting, rhs, along,
+    grads, back_xy, back_z, back_along, rest, tables, stiffness, quad_y, quad_z, grad, flux, done,
 ):
+    copies = loads(
+        (
+            (along_in, along),
+            (grads_in, grads),
+            (stiffness_in, stiffness),
+            (quad_y_in, quad_y),
+            (quad_z_in, quad_z),
+            (xy_in, back_xy),
+            (z_in, back_z),
+            (back_in, back_along),
+            (rhs_in, rhs),
+            (rest_in, rest),
+            (tables_in, tables),
+        ),
+        done,
+    )
     keep = keep_rows[...]
     fields = [
         [jnp.concatenate([own_rows(state, c), halo[48 + c * 16 : 64 + c * 16, :]], axis=0) for c in range(3)],
@@ -331,7 +380,12 @@
             for c in range(3)
         ],
     ]
+    for copy in copies[:5]:
+        copy.wait()
+    weighting[...] = exact(exact(quad_y[...], stiffness[...]), quad_z[...])
     gradients(fields, along, grads, (state_grad, grad))
+    for copy in copies[5:]:
+        copy.wait()
     physics(state_grad, grad, weighting, flux)
     image = images(flux, back_xy, back_z, back_along)
     keep_right = halo[96:112, :]
@@ -493,24 +547,19 @@
 def shards(state, direction, rhs, clamp, stiffness, coarse_owner, coarse_inverse):
     k = constants()
     names = ("along", "grads", "back_xy", "back_z", "back_along", "rest", "tables")
-    kept = [state, direction, rhs] + [jnp.asarray(k[name]) for name in names] + [coarse_owner]
-    inverse = coarse_inverse.reshape(384, 192)
-    used = [
-        clamp, coarse_owner, inverse, stiffness[0],
-        jnp.asarray(k["quad_y"]), jnp.asarray(k["quad_z"]),
-    ]
-    message, keep_rows, rows, weighting, state, direction, rhs, *shared, owner = prepare(kept, used)
+    message, keep_rows, rows, state, direction, owner = prepare(
+        state, direction, clamp, coarse_owner, coarse_inverse.reshape(384, 192)
+    )
     halo = shifted(message, -1)
     rows = lax.all_to_all(
         rows.reshape(576, 1, 128), "grp", split_axis=0, concat_axis=0, tiled=True
     ).reshape(576, 128)
-    big = (3 * ROWS, 3 * WIDE)
-    scratch = (pltpu.VMEM(big, F32), pltpu.VMEM(big, F32))
-    state_grad, sums = call(
-        first_body,
-        [big, (8, 128)],
-        state, direction, rhs, keep_rows, halo, weighting, *shared, owner,
-        scratch=scratch, cost=pl.CostEstimate(flops=20000000000, bytes_accessed=4 * 10**6, transcendentals=0),
+    scratch = [pltpu.VMEM((3 * ROWS, 3 * WIDE), F32)] * 2
+    state_grad, sums, weighting, rhs, *shared = first_apply(
+        (state, direction, keep_rows, halo, owner),
+        (rhs, *[jnp.asarray(k[name]) for name in names]),
+        (stiffness[0], jnp.asarray(k["quad_y"]), jnp.asarray(k["quad_z"])),
+        scratch,
     )
     arrived = lax.ppermute(sums, ("grp", "mem"), ring())[4:8]
     wraps = lax.axis_index("mem") == 0

time: 75.9 us -> 76.6 us (level)
  blocking collectives: 15.5 us -> 17 us
  waiting for transfers between devices: 14.6 us -> 13.2 us
    pallas_call x1 -> x2, Pallas kernels: 2.9 us -> 6.45 us  [the longest x1 4.28 us: first_apply(): pl.pallas_call(first_body, out_shape=outs, in_specs=[vmem] * len(ready) +...]
    pallas_call x3 -> x2, Pallas kernels: 6.38 us -> 3.56 us  [call(): pl.pallas_call(body, out_shape=[pltpu.VMEM(s, F32) for s in outs], in_spe...]
    all_to_all x1, waiting for transfers between devices: 4.29 us -> 2.84 us  [shards(): lax.all_to_all(rows.reshape(576, 1, 128), 'grp', split_axis=0, concat_axi...]
    all_to_all x1, blocking collectives: 15.5 us -> 17 us  [shards(): lax.all_to_all(total, 'grp', split_axis=0, concat_axis=0, tiled=True, axi...]
  transfers between devices with their start and end apart: 5 -> 5, of which waited for: 4 -> 4; matrix products, arithmetic and copies ran while one was open for 1% -> 1% of each run, Pallas kernels for 4% -> 6%
where the time goes in v4:
time: 76.6 us; the launch traced here: 76.3 us
  starting transfers between devices  34.1 us (45%)
  blocking collectives  17 us (22%)
  waiting for transfers between devices  13.2 us (17%)
  Pallas kernels  10.7 us (14%)
    all_to_all x1, starting transfers between devices, shards(): lax.all_to_all(rows.reshape(576, 1, 128), 'grp', split_axis=0, concat_axi...  22.7 us
    all_to_all x1, blocking collectives, shards(): lax.all_to_all(total, 'grp', split_axis=0, concat_axis=0, tiled=True, axi...  17 us
    ppermute x3, starting transfers between devices, shifted(): return lax.ppermute(block, axes, route)  9.43 us
    ppermute x3, waiting for transfers between devices, shifted(): return lax.ppermute(block, axes, route)  6.12 us
    pallas_call x1, Pallas kernels, first_apply(): pl.pallas_call(first_body, out_shape=outs, in_specs=[vmem] * len(ready) +...  4.28 us
    ppermute x1, waiting for transfers between devices, shards(): arrived = lax.ppermute(sums, ('grp', 'mem'), ring())[4:8]  4.2 us
    pallas_call x2, Pallas kernels, call(): pl.pallas_call(body, out_shape=[pltpu.VMEM(s, F32) for s in outs], in_spe...  3.56 us
    all_to_all x1, waiting for transfers between devices, shards(): lax.all_to_all(rows.reshape(576, 1, 128), 'grp', split_axis=0, concat_axi...  2.84 us
  transfers between devices with their start and end apart: 5, of which 4 were waited for; matrix products, arithmetic and copies ran while one was open for 1% of the time, Pallas kernels for 6%

profile of v4, /device:TPU:2, one launch (start us, length us, event | category | flops | bytes accessed | tf_op | source)
XLA Modules:
  0.0 76.3 jit_solution(14564433599318786828)
XLA Ops:
  0.6 2.2 %shard_map.175 = (f32[120,128]{1,0:T(8,128)S(1)}, f32[64,128]{1,0:T(8,128)S(1)}, f32[576,128]{1,0:T(8,128)}, f32[3,4,16,128]{3,2,1,0:T(8,128)S(1)}, f32[3,4,16,128]{3,2,1,0:T(8,128)S(1)}, /*index=5*/s32[1,128]{1,0:T(1,128)S(1)}) custom-call(f32[3,4,16,128]{3,2,1,0:T(8,128)} %state_in.1, f32[3,4,16,128]{3,2,1,0:T(8,128)} %direction_in.1, s32[4,16]{1,0:T(4,128)} %clamp_in.1, ...), custom_call_target="tpu_custom_call" | custom-call | tf_op jit(solution)/shard_map/pallas_call | solution.py:232
  2.8 5.6 %collective-permute-start = (f32[120,128]{1,0:T(8,128)S(1)}, f32[120,128]{1,0:T(8,128)S(1)}, u32[]{:S(2)}, u32[]{:S(2)}) collective-permute-start(f32[120,128]{1,0:T(8,128)S(1)} %get-tuple-element.31), channel_id=1, source_target_pairs={{1,0},{2,1},{3,2},{4,3},{5,4},{6,5},{7,6},{8,7},{9,8},{10,9},{11,1... | collective-permute-start | bytes 184328 | tf_op jit(solution)/shard_map/ppermute | solution.py:532
  8.4 22.7 %all-to-all-start = ((f32[576,1,128]{2,1,0:T(1,128)}), f32[576,1,128]{2,1,0:T(1,128)S(1)}, u32[]{:S(2)}, u32[]{:S(2)}) async-start(f32[576,1,128]{2,1,0:T(1,128)} %bitcast.4), calls=%async_computation | async-start | bytes 589824 | tf_op jit(solution)/shard_map/all_to_all | solution.py:554
  31.1 0.0 collective-permute-done.halo
  31.1 4.3 %shard_map.176 = (f32[336,768]{1,0:T(8,128)S(1)}, f32[8,128]{1,0:T(8,128)S(1)}, f32[112,256]{1,0:T(8,128)S(1)}, f32[3,4,16,128]{3,2,1,0:T(8,128)S(1)}, bf16[384,...) custom-call(f32[3,4,16,128]{3,2,1,0:T(8,128)S(1)} %get-tuple-element, ...), custom_call_target="tpu_custom_call" | custom-call | flops 20000000000 | bytes 4000000 | tf_op jit(solution)/shard_map/pallas_call | solution.py:334
  35.4 1.9 %collective-permute-start.1 = (f32[8,128]{1,0:T(8,128)S(1)}, f32[8,128]{1,0:T(8,128)S(1)}, u32[]{:S(2)}, u32[]{:S(2)}) collective-permute-start(f32[8,128]{1,0:T(8,128)S(1)} %get-tuple-element.33), channel_id=1, source_target_pairs={{0,1},{1,2},{2,3},{3,4},{4,5},{5,6},{6,7},{7,8},{8,9},{9,10},{10,1... | collective-permute-start | bytes 12296 | tf_op jit(solution)/shard_map/ppermute | solution.py:564
  37.4 4.2 %collective-permute-done.1 = f32[8,128]{1,0:T(8,128)S(1)} collective-permute-done((f32[8,128]{1,0:T(8,128)S(1)}, f32[8,128]{1,0:T(8,128)S(1)}, u32[]{:S(2)}, u32[]{:S(2)}) %collective-permute-start.1) | collective-permute-done | bytes 4128 | tf_op jit(solution)/shard_map/ppermute | solution.py:564
  41.6 2.8 %all-to-all-done = f32[576,1,128]{2,1,0:T(1,128)S(1)} async-done(((f32[576,1,128]{2,1,0:T(1,128)}), f32[576,1,128]{2,1,0:T(1,128)S(1)}, u32[]{:S(2)}, u32[]{:S(2)}) %all-to-all-start) | async-done | bytes 294944 | tf_op jit(solution)/shard_map/all_to_all | solution.py:554
  44.4 17.0 %all_to_all.16 = f32[32,8,128]{2,1,0:T(8,128)S(1)} all-to-all(f32[32,8,128]{2,1,0:T(8,128)S(1)} %bitcast.15), channel_id=1, replica_groups={{0,16,32,48,64,80,96,112,128,144,160,176,192,208,224,240,256,272,288,30..., dimensions={0} | all-to-all | bytes 262144 | tf_op jit(solution)/shard_map/all_to_all | solution.py:572
  61.4 0.7 shard_map.177.correction
  62.2 1.9 %collective-permute-start.2 = (f32[8,128]{1,0:T(8,128)S(1)}, f32[8,128]{1,0:T(8,128)S(1)}, u32[]{:S(2)}, u32[]{:S(2)}) collective-permute-start(f32[8,128]{1,0:T(8,128)S(1)} %shard_map.177.correction), channel_id=1, source_target_pairs={{1,0},{2,1},{3,2},{4,3},{5,4},{6,5},{7,6},{8,7},{9,8},{10,9},{11,1... | collective-permute-start | bytes 12296 | tf_op jit(solution)/shard_map/ppermute | solution.py:532
  64.1 1.3 %collective-permute-done.2.right = f32[8,128]{1,0:T(8,128)S(1)} collective-permute-done((f32[8,128]{1,0:T(8,128)S(1)}, f32[8,128]{1,0:T(8,128)S(1)}, u32[]{:S(2)}, u32[]{:S(2)}) %collective-permute-start.2) | collective-permute-done | bytes 4128 | tf_op jit(solution)/shard_map/ppermute | solution.py:532
  65.4 2.8 %shard_map.178 = (f32[3,4,16,128]{3,2,1,0:T(8,128)S(1)}, f32[3,4,16,128]{3,2,1,0:T(8,128)S(1)}, f32[72,128]{1,0:T(8,128)S(1)}, f32[3,4,32]{2,1,0:T(4,128)S(1)}) custom-call(f32[8,128]{1,0:T(8,128)S(1)} %shard_map.177.correction, f32[8,128]{1,0:T(8,128)S(1)} %collective-permute-done.2.right, f32[336,768]{1,0:T(8,128)S(1)} %get-tuple-element.37.state_grad, ...), custom_call_target="tpu_custom_call" | custom-call | tf_op jit(solution)/shard_map/pallas_call | solution.py:157
  68.2 1.9 %collective-permute-start.3 = (f32[72,128]{1,0:T(8,128)S(1)}, f32[72,128]{1,0:T(8,128)S(1)}, u32[]{:S(2)}, u32[]{:S(2)}) collective-permute-start(f32[72,128]{1,0:T(8,128)S(1)} %get-tuple-element.49), channel_id=1, source_target_pairs={{0,1},{1,2},{2,3},{3,4},{4,5},{5,6},{6,7},{7,8},{8,9},{9,10},{10,1... | collective-permute-start | bytes 110600 | tf_op jit(solution)/shard_map/ppermute | solution.py:532
  70.2 0.6 copy.22
  70.8 4.8 %collective-permute-done.3.arrived = f32[72,128]{1,0:T(8,128)S(1)} collective-permute-done((f32[72,128]{1,0:T(8,128)S(1)}, f32[72,128]{1,0:T(8,128)S(1)}, u32[]{:S(2)}, u32[]{:S(2)}) %collective-permute-start.3) | collective-permute-done | bytes 36896 | tf_op jit(solution)/shard_map/ppermute | solution.py:532
  75.6 0.7 shard_map.179
  (3 shorter events, 0.0 us)
Async XLA Ops:
  2.8 28.3 %collective-permute-start = (f32[120,128]{1,0:T(8,128)S(1)}, f32[120,128]{1,0:T(8,128)S(1)}, u32[]{:S(2)}, u32[]{:S(2)}) collective-permute-start(f32[120,128]{1,0:T(8,128)S(1)} %get-tuple-element.31), channel_id=1, source_target_pairs={{1,0},{2,1},{3,2},{4,3},{5,4},{6,5},{7,6},{8,7},{9,8},{10,9},{11,1... | collective-permute-start | bytes 184328 | tf_op jit(solution)/shard_map/ppermute | solution.py:532
  8.4 36.0 %all-to-all-start = ((f32[576,1,128]{2,1,0:T(1,128)}), f32[576,1,128]{2,1,0:T(1,128)S(1)}, u32[]{:S(2)}, u32[]{:S(2)}) async-start(f32[576,1,128]{2,1,0:T(1,128)} %bitcast.4), calls=%async_computation | async-start | bytes 589824 | tf_op jit(solution)/shard_map/all_to_all | solution.py:554
  35.4 6.1 %collective-permute-start.1 = (f32[8,128]{1,0:T(8,128)S(1)}, f32[8,128]{1,0:T(8,128)S(1)}, u32[]{:S(2)}, u32[]{:S(2)}) collective-permute-start(f32[8,128]{1,0:T(8,128)S(1)} %get-tuple-element.33), channel_id=1, source_target_pairs={{0,1},{1,2},{2,3},{3,4},{4,5},{5,6},{6,7},{7,8},{8,9},{9,10},{10,1... | collective-permute-start | bytes 12296 | tf_op jit(solution)/shard_map/ppermute | solution.py:564
  62.2 3.2 %collective-permute-start.2 = (f32[8,128]{1,0:T(8,128)S(1)}, f32[8,128]{1,0:T(8,128)S(1)}, u32[]{:S(2)}, u32[]{:S(2)}) collective-permute-start(f32[8,128]{1,0:T(8,128)S(1)} %shard_map.177.correction), channel_id=1, source_target_pairs={{1,0},{2,1},{3,2},{4,3},{5,4},{6,5},{7,6},{8,7},{9,8},{10,9},{11,1... | collective-permute-start | bytes 12296 | tf_op jit(solution)/shard_map/ppermute | solution.py:532
  68.2 7.4 %collective-permute-start.3 = (f32[72,128]{1,0:T(8,128)S(1)}, f32[72,128]{1,0:T(8,128)S(1)}, u32[]{:S(2)}, u32[]{:S(2)}) collective-permute-start(f32[72,128]{1,0:T(8,128)S(1)} %get-tuple-element.49), channel_id=1, source_target_pairs={{0,1},{1,2},{2,3},{3,4},{4,5},{5,6},{6,7},{7,8},{8,9},{9,10},{10,1... | collective-permute-start | bytes 110600 | tf_op jit(solution)/shard_map/ppermute | solution.py:532

commit v5 on v3

--- a/solution.py
+++ b/solution.py
@@ -71,8 +71,7 @@
 
 
 def stack_right(table):
-    high, low = halves(table)
-    return np.concatenate([high, high, low], axis=0)
+    return np.concatenate(halves(table), axis=0)
 
 
 @functools.lru_cache(maxsize=None)
@@ -112,14 +111,10 @@
         back_z=stack_left(kinds[2].T),
         back_along=stack_right(along.T),
         rest=stack_left(rest),
-        tables=np.concatenate(
-            [
-                np.tile(hat_z.T, (1, 4)),
-                np.pad(fold, ((0, 0), (0, 104))),
-                np.pad(rest[:8].T, ((0, 0), (0, 120))),
-            ],
-            axis=0,
-        ).astype(np.float32),
+        hat_down=stack_right(np.tile(hat_z.T, (1, 4))),
+        hat_up=stack_right(np.tile(hat_z, (4, 1))),
+        fold=np.pad(np.concatenate([fold, fold], axis=1), ((0, 8), (0, 0))).astype(BF16),
+        spread=stack_left(rest[:8].T),
         quad_y=np.asarray(quad_y, np.float32),
         quad_z=np.asarray(quad_z, np.float32),
     )
@@ -150,6 +145,11 @@
 
 def near(x):
     return pltpu.with_memory_space_constraint(x, pltpu.VMEM)
+
+
+def thrice(ref):
+    half = ref.shape[0] // 2
+    return jnp.concatenate([ref[0:half, :], ref[0:half, :], ref[half:, :]], axis=0)
 
 
 def call(body, outs, *operands, scratch=(), cost=None):
@@ -235,7 +235,7 @@
 
 def gradients(fields, along, grads, refs):
     lines = jnp.concatenate([f for field in fields for f in field], axis=0)
-    flat = dot(beside(lines), along[...])
+    flat = dot(beside(lines), thrice(along))
     for i, ref in enumerate(refs):
         parts = [flat[(3 * i + c) * NODES : (3 * i + c + 1) * NODES] for c in range(3)]
         plain = jnp.concatenate([p[:, :WIDE] for p in parts], axis=1)
@@ -244,7 +244,7 @@
         ref[2 * ROWS :, :] = dot(grads[2 * ROWS :, :], under(sloped))
 
 
-def physics(state_grad, grad, weighting, flux):
+def physics(state_grad, grad, weighting, stress, flux, fresh):
     pairs = ((0, 0), (1, 1), (2, 2), (0, 1), (0, 2), (1, 2))
     for start in range(0, LIVE, 8):
         here = slice(start, start + 8)
@@ -258,17 +258,22 @@
             for c in range(3)
         ]
         change = [[piece(grad, c, a) for a in range(3)] for c in range(3)]
-        square = {
-            (a, b): deform[0][a] * deform[0][b]
-            + deform[1][a] * deform[1][b]
-            + deform[2][a] * deform[2][b]
-            for a, b in pairs
-        }
-        shift = 0.6 * (square[0, 0] + square[1, 1] + square[2, 2] - 3.0)
-        held = {
-            (a, b): w * (0.8 * (square[a, b] - 1.0) + shift) if a == b else (0.8 * w) * square[a, b]
-            for a, b in pairs
-        }
+        if fresh:
+            square = {
+                (a, b): deform[0][a] * deform[0][b]
+                + deform[1][a] * deform[1][b]
+                + deform[2][a] * deform[2][b]
+                for a, b in pairs
+            }
+            shift = 0.6 * (square[0, 0] + square[1, 1] + square[2, 2] - 3.0)
+            held = {
+                (a, b): w * (0.8 * (square[a, b] - 1.0) + shift) if a == b else (0.8 * w) * square[a, b]
+                for a, b in pairs
+            }
+            for i, pair in enumerate(pairs):
+                stress[i, here, :] = held[pair]
+        else:
+            held = {pair: stress[i, here, :] for i, pair in enumerate(pairs)}
         cross = [
             [
                 deform[0][a] * change[0][b] + deform[1][a] * change[1][b] + deform[2][a] * change[2][b]
@@ -307,7 +312,7 @@
         ],
         axis=0,
     )
-    return dot(beside(lines), back_along[...])
+    return dot(beside(lines), thrice(back_along))
 
 
 def coarse_rows(extended, rest):
@@ -321,7 +326,7 @@
 
 def first_body(
     state, direction, rhs, keep_rows, halo, weighting, along, grads, back_xy, back_z, back_along,
-    rest, tables, owner, state_grad, sums, grad, flux,
+    rest, hat_down, hat_up, fold, spread, owner, state_grad, stress, sums, grad, flux,
 ):
     keep = keep_rows[...]
     fields = [
@@ -332,7 +337,7 @@
         ],
     ]
     gradients(fields, along, grads, (state_grad, grad))
-    physics(state_grad, grad, weighting, flux)
+    physics(state_grad, grad, weighting, stress, flux, True)
     image = images(flux, back_xy, back_z, back_along)
     keep_right = halo[96:112, :]
     extended = []
@@ -340,11 +345,11 @@
         part = image[c * NODES : (c + 1) * NODES]
         own = own_rows(rhs, c) - keep * part[:64] - (1.0 - keep) * own_rows(direction, c)
         extended.append(jnp.concatenate([own, -keep_right * part[64:]], axis=0))
-    levels = exact(coarse_rows(extended, rest), tables[0:128, :])
+    levels = dot(beside(coarse_rows(extended, rest)), thrice(hat_down))
     row = lax.broadcasted_iota(jnp.int32, (24, 128), 0)
     lane = lax.broadcasted_iota(jnp.int32, (24, 128), 1)
     levels = jnp.where(lane // EZ == row % EY, levels, 0.0)
-    levels = exact(tables[128:136, 0:24], levels)
+    levels = dot(fold[...], jnp.concatenate(split(levels), axis=0))[0:8]
     sums[0:4, :] = placed(levels, owner[...])[0:4]
     sums[4:8, :] = placed(levels, halo[112:113, :].astype(jnp.int32))[4:8]
 
@@ -400,8 +405,9 @@
 
 
 def second_body(
-    correction, right, state_grad, direction, rhs, keep_rows, halo, weighting, along, grads,
-    back_xy, back_z, back_along, rest, tables, new, partial, message, own_coarse, grad, flux,
+    correction, right, state_grad, stress, direction, rhs, keep_rows, halo, weighting, along, grads,
+    back_xy, back_z, back_along, rest, hat_down, hat_up, fold, spread, new, partial, message,
+    own_coarse, grad, flux,
 ):
     keep = keep_rows[...]
     keep_right = halo[96:112, :]
@@ -415,12 +421,9 @@
     )
     row = lax.broadcasted_iota(jnp.int32, (24, 128), 0)
     lane = lax.broadcasted_iota(jnp.int32, (24, 128), 1)
-    levels = lax.dot_general(
-        jnp.where(lane // EZ == row % EY, rows, 0.0), tables[0:128, :], (((1,), (1,)), ((), ())),
-        preferred_element_type=F32, precision=HIGHEST,
-    )
+    levels = dot(beside(jnp.where(lane // EZ == row % EY, rows, 0.0)), thrice(hat_up))
     levels = jnp.concatenate([levels[c * 8 : (c + 1) * 8] for c in range(3)], axis=1)
-    update = exact(tables[136:216, 0:8], levels)
+    update = dot(spread[...], under(levels))
     field = []
     fresh = []
     for c in range(3):
@@ -434,7 +437,7 @@
             )
         )
     gradients([field], along, grads, (grad,))
-    physics(state_grad, grad, weighting, flux)
+    physics(state_grad, grad, weighting, stress, flux, False)
     image = images(flux, back_xy, back_z, back_along)
     extended = []
     for c in range(3):
@@ -444,7 +447,7 @@
         partial[c] = own.reshape(4, 16, 128)
         message[c * 16 : (c + 1) * 16, :] = last
         extended.append(jnp.concatenate([own, last], axis=0))
-    levels = exact(coarse_rows(extended, rest), tables[0:128, :])
+    levels = dot(beside(coarse_rows(extended, rest)), thrice(hat_down))
     message[48:72, :] = levels
     for c in range(3):
         own_coarse[c] = levels[c * 8 : c * 8 + 4, :EZ]
@@ -492,7 +495,7 @@
 
 def shards(state, direction, rhs, clamp, stiffness, coarse_owner, coarse_inverse):
     k = constants()
-    names = ("along", "grads", "back_xy", "back_z", "back_along", "rest", "tables")
+    names = ("along", "grads", "back_xy", "back_z", "back_along", "rest", "hat_down", "hat_up", "fold", "spread")
     kept = [state, direction, rhs] + [jnp.asarray(k[name]) for name in names] + [coarse_owner]
     inverse = coarse_inverse.reshape(384, 192)
     used = [
@@ -506,9 +509,9 @@
     ).reshape(576, 128)
     big = (3 * ROWS, 3 * WIDE)
     scratch = (pltpu.VMEM(big, F32), pltpu.VMEM(big, F32))
-    state_grad, sums = call(
+    state_grad, stress, sums = call(
         first_body,
-        [big, (8, 128)],
+        [big, (6, LIVE, WIDE), (8, 128)],
         state, direction, rhs, keep_rows, halo, weighting, *shared, owner,
         scratch=scratch, cost=pl.CostEstimate(flops=20000000000, bytes_accessed=4 * 10**6, transcendentals=0),
     )
@@ -529,7 +532,7 @@
     new, partial, last, own_coarse = call(
         second_body,
         [field, field, (72, 128), (3, EY, EZ)],
-        correction, right, state_grad, direction, rhs, keep_rows, halo, weighting, *shared,
+        correction, right, state_grad, stress, direction, rhs, keep_rows, halo, weighting, *shared,
         scratch=scratch,
     )
     residual, coarse = finish(partial, shifted(last, 1), own_coarse)

time: 75.9 us -> 75.3 us (level)
  no operation moved by 1% of the time
where the time goes in v5:
time: 75.3 us; the launch traced here: 75 us
  starting transfers between devices  34.1 us (45%)
  blocking collectives  15.5 us (21%)
  waiting for transfers between devices  14.7 us (20%)
  Pallas kernels  9.35 us (12%)
    all_to_all x1, starting transfers between devices, shards(): lax.all_to_all(rows.reshape(576, 1, 128), 'grp', split_axis=0, concat_axi...  22.7 us
    all_to_all x1, blocking collectives, shards(): lax.all_to_all(total, 'grp', split_axis=0, concat_axis=0, tiled=True, axi...  15.5 us
    ppermute x3, starting transfers between devices, shifted(): return lax.ppermute(block, axes, route)  9.44 us
    ppermute x3, waiting for transfers between devices, shifted(): return lax.ppermute(block, axes, route)  6.12 us
    pallas_call x3, Pallas kernels, call(): pl.pallas_call(body, out_shape=[pltpu.VMEM(s, F32) for s in outs], in_spe...  5.82 us
    all_to_all x1, waiting for transfers between devices, shards(): lax.all_to_all(rows.reshape(576, 1, 128), 'grp', split_axis=0, concat_axi...  4.34 us
    ppermute x1, waiting for transfers between devices, shards(): arrived = lax.ppermute(sums, ('grp', 'mem'), ring())[4:8]  4.2 us
    pallas_call x1, Pallas kernels, prepare(): pl.pallas_call(functools.partial(prepare_body, len(operands)), out_shape=...  2.88 us
  transfers between devices with their start and end apart: 5, of which 4 were waited for; matrix products, arithmetic and copies ran while one was open for 1% of the time, Pallas kernels for 4%

profile of v5, /device:TPU:2, one launch (start us, length us, event | category | flops | bytes accessed | tf_op | source)
XLA Modules:
  0.0 75.0 jit_solution(6627329545548867630)
XLA Ops:
  0.6 2.9 %shard_map.202 = (f32[120,128]{1,0:T(8,128)S(1)}, f32[64,128]{1,0:T(8,128)S(1)}, f32[576,128]{1,0:T(8,128)}, f32[112,256]{1,0:T(8,128)S(1)}, f32[3,4,16,128]{3,2...) custom-call(f32[3,4,16,128]{3,2,1,0:T(8,128)} %refs_0_.1, ...), custom_call_target="tpu_custom_call" | custom-call | tf_op jit(solution)/shard_map/pallas_call | solution.py:224
  3.5 5.6 %collective-permute-start = (f32[120,128]{1,0:T(8,128)S(1)}, f32[120,128]{1,0:T(8,128)S(1)}, u32[]{:S(2)}, u32[]{:S(2)}) collective-permute-start(f32[120,128]{1,0:T(8,128)S(1)} %get-tuple-element.36), channel_id=1, source_target_pairs={{1,0},{2,1},{3,2},{4,3},{5,4},{6,5},{7,6},{8,7},{9,8},{10,9},{11,1... | collective-permute-start | bytes 184328 | tf_op jit(solution)/shard_map/ppermute | solution.py:481
  9.1 22.7 %all-to-all-start = ((f32[576,1,128]{2,1,0:T(1,128)}), f32[576,1,128]{2,1,0:T(1,128)S(1)}, u32[]{:S(2)}, u32[]{:S(2)}) async-start(f32[576,1,128]{2,1,0:T(1,128)} %bitcast.4), calls=%async_computation | async-start | bytes 589824 | tf_op jit(solution)/shard_map/all_to_all | solution.py:507
  31.8 0.0 collective-permute-done.halo
  31.9 2.8 %shard_map.203 = (f32[336,768]{1,0:T(8,128)S(1)}, f32[6,104,256]{2,1,0:T(8,128)S(1)}, f32[8,128]{1,0:T(8,128)S(1)}) custom-call(f32[3,4,16,128]{3,2,1,0:T(8,128)S(1)} %get-tuple-element.32.state, f32[3,4,16,128]{3,2,1,0:T(8,128)S(1)} %get-tuple-element.33.direction, f32[3,4,16,128]{3,2,1,0:T(8,128)S(1)} %get-tuple-element.34.rhs, ...), custom_call_target="tpu_custom_call" | custom-call | flops 20000000000 | bytes 4000000 | tf_op jit(solution)/shard_map/pallas_call | solution.py:157
  34.6 1.9 %collective-permute-start.1 = (f32[8,128]{1,0:T(8,128)S(1)}, f32[8,128]{1,0:T(8,128)S(1)}, u32[]{:S(2)}, u32[]{:S(2)}) collective-permute-start(f32[8,128]{1,0:T(8,128)S(1)} %get-tuple-element.49), channel_id=1, source_target_pairs={{0,1},{1,2},{2,3},{3,4},{4,5},{5,6},{6,7},{7,8},{8,9},{9,10},{10,1... | collective-permute-start | bytes 12296 | tf_op jit(solution)/shard_map/ppermute | solution.py:518
  36.6 4.2 %collective-permute-done.1 = f32[8,128]{1,0:T(8,128)S(1)} collective-permute-done((f32[8,128]{1,0:T(8,128)S(1)}, f32[8,128]{1,0:T(8,128)S(1)}, u32[]{:S(2)}, u32[]{:S(2)}) %collective-permute-start.1) | collective-permute-done | bytes 4128 | tf_op jit(solution)/shard_map/ppermute | solution.py:518
  40.8 4.3 %all-to-all-done = f32[576,1,128]{2,1,0:T(1,128)S(1)} async-done(((f32[576,1,128]{2,1,0:T(1,128)}), f32[576,1,128]{2,1,0:T(1,128)S(1)}, u32[]{:S(2)}, u32[]{:S(2)}) %all-to-all-start) | async-done | bytes 294944 | tf_op jit(solution)/shard_map/all_to_all | solution.py:507
  45.2 15.5 %all_to_all.16 = f32[32,8,128]{2,1,0:T(8,128)S(1)} all-to-all(f32[32,8,128]{2,1,0:T(8,128)S(1)} %bitcast.15), channel_id=1, replica_groups={{0,16,32,48,64,80,96,112,128,144,160,176,192,208,224,240,256,272,288,30..., dimensions={0} | all-to-all | bytes 262144 | tf_op jit(solution)/shard_map/all_to_all | solution.py:526
  60.6 0.7 shard_map.204.correction
  61.4 1.9 %collective-permute-start.2 = (f32[8,128]{1,0:T(8,128)S(1)}, f32[8,128]{1,0:T(8,128)S(1)}, u32[]{:S(2)}, u32[]{:S(2)}) collective-permute-start(f32[8,128]{1,0:T(8,128)S(1)} %shard_map.204.correction), channel_id=1, source_target_pairs={{1,0},{2,1},{3,2},{4,3},{5,4},{6,5},{7,6},{8,7},{9,8},{10,9},{11,1... | collective-permute-start | bytes 12296 | tf_op jit(solution)/shard_map/ppermute | solution.py:481
  63.3 1.3 %collective-permute-done.2.right = f32[8,128]{1,0:T(8,128)S(1)} collective-permute-done((f32[8,128]{1,0:T(8,128)S(1)}, f32[8,128]{1,0:T(8,128)S(1)}, u32[]{:S(2)}, u32[]{:S(2)}) %collective-permute-start.2) | collective-permute-done | bytes 4128 | tf_op jit(solution)/shard_map/ppermute | solution.py:481
  64.6 2.3 %shard_map.205 = (f32[3,4,16,128]{3,2,1,0:T(8,128)S(1)}, f32[3,4,16,128]{3,2,1,0:T(8,128)S(1)}, f32[72,128]{1,0:T(8,128)S(1)}, f32[3,4,32]{2,1,0:T(4,128)S(1)}) custom-call(f32[8,128]{1,0:T(8,128)S(1)} %shard_map.204.correction, f32[8,128]{1,0:T(8,128)S(1)} %collective-permute-done.2.right, f32[336,768]{1,0:T(8,128)S(1)} %get-tuple-element.53.state_grad, ...), custom_call_target="tpu_custom_call" | custom-call | tf_op jit(solution)/shard_map/pallas_call | solution.py:157
  66.9 1.9 %collective-permute-start.3 = (f32[72,128]{1,0:T(8,128)S(1)}, f32[72,128]{1,0:T(8,128)S(1)}, u32[]{:S(2)}, u32[]{:S(2)}) collective-permute-start(f32[72,128]{1,0:T(8,128)S(1)} %get-tuple-element.57), channel_id=1, source_target_pairs={{0,1},{1,2},{2,3},{3,4},{4,5},{5,6},{6,7},{7,8},{8,9},{9,10},{10,1... | collective-permute-start | bytes 110600 | tf_op jit(solution)/shard_map/ppermute | solution.py:481
  68.9 0.6 copy.25
  69.5 4.8 %collective-permute-done.3.arrived = f32[72,128]{1,0:T(8,128)S(1)} collective-permute-done((f32[72,128]{1,0:T(8,128)S(1)}, f32[72,128]{1,0:T(8,128)S(1)}, u32[]{:S(2)}, u32[]{:S(2)}) %collective-permute-start.3) | collective-permute-done | bytes 36896 | tf_op jit(solution)/shard_map/ppermute | solution.py:481
  74.3 0.7 shard_map.206
  (3 shorter events, 0.0 us)
Async XLA Ops:
  3.5 28.3 %collective-permute-start = (f32[120,128]{1,0:T(8,128)S(1)}, f32[120,128]{1,0:T(8,128)S(1)}, u32[]{:S(2)}, u32[]{:S(2)}) collective-permute-start(f32[120,128]{1,0:T(8,128)S(1)} %get-tuple-element.36), channel_id=1, source_target_pairs={{1,0},{2,1},{3,2},{4,3},{5,4},{6,5},{7,6},{8,7},{9,8},{10,9},{11,1... | collective-permute-start | bytes 184328 | tf_op jit(solution)/shard_map/ppermute | solution.py:481
  9.1 36.0 %all-to-all-start = ((f32[576,1,128]{2,1,0:T(1,128)}), f32[576,1,128]{2,1,0:T(1,128)S(1)}, u32[]{:S(2)}, u32[]{:S(2)}) async-start(f32[576,1,128]{2,1,0:T(1,128)} %bitcast.4), calls=%async_computation | async-start | bytes 589824 | tf_op jit(solution)/shard_map/all_to_all | solution.py:507
  34.6 6.2 %collective-permute-start.1 = (f32[8,128]{1,0:T(8,128)S(1)}, f32[8,128]{1,0:T(8,128)S(1)}, u32[]{:S(2)}, u32[]{:S(2)}) collective-permute-start(f32[8,128]{1,0:T(8,128)S(1)} %get-tuple-element.49), channel_id=1, source_target_pairs={{0,1},{1,2},{2,3},{3,4},{4,5},{5,6},{6,7},{7,8},{8,9},{9,10},{10,1... | collective-permute-start | bytes 12296 | tf_op jit(solution)/shard_map/ppermute | solution.py:518
  61.4 3.2 %collective-permute-start.2 = (f32[8,128]{1,0:T(8,128)S(1)}, f32[8,128]{1,0:T(8,128)S(1)}, u32[]{:S(2)}, u32[]{:S(2)}) collective-permute-start(f32[8,128]{1,0:T(8,128)S(1)} %shard_map.204.correction), channel_id=1, source_target_pairs={{1,0},{2,1},{3,2},{4,3},{5,4},{6,5},{7,6},{8,7},{9,8},{10,9},{11,1... | collective-permute-start | bytes 12296 | tf_op jit(solution)/shard_map/ppermute | solution.py:481
  66.9 7.4 %collective-permute-start.3 = (f32[72,128]{1,0:T(8,128)S(1)}, f32[72,128]{1,0:T(8,128)S(1)}, u32[]{:S(2)}, u32[]{:S(2)}) collective-permute-start(f32[72,128]{1,0:T(8,128)S(1)} %get-tuple-element.57), channel_id=1, source_target_pairs={{0,1},{1,2},{2,3},{3,4},{4,5},{5,6},{6,7},{7,8},{8,9},{9,10},{10,1... | collective-permute-start | bytes 110600 | tf_op jit(solution)/shard_map/ppermute | solution.py:481

commit v6 on v5

--- a/solution.py
+++ b/solution.py
@@ -168,16 +168,35 @@
 def prepare_body(count, *refs):
     sources, refs = refs[:count], refs[count:]
     message, keep_rows, rows, weighting = refs[:4]
-    targets, (halves_of, done) = refs[4:-2], refs[-2:]
+    targets, (halves_of, sorted_rows, done) = refs[4:-3], refs[-3:]
     copies = [
         pltpu.make_async_copy(source, target, done.at[i])
         for i, (source, target) in enumerate(zip(sources, targets))
     ]
-    urgent = (0, 1, count - 6, count - 5, count - 4)
+    writes = [
+        pltpu.make_async_copy(part(sorted_rows, b), part(rows, b), done.at[count + b])
+        for b in range(2)
+    ]
+    urgent = (count - 4, count - 6, count - 5, 1, 0)
     for i in urgent + tuple(i for i in range(count) if i not in urgent):
         copies[i].start()
     state, direction = targets[0], targets[1]
     clamp, owner, inverse, stiffness, quad_y, quad_z = targets[-6:]
+    copies[count - 4].wait()
+    halves_of[0] = inverse[:, 0:128]
+    halves_of[1] = jnp.concatenate([inverse[:, 128:192]] * 2, axis=1)
+    low = lax.broadcasted_iota(jnp.int32, (32, 128), 1) < 64
+    for b in range(2):
+        for c in range(3):
+            first, second = [pl.ds(b * 192 + c * 64 + q, 32, stride=2) for q in range(2)]
+            values = (
+                halves_of[0, first, :],
+                jnp.where(low, halves_of[1, first, :], halves_of[1, second, :]),
+                halves_of[0, second, :],
+            )
+            for i in range(3):
+                sorted_rows[pl.ds(b * 288 + c * 3 + i, 32, stride=9), :] = values[i]
+        writes[b].start()
     for i in (0, 1, count - 6, count - 5):
         copies[i].wait()
     eye = lax.broadcasted_iota(jnp.int32, (16, 16), 0) == lax.broadcasted_iota(
@@ -195,24 +214,17 @@
             for c in range(3):
                 message[c * 16 : (c + 1) * 16, :] = keep * direction[c, 0]
                 message[48 + c * 16 : 48 + (c + 1) * 16, :] = state[c, 0]
-    for i in range(count - 4, count):
+    for i in range(count - 3, count):
         copies[i].wait()
-    halves_of[0] = inverse[:, 0:128]
-    halves_of[1] = jnp.concatenate([inverse[:, 128:192]] * 2, axis=1)
-    low = lax.broadcasted_iota(jnp.int32, (32, 128), 1) < 64
-    for b in range(2):
-        for c in range(3):
-            first, second = [pl.ds(b * 192 + c * 64 + q, 32, stride=2) for q in range(2)]
-            values = (
-                halves_of[0, first, :],
-                jnp.where(low, halves_of[1, first, :], halves_of[1, second, :]),
-                halves_of[0, second, :],
-            )
-            for i in range(3):
-                rows[pl.ds(b * 32 * 9 + c * 3 + i, 32, stride=9), :] = values[i]
     weighting[...] = exact(exact(quad_y[...], stiffness[...]), quad_z[...])
     for i in range(2, count - 6):
         copies[i].wait()
+    for write in writes:
+        write.wait()
+
+
+def part(ref, b):
+    return ref.at[b * 288 : (b + 1) * 288]
 
 
 def prepare(kept, used):
@@ -221,14 +233,15 @@
     vmem = pl.BlockSpec(memory_space=pltpu.VMEM)
     made = [(120, 128), (64, 128), (576, 128), (ROWS, WIDE)]
     outs = [pltpu.VMEM(s, F32) for s in made] + [pltpu.VMEM(x.shape, x.dtype) for x in kept]
+    outs[2] = jax.ShapeDtypeStruct(made[2], F32)
     return pl.pallas_call(
         functools.partial(prepare_body, len(operands)),
         out_shape=outs,
         in_specs=[far] * len(operands),
-        out_specs=[vmem] * len(outs),
+        out_specs=[vmem, vmem, far] + [vmem] * (len(outs) - 3),
         scratch_shapes=[pltpu.VMEM(x.shape, x.dtype) for x in used]
-        + [pltpu.VMEM((2, 384, 128), F32)]
-        + [pltpu.SemaphoreType.DMA((len(operands),))],
+        + [pltpu.VMEM((2, 384, 128), F32), pltpu.VMEM((576, 128), F32)]
+        + [pltpu.SemaphoreType.DMA((len(operands) + 2,))],
         compiler_params=pltpu.CompilerParams(vmem_limit_bytes=24 * 2**20),
     )(*[pltpu.with_memory_space_constraint(x, pltpu.HBM) for x in operands])
 

time: 75.3 us -> 74.6 us (level)
  no operation moved by 1% of the time
where the time goes in v6:
time: 74.6 us; the launch traced here: 74.2 us
  starting transfers between devices  34.1 us (46%)
  blocking collectives  15.5 us (21%)
  waiting for transfers between devices  14.7 us (20%)
  Pallas kernels  8.6 us (12%)
    all_to_all x1, starting transfers between devices, shards(): lax.all_to_all(rows.reshape(576, 1, 128), 'grp', split_axis=0, concat_axi...  22.7 us
    all_to_all x1, blocking collectives, shards(): lax.all_to_all(total, 'grp', split_axis=0, concat_axis=0, tiled=True, axi...  15.5 us
    ppermute x3, starting transfers between devices, shifted(): return lax.ppermute(block, axes, route)  9.44 us
    ppermute x3, waiting for transfers between devices, shifted(): return lax.ppermute(block, axes, route)  6.12 us
    pallas_call x3, Pallas kernels, call(): pl.pallas_call(body, out_shape=[pltpu.VMEM(s, F32) for s in outs], in_spe...  5.82 us
    all_to_all x1, waiting for transfers between devices, shards(): lax.all_to_all(rows.reshape(576, 1, 128), 'grp', split_axis=0, concat_axi...  4.34 us
    ppermute x1, waiting for transfers between devices, shards(): arrived = lax.ppermute(sums, ('grp', 'mem'), ring())[4:8]  4.2 us
    pallas_call x1, Pallas kernels, prepare(): pl.pallas_call(functools.partial(prepare_body, len(operands)), out_shape=...  2.13 us
  transfers between devices with their start and end apart: 5, of which 4 were waited for; matrix products, arithmetic and copies ran while one was open for 1% of the time, Pallas kernels for 4%

profile of v6, /device:TPU:2, one launch (start us, length us, event | category | flops | bytes accessed | tf_op | source)
XLA Modules:
  0.0 74.2 jit_solution(11134455489387554237)
XLA Ops:
  0.6 2.1 %shard_map.202 = (f32[120,128]{1,0:T(8,128)S(1)}, f32[64,128]{1,0:T(8,128)S(1)}, f32[576,128]{1,0:T(8,128)}, f32[112,256]{1,0:T(8,128)S(1)}, f32[3,4,16,128]{3,2...) custom-call(f32[3,4,16,128]{3,2,1,0:T(8,128)} %refs_0_.1, ...), custom_call_target="tpu_custom_call" | custom-call | tf_op jit(solution)/shard_map/pallas_call | solution.py:237
  2.8 5.6 %collective-permute-start = (f32[120,128]{1,0:T(8,128)S(1)}, f32[120,128]{1,0:T(8,128)S(1)}, u32[]{:S(2)}, u32[]{:S(2)}) collective-permute-start(f32[120,128]{1,0:T(8,128)S(1)} %get-tuple-element.36), channel_id=1, source_target_pairs={{1,0},{2,1},{3,2},{4,3},{5,4},{6,5},{7,6},{8,7},{9,8},{10,9},{11,1... | collective-permute-start | bytes 184328 | tf_op jit(solution)/shard_map/ppermute | solution.py:494
  8.4 22.7 %all-to-all-start = ((f32[576,1,128]{2,1,0:T(1,128)}), f32[576,1,128]{2,1,0:T(1,128)S(1)}, u32[]{:S(2)}, u32[]{:S(2)}) async-start(f32[576,1,128]{2,1,0:T(1,128)} %bitcast.4), calls=%async_computation | async-start | bytes 589824 | tf_op jit(solution)/shard_map/all_to_all | solution.py:520
  31.1 0.0 collective-permute-done.halo
  31.1 2.8 %shard_map.203 = (f32[336,768]{1,0:T(8,128)S(1)}, f32[6,104,256]{2,1,0:T(8,128)S(1)}, f32[8,128]{1,0:T(8,128)S(1)}) custom-call(f32[3,4,16,128]{3,2,1,0:T(8,128)S(1)} %get-tuple-element.32.state, f32[3,4,16,128]{3,2,1,0:T(8,128)S(1)} %get-tuple-element.33.direction, f32[3,4,16,128]{3,2,1,0:T(8,128)S(1)} %get-tuple-element.34.rhs, ...), custom_call_target="tpu_custom_call" | custom-call | flops 20000000000 | bytes 4000000 | tf_op jit(solution)/shard_map/pallas_call | solution.py:157
  33.9 1.9 %collective-permute-start.1 = (f32[8,128]{1,0:T(8,128)S(1)}, f32[8,128]{1,0:T(8,128)S(1)}, u32[]{:S(2)}, u32[]{:S(2)}) collective-permute-start(f32[8,128]{1,0:T(8,128)S(1)} %get-tuple-element.49), channel_id=1, source_target_pairs={{0,1},{1,2},{2,3},{3,4},{4,5},{5,6},{6,7},{7,8},{8,9},{9,10},{10,1... | collective-permute-start | bytes 12296 | tf_op jit(solution)/shard_map/ppermute | solution.py:531
  35.8 4.2 %collective-permute-done.1 = f32[8,128]{1,0:T(8,128)S(1)} collective-permute-done((f32[8,128]{1,0:T(8,128)S(1)}, f32[8,128]{1,0:T(8,128)S(1)}, u32[]{:S(2)}, u32[]{:S(2)}) %collective-permute-start.1) | collective-permute-done | bytes 4128 | tf_op jit(solution)/shard_map/ppermute | solution.py:531
  40.1 4.3 %all-to-all-done = f32[576,1,128]{2,1,0:T(1,128)S(1)} async-done(((f32[576,1,128]{2,1,0:T(1,128)}), f32[576,1,128]{2,1,0:T(1,128)S(1)}, u32[]{:S(2)}, u32[]{:S(2)}) %all-to-all-start) | async-done | bytes 294944 | tf_op jit(solution)/shard_map/all_to_all | solution.py:520
  44.4 15.5 %all_to_all.16 = f32[32,8,128]{2,1,0:T(8,128)S(1)} all-to-all(f32[32,8,128]{2,1,0:T(8,128)S(1)} %bitcast.15), channel_id=1, replica_groups={{0,16,32,48,64,80,96,112,128,144,160,176,192,208,224,240,256,272,288,30..., dimensions={0} | all-to-all | bytes 262144 | tf_op jit(solution)/shard_map/all_to_all | solution.py:539
  59.9 0.7 shard_map.204.correction
  60.6 1.9 %collective-permute-start.2 = (f32[8,128]{1,0:T(8,128)S(1)}, f32[8,128]{1,0:T(8,128)S(1)}, u32[]{:S(2)}, u32[]{:S(2)}) collective-permute-start(f32[8,128]{1,0:T(8,128)S(1)} %shard_map.204.correction), channel_id=1, source_target_pairs={{1,0},{2,1},{3,2},{4,3},{5,4},{6,5},{7,6},{8,7},{9,8},{10,9},{11,1... | collective-permute-start | bytes 12296 | tf_op jit(solution)/shard_map/ppermute | solution.py:494
  62.6 1.3 %collective-permute-done.2.right = f32[8,128]{1,0:T(8,128)S(1)} collective-permute-done((f32[8,128]{1,0:T(8,128)S(1)}, f32[8,128]{1,0:T(8,128)S(1)}, u32[]{:S(2)}, u32[]{:S(2)}) %collective-permute-start.2) | collective-permute-done | bytes 4128 | tf_op jit(solution)/shard_map/ppermute | solution.py:494
  63.9 2.3 %shard_map.205 = (f32[3,4,16,128]{3,2,1,0:T(8,128)S(1)}, f32[3,4,16,128]{3,2,1,0:T(8,128)S(1)}, f32[72,128]{1,0:T(8,128)S(1)}, f32[3,4,32]{2,1,0:T(4,128)S(1)}) custom-call(f32[8,128]{1,0:T(8,128)S(1)} %shard_map.204.correction, f32[8,128]{1,0:T(8,128)S(1)} %collective-permute-done.2.right, f32[336,768]{1,0:T(8,128)S(1)} %get-tuple-element.53.state_grad, ...), custom_call_target="tpu_custom_call" | custom-call | tf_op jit(solution)/shard_map/pallas_call | solution.py:157
  66.2 1.9 %collective-permute-start.3 = (f32[72,128]{1,0:T(8,128)S(1)}, f32[72,128]{1,0:T(8,128)S(1)}, u32[]{:S(2)}, u32[]{:S(2)}) collective-permute-start(f32[72,128]{1,0:T(8,128)S(1)} %get-tuple-element.57), channel_id=1, source_target_pairs={{0,1},{1,2},{2,3},{3,4},{4,5},{5,6},{6,7},{7,8},{8,9},{9,10},{10,1... | collective-permute-start | bytes 110600 | tf_op jit(solution)/shard_map/ppermute | solution.py:494
  68.1 0.6 copy.25
  68.8 4.8 %collective-permute-done.3.arrived = f32[72,128]{1,0:T(8,128)S(1)} collective-permute-done((f32[72,128]{1,0:T(8,128)S(1)}, f32[72,128]{1,0:T(8,128)S(1)}, u32[]{:S(2)}, u32[]{:S(2)}) %collective-permute-start.3) | collective-permute-done | bytes 36896 | tf_op jit(solution)/shard_map/ppermute | solution.py:494
  73.6 0.7 shard_map.206
  (3 shorter events, 0.0 us)
Async XLA Ops:
  2.8 28.3 %collective-permute-start = (f32[120,128]{1,0:T(8,128)S(1)}, f32[120,128]{1,0:T(8,128)S(1)}, u32[]{:S(2)}, u32[]{:S(2)}) collective-permute-start(f32[120,128]{1,0:T(8,128)S(1)} %get-tuple-element.36), channel_id=1, source_target_pairs={{1,0},{2,1},{3,2},{4,3},{5,4},{6,5},{7,6},{8,7},{9,8},{10,9},{11,1... | collective-permute-start | bytes 184328 | tf_op jit(solution)/shard_map/ppermute | solution.py:494
  8.4 36.1 %all-to-all-start = ((f32[576,1,128]{2,1,0:T(1,128)}), f32[576,1,128]{2,1,0:T(1,128)S(1)}, u32[]{:S(2)}, u32[]{:S(2)}) async-start(f32[576,1,128]{2,1,0:T(1,128)} %bitcast.4), calls=%async_computation | async-start | bytes 589824 | tf_op jit(solution)/shard_map/all_to_all | solution.py:520
  33.9 6.2 %collective-permute-start.1 = (f32[8,128]{1,0:T(8,128)S(1)}, f32[8,128]{1,0:T(8,128)S(1)}, u32[]{:S(2)}, u32[]{:S(2)}) collective-permute-start(f32[8,128]{1,0:T(8,128)S(1)} %get-tuple-element.49), channel_id=1, source_target_pairs={{0,1},{1,2},{2,3},{3,4},{4,5},{5,6},{6,7},{7,8},{8,9},{9,10},{10,1... | collective-permute-start | bytes 12296 | tf_op jit(solution)/shard_map/ppermute | solution.py:531
  60.6 3.2 %collective-permute-start.2 = (f32[8,128]{1,0:T(8,128)S(1)}, f32[8,128]{1,0:T(8,128)S(1)}, u32[]{:S(2)}, u32[]{:S(2)}) collective-permute-start(f32[8,128]{1,0:T(8,128)S(1)} %shard_map.204.correction), channel_id=1, source_target_pairs={{1,0},{2,1},{3,2},{4,3},{5,4},{6,5},{7,6},{8,7},{9,8},{10,9},{11,1... | collective-permute-start | bytes 12296 | tf_op jit(solution)/shard_map/ppermute | solution.py:494
  66.2 7.4 %collective-permute-start.3 = (f32[72,128]{1,0:T(8,128)S(1)}, f32[72,128]{1,0:T(8,128)S(1)}, u32[]{:S(2)}, u32[]{:S(2)}) collective-permute-start(f32[72,128]{1,0:T(8,128)S(1)} %get-tuple-element.57), channel_id=1, source_target_pairs={{0,1},{1,2},{2,3},{3,4},{4,5},{5,6},{6,7},{7,8},{8,9},{9,10},{10,1... | collective-permute-start | bytes 110600 | tf_op jit(solution)/shard_map/ppermute | solution.py:494

commit v7 on v6

--- a/solution.py
+++ b/solution.py
@@ -381,13 +381,15 @@
 def solve_body(gathered, rows, owner, correction):
     tn = (((0,), (0,)), ((), ()))
     values = gathered[...]
-    row = lax.broadcasted_iota(jnp.int32, (256, 256), 0)
-    lane = lax.broadcasted_iota(jnp.int32, (256, 256), 1)
+    row = lax.broadcasted_iota(jnp.int32, (192, 256), 0)
+    lane = lax.broadcasted_iota(jnp.int32, (192, 256), 1)
     side = lax.axis_index("grp") // 32
-    holder = row // 8
-    target = jnp.where(row % 8 < 4, holder, holder + 1 - jnp.where(holder % 8 == 7, 8 * side, 0))
+    holder = (row * 171) >> 10
+    place = row - 6 * holder
+    target = jnp.where(place < 3, holder, holder + 1 - jnp.where(holder % 8 == 7, 8 * side, 0))
     column = jnp.where(lane < 192, lane, lane - 64)
-    match = (target == column % 64 // 2) & (row % 4 == column // 64)
+    part = jnp.where(place < 3, place, place - 3)
+    match = (target == column % 64 // 2) & (part == column // 64)
     need = None
     for q in range(2):
         pick = (match & (column % 2 == q)).astype(BF16)
@@ -528,17 +530,17 @@
         state, direction, rhs, keep_rows, halo, weighting, *shared, owner,
         scratch=scratch, cost=pl.CostEstimate(flops=20000000000, bytes_accessed=4 * 10**6, transcendentals=0),
     )
-    arrived = lax.ppermute(sums, ("grp", "mem"), ring())[4:8]
+    arrived = lax.ppermute(sums, ("grp", "mem"), ring())[4:7]
     wraps = lax.axis_index("mem") == 0
     total = jnp.concatenate(
-        [sums[0:4] + jnp.where(wraps, 0.0, arrived), jnp.where(wraps, arrived, 0.0)], axis=0
-    )
-    total = jnp.broadcast_to(total[None], (32, 8, 128)).reshape(256, 128)
+        [sums[0:3] + jnp.where(wraps, 0.0, arrived), jnp.where(wraps, arrived, 0.0)], axis=0
+    )
+    total = jnp.broadcast_to(total[None, :, None], (32, 6, 1, 128)).reshape(192, 1, 128)
     total, rows = lax.optimization_barrier((total, rows))
     sides = [list(range(32)), list(range(32, 64))]
     gathered = lax.all_to_all(
         total, "grp", split_axis=0, concat_axis=0, tiled=True, axis_index_groups=sides
-    )
+    ).reshape(192, 128)
     (correction,) = call(solve_body, [(8, 128)], gathered, rows, owner)
     right = shifted(correction, -1)
     field = (3, 4, 16, 128)

time: 74.6 us -> 75.1 us (level)
  transfers between devices with their start and end apart: 5 -> 5, of which waited for: 4 -> 4; matrix products, arithmetic and copies ran while one was open for 1% -> 2% of each run, Pallas kernels for 4% -> 4%
where the time goes in v7:
time: 75.1 us; the launch traced here: 74.8 us
  starting transfers between devices  34.1 us (45%)
  blocking collectives  16 us (21%)
  waiting for transfers between devices  14 us (19%)
  Pallas kernels  8.57 us (11%)
  local copies, waits for them, and re-layouts  1.31 us (2%)
    all_to_all x1, starting transfers between devices, shards(): lax.all_to_all(rows.reshape(576, 1, 128), 'grp', split_axis=0, concat_axi...  22.7 us
    all_to_all x1, blocking collectives, shards(): lax.all_to_all(total, 'grp', split_axis=0, concat_axis=0, tiled=True, axi...  16 us
    ppermute x3, starting transfers between devices, shifted(): return lax.ppermute(block, axes, route)  9.44 us
    ppermute x3, waiting for transfers between devices, shifted(): return lax.ppermute(block, axes, route)  6.12 us
    pallas_call x3, Pallas kernels, call(): pl.pallas_call(body, out_shape=[pltpu.VMEM(s, F32) for s in outs], in_spe...  5.79 us
    ppermute x1, waiting for transfers between devices, shards(): arrived = lax.ppermute(sums, ('grp', 'mem'), ring())[4:7]  4.2 us
    all_to_all x1, waiting for transfers between devices, shards(): lax.all_to_all(rows.reshape(576, 1, 128), 'grp', split_axis=0, concat_axi...  3.7 us
    pallas_call x1, Pallas kernels, prepare(): pl.pallas_call(functools.partial(prepare_body, len(operands)), out_shape=...  2.13 us
  transfers between devices with their start and end apart: 5, of which 4 were waited for; matrix products, arithmetic and copies ran while one was open for 2% of the time, Pallas kernels for 4%

profile of v7, /device:TPU:2, one launch (start us, length us, event | category | flops | bytes accessed | tf_op | source)
XLA Modules:
  0.0 74.8 jit_solution(13922421184700722355)
XLA Ops:
  0.6 2.1 %shard_map.202 = (f32[120,128]{1,0:T(8,128)S(1)}, f32[64,128]{1,0:T(8,128)S(1)}, f32[576,128]{1,0:T(8,128)}, f32[112,256]{1,0:T(8,128)S(1)}, f32[3,4,16,128]{3,2...) custom-call(f32[3,4,16,128]{3,2,1,0:T(8,128)} %refs_0_.1, ...), custom_call_target="tpu_custom_call" | custom-call | tf_op jit(solution)/shard_map/pallas_call | solution.py:237
  2.8 5.6 %collective-permute-start = (f32[120,128]{1,0:T(8,128)S(1)}, f32[120,128]{1,0:T(8,128)S(1)}, u32[]{:S(2)}, u32[]{:S(2)}) collective-permute-start(f32[120,128]{1,0:T(8,128)S(1)} %get-tuple-element.36), channel_id=1, source_target_pairs={{1,0},{2,1},{3,2},{4,3},{5,4},{6,5},{7,6},{8,7},{9,8},{10,9},{11,1... | collective-permute-start | bytes 184328 | tf_op jit(solution)/shard_map/ppermute | solution.py:496
  8.4 22.7 %all-to-all-start = ((f32[576,1,128]{2,1,0:T(1,128)}), f32[576,1,128]{2,1,0:T(1,128)S(1)}, u32[]{:S(2)}, u32[]{:S(2)}) async-start(f32[576,1,128]{2,1,0:T(1,128)} %bitcast.3), calls=%async_computation | async-start | bytes 589824 | tf_op jit(solution)/shard_map/all_to_all | solution.py:522
  31.1 0.0 collective-permute-done.halo
  31.1 2.8 %shard_map.203 = (f32[336,768]{1,0:T(8,128)S(1)}, f32[6,104,256]{2,1,0:T(8,128)S(1)}, f32[8,128]{1,0:T(8,128)S(1)}) custom-call(f32[3,4,16,128]{3,2,1,0:T(8,128)S(1)} %get-tuple-element.32.state, f32[3,4,16,128]{3,2,1,0:T(8,128)S(1)} %get-tuple-element.33.direction, f32[3,4,16,128]{3,2,1,0:T(8,128)S(1)} %get-tuple-element.34.rhs, ...), custom_call_target="tpu_custom_call" | custom-call | flops 20000000000 | bytes 4000000 | tf_op jit(solution)/shard_map/pallas_call | solution.py:157
  33.9 1.9 %collective-permute-start.1 = (f32[8,128]{1,0:T(8,128)S(1)}, f32[8,128]{1,0:T(8,128)S(1)}, u32[]{:S(2)}, u32[]{:S(2)}) collective-permute-start(f32[8,128]{1,0:T(8,128)S(1)} %get-tuple-element.49), channel_id=1, source_target_pairs={{0,1},{1,2},{2,3},{3,4},{4,5},{5,6},{6,7},{7,8},{8,9},{9,10},{10,1... | collective-permute-start | bytes 12296 | tf_op jit(solution)/shard_map/ppermute | solution.py:533
  35.8 4.2 %collective-permute-done.1 = f32[8,128]{1,0:T(8,128)S(1)} collective-permute-done((f32[8,128]{1,0:T(8,128)S(1)}, f32[8,128]{1,0:T(8,128)S(1)}, u32[]{:S(2)}, u32[]{:S(2)}) %collective-permute-start.1) | collective-permute-done | bytes 4128 | tf_op jit(solution)/shard_map/ppermute | solution.py:533
  40.1 0.7 broadcast_in_dim.19
  40.7 3.7 %all-to-all-done = f32[576,1,128]{2,1,0:T(1,128)S(1)} async-done(((f32[576,1,128]{2,1,0:T(1,128)}), f32[576,1,128]{2,1,0:T(1,128)S(1)}, u32[]{:S(2)}, u32[]{:S(2)}) %all-to-all-start) | async-done | bytes 294944 | tf_op jit(solution)/shard_map/all_to_all | solution.py:522
  44.4 16.0 %all_to_all.10 = f32[192,1,128]{2,1,0:T(1,128)S(1)} all-to-all(f32[192,1,128]{2,1,0:T(1,128)} %bitcast.13), channel_id=1, replica_groups={{0,16,32,48,64,80,96,112,128,144,160,176,192,208,224,240,256,272,288,30..., dimensions={0} | all-to-all | bytes 196608 | tf_op jit(solution)/shard_map/all_to_all | solution.py:541
  60.4 0.7 shard_map.204.correction
  61.1 1.9 %collective-permute-start.2 = (f32[8,128]{1,0:T(8,128)S(1)}, f32[8,128]{1,0:T(8,128)S(1)}, u32[]{:S(2)}, u32[]{:S(2)}) collective-permute-start(f32[8,128]{1,0:T(8,128)S(1)} %shard_map.204.correction), channel_id=1, source_target_pairs={{1,0},{2,1},{3,2},{4,3},{5,4},{6,5},{7,6},{8,7},{9,8},{10,9},{11,1... | collective-permute-start | bytes 12296 | tf_op jit(solution)/shard_map/ppermute | solution.py:496
  63.1 1.3 %collective-permute-done.2.right = f32[8,128]{1,0:T(8,128)S(1)} collective-permute-done((f32[8,128]{1,0:T(8,128)S(1)}, f32[8,128]{1,0:T(8,128)S(1)}, u32[]{:S(2)}, u32[]{:S(2)}) %collective-permute-start.2) | collective-permute-done | bytes 4128 | tf_op jit(solution)/shard_map/ppermute | solution.py:496
  64.4 2.3 %shard_map.205 = (f32[3,4,16,128]{3,2,1,0:T(8,128)S(1)}, f32[3,4,16,128]{3,2,1,0:T(8,128)S(1)}, f32[72,128]{1,0:T(8,128)S(1)}, f32[3,4,32]{2,1,0:T(4,128)S(1)}) custom-call(f32[8,128]{1,0:T(8,128)S(1)} %shard_map.204.correction, f32[8,128]{1,0:T(8,128)S(1)} %collective-permute-done.2.right, f32[336,768]{1,0:T(8,128)S(1)} %get-tuple-element.53.state_grad, ...), custom_call_target="tpu_custom_call" | custom-call | tf_op jit(solution)/shard_map/pallas_call | solution.py:157
  66.7 1.9 %collective-permute-start.3 = (f32[72,128]{1,0:T(8,128)S(1)}, f32[72,128]{1,0:T(8,128)S(1)}, u32[]{:S(2)}, u32[]{:S(2)}) collective-permute-start(f32[72,128]{1,0:T(8,128)S(1)} %get-tuple-element.57), channel_id=1, source_target_pairs={{0,1},{1,2},{2,3},{3,4},{4,5},{5,6},{6,7},{7,8},{8,9},{9,10},{10,1... | collective-permute-start | bytes 110600 | tf_op jit(solution)/shard_map/ppermute | solution.py:496
  68.7 0.6 copy.27
  69.3 4.8 %collective-permute-done.3.arrived = f32[72,128]{1,0:T(8,128)S(1)} collective-permute-done((f32[72,128]{1,0:T(8,128)S(1)}, f32[72,128]{1,0:T(8,128)S(1)}, u32[]{:S(2)}, u32[]{:S(2)}) %collective-permute-start.3) | collective-permute-done | bytes 36896 | tf_op jit(solution)/shard_map/ppermute | solution.py:496
  74.1 0.7 shard_map.206
  (3 shorter events, 0.0 us)
Async XLA Ops:
  2.8 28.3 %collective-permute-start = (f32[120,128]{1,0:T(8,128)S(1)}, f32[120,128]{1,0:T(8,128)S(1)}, u32[]{:S(2)}, u32[]{:S(2)}) collective-permute-start(f32[120,128]{1,0:T(8,128)S(1)} %get-tuple-element.36), channel_id=1, source_target_pairs={{1,0},{2,1},{3,2},{4,3},{5,4},{6,5},{7,6},{8,7},{9,8},{10,9},{11,1... | collective-permute-start | bytes 184328 | tf_op jit(solution)/shard_map/ppermute | solution.py:496
  8.4 36.1 %all-to-all-start = ((f32[576,1,128]{2,1,0:T(1,128)}), f32[576,1,128]{2,1,0:T(1,128)S(1)}, u32[]{:S(2)}, u32[]{:S(2)}) async-start(f32[576,1,128]{2,1,0:T(1,128)} %bitcast.3), calls=%async_computation | async-start | bytes 589824 | tf_op jit(solution)/shard_map/all_to_all | solution.py:522
  33.9 6.2 %collective-permute-start.1 = (f32[8,128]{1,0:T(8,128)S(1)}, f32[8,128]{1,0:T(8,128)S(1)}, u32[]{:S(2)}, u32[]{:S(2)}) collective-permute-start(f32[8,128]{1,0:T(8,128)S(1)} %get-tuple-element.49), channel_id=1, source_target_pairs={{0,1},{1,2},{2,3},{3,4},{4,5},{5,6},{6,7},{7,8},{8,9},{9,10},{10,1... | collective-permute-start | bytes 12296 | tf_op jit(solution)/shard_map/ppermute | solution.py:533
  61.1 3.2 %collective-permute-start.2 = (f32[8,128]{1,0:T(8,128)S(1)}, f32[8,128]{1,0:T(8,128)S(1)}, u32[]{:S(2)}, u32[]{:S(2)}) collective-permute-start(f32[8,128]{1,0:T(8,128)S(1)} %shard_map.204.correction), channel_id=1, source_target_pairs={{1,0},{2,1},{3,2},{4,3},{5,4},{6,5},{7,6},{8,7},{9,8},{10,9},{11,1... | collective-permute-start | bytes 12296 | tf_op jit(solution)/shard_map/ppermute | solution.py:496
  66.7 7.4 %collective-permute-start.3 = (f32[72,128]{1,0:T(8,128)S(1)}, f32[72,128]{1,0:T(8,128)S(1)}, u32[]{:S(2)}, u32[]{:S(2)}) collective-permute-start(f32[72,128]{1,0:T(8,128)S(1)} %get-tuple-element.57), channel_id=1, source_target_pairs={{0,1},{1,2},{2,3},{3,4},{4,5},{5,6},{6,7},{7,8},{8,9},{9,10},{10,1... | collective-permute-start | bytes 110600 | tf_op jit(solution)/shard_map/ppermute | solution.py:496

commit v8 on v6

--- a/solution.py
+++ b/solution.py
@@ -381,13 +381,10 @@
 def solve_body(gathered, rows, owner, correction):
     tn = (((0,), (0,)), ((), ()))
     values = gathered[...]
-    row = lax.broadcasted_iota(jnp.int32, (256, 256), 0)
-    lane = lax.broadcasted_iota(jnp.int32, (256, 256), 1)
-    side = lax.axis_index("grp") // 32
-    holder = row // 8
-    target = jnp.where(row % 8 < 4, holder, holder + 1 - jnp.where(holder % 8 == 7, 8 * side, 0))
+    row = lax.broadcasted_iota(jnp.int32, (128, 256), 0)
+    lane = lax.broadcasted_iota(jnp.int32, (128, 256), 1)
     column = jnp.where(lane < 192, lane, lane - 64)
-    match = (target == column % 64 // 2) & (row % 4 == column // 64)
+    match = (row // 4 == column % 64 // 2) & (row % 4 == column // 64)
     need = None
     for q in range(2):
         pick = (match & (column % 2 == q)).astype(BF16)
@@ -492,18 +489,6 @@
     count = lax.axis_size(axes)
     route = [(i - distance, i) for i in range(count) if 0 <= i - distance < count]
     return lax.ppermute(block, axes, route)
-
-
-def ring():
-    groups, members = lax.axis_size("grp"), lax.axis_size("mem")
-    route = []
-    for g in range(groups):
-        route += [(g * members + m, g * members + m + 1) for m in range(members - 1)]
-        last = g >= groups // 2 - 1 and g % 8 == 7
-        to = g + 8 if last else g
-        if to < groups:
-            route.append((g * members + members - 1, to * members))
-    return route
 
 
 def shards(state, direction, rhs, clamp, stiffness, coarse_owner, coarse_inverse):
@@ -528,12 +513,8 @@
         state, direction, rhs, keep_rows, halo, weighting, *shared, owner,
         scratch=scratch, cost=pl.CostEstimate(flops=20000000000, bytes_accessed=4 * 10**6, transcendentals=0),
     )
-    arrived = lax.ppermute(sums, ("grp", "mem"), ring())[4:8]
-    wraps = lax.axis_index("mem") == 0
-    total = jnp.concatenate(
-        [sums[0:4] + jnp.where(wraps, 0.0, arrived), jnp.where(wraps, arrived, 0.0)], axis=0
-    )
-    total = jnp.broadcast_to(total[None], (32, 8, 128)).reshape(256, 128)
+    total = sums[0:4] + shifted(sums, 1)[4:8]
+    total = jnp.broadcast_to(total[None], (32, 4, 128)).reshape(128, 128)
     total, rows = lax.optimization_barrier((total, rows))
     sides = [list(range(32)), list(range(32, 64))]
     gathered = lax.all_to_all(

time: 74.6 us -> 76.1 us (1.020)
  the two profiles are of different devices: /device:TPU:2 before, /device:TPU:128 now
where the time goes in v8:
time: 76.1 us; the launch traced here: 75.8 us
  starting transfers between devices  32.3 us (42%)
  blocking collectives  17.2 us (23%)
  waiting for transfers between devices  16.4 us (22%)
  Pallas kernels  8.53 us (11%)
    all_to_all x1, starting transfers between devices, shards(): lax.all_to_all(rows.reshape(576, 1, 128), 'grp', split_axis=0, concat_axi...  20.4 us
    all_to_all x1, blocking collectives, shards(): lax.all_to_all(total, 'grp', split_axis=0, concat_axis=0, tiled=True, axi...  17.2 us
    ppermute x4, waiting for transfers between devices, shifted(): return lax.ppermute(block, axes, route)  15.4 us
    ppermute x4, starting transfers between devices, shifted(): return lax.ppermute(block, axes, route)  11.9 us
    pallas_call x3, Pallas kernels, call(): pl.pallas_call(body, out_shape=[pltpu.VMEM(s, F32) for s in outs], in_spe...  5.76 us
    pallas_call x1, Pallas kernels, prepare(): pl.pallas_call(functools.partial(prepare_body, len(operands)), out_shape=...  2.12 us
  transfers between devices with their start and end apart: 5, of which 4 were waited for; matrix products, arithmetic and copies ran while one was open for 1% of the time, Pallas kernels for 4%

profile of v8, /device:TPU:128, one launch (start us, length us, event | category | flops | bytes accessed | tf_op | source)
XLA Modules:
  0.0 75.8 jit_solution(1677165996297692046)
XLA Ops:
  0.6 2.1 %shard_map.202 = (f32[120,128]{1,0:T(8,128)S(1)}, f32[64,128]{1,0:T(8,128)S(1)}, f32[576,128]{1,0:T(8,128)}, f32[112,256]{1,0:T(8,128)S(1)}, f32[3,4,16,128]{3,2...) custom-call(f32[3,4,16,128]{3,2,1,0:T(8,128)} %refs_0_.1, ...), custom_call_target="tpu_custom_call" | custom-call | tf_op jit(solution)/shard_map/pallas_call | solution.py:237
  2.8 6.1 %collective-permute-start = (f32[120,128]{1,0:T(8,128)S(1)}, f32[120,128]{1,0:T(8,128)S(1)}, u32[]{:S(2)}, u32[]{:S(2)}) collective-permute-start(f32[120,128]{1,0:T(8,128)S(1)} %get-tuple-element.36), channel_id=1, source_target_pairs={{1,0},{2,1},{3,2},{4,3},{5,4},{6,5},{7,6},{8,7},{9,8},{10,9},{11,1... | collective-permute-start | bytes 184328 | tf_op jit(solution)/shard_map/ppermute | solution.py:491
  8.9 20.4 %all-to-all-start = ((f32[576,1,128]{2,1,0:T(1,128)}), f32[576,1,128]{2,1,0:T(1,128)S(1)}, u32[]{:S(2)}, u32[]{:S(2)}) async-start(f32[576,1,128]{2,1,0:T(1,128)} %bitcast.4), calls=%async_computation | async-start | bytes 589824 | tf_op jit(solution)/shard_map/all_to_all | solution.py:505
  29.3 0.0 collective-permute-done.halo
  29.3 2.8 %shard_map.203 = (f32[336,768]{1,0:T(8,128)S(1)}, f32[6,104,256]{2,1,0:T(8,128)S(1)}, f32[8,128]{1,0:T(8,128)S(1)}) custom-call(f32[3,4,16,128]{3,2,1,0:T(8,128)S(1)} %get-tuple-element.32.state, f32[3,4,16,128]{3,2,1,0:T(8,128)S(1)} %get-tuple-element.33.direction, f32[3,4,16,128]{3,2,1,0:T(8,128)S(1)} %get-tuple-element.34.rhs, ...), custom_call_target="tpu_custom_call" | custom-call | flops 20000000000 | bytes 4000000 | tf_op jit(solution)/shard_map/pallas_call | solution.py:157
  32.1 1.9 %collective-permute-start.1 = (f32[8,128]{1,0:T(8,128)S(1)}, f32[8,128]{1,0:T(8,128)S(1)}, u32[]{:S(2)}, u32[]{:S(2)}) collective-permute-start(f32[8,128]{1,0:T(8,128)S(1)} %get-tuple-element.49), channel_id=1, source_target_pairs={{0,1},{1,2},{2,3},{3,4},{4,5},{5,6},{6,7},{7,8},{8,9},{9,10},{10,1... | collective-permute-start | bytes 12296 | tf_op jit(solution)/shard_map/ppermute | solution.py:491
  34.0 7.2 %collective-permute-done.1 = f32[8,128]{1,0:T(8,128)S(1)} collective-permute-done((f32[8,128]{1,0:T(8,128)S(1)}, f32[8,128]{1,0:T(8,128)S(1)}, u32[]{:S(2)}, u32[]{:S(2)}) %collective-permute-start.1) | collective-permute-done | bytes 4128 | tf_op jit(solution)/shard_map/ppermute | solution.py:491
  41.3 0.9 %all-to-all-done = f32[576,1,128]{2,1,0:T(1,128)S(1)} async-done(((f32[576,1,128]{2,1,0:T(1,128)}), f32[576,1,128]{2,1,0:T(1,128)S(1)}, u32[]{:S(2)}, u32[]{:S(2)}) %all-to-all-start) | async-done | bytes 294944 | tf_op jit(solution)/shard_map/all_to_all | solution.py:505
  42.2 17.2 %all_to_all.16 = f32[32,4,128]{2,1,0:T(4,128)S(1)} all-to-all(f32[32,4,128]{2,1,0:T(4,128)S(1)} %broadcast_in_dim.4), channel_id=1, replica_groups={{0,16,32,48,64,80,96,112,128,144,160,176,192,208,224,240,256,272,288,30..., dimensions={0} | all-to-all | bytes 131072 | tf_op jit(solution)/shard_map/all_to_all | solution.py:520
  59.4 0.7 shard_map.204.correction
  60.1 1.9 %collective-permute-start.2 = (f32[8,128]{1,0:T(8,128)S(1)}, f32[8,128]{1,0:T(8,128)S(1)}, u32[]{:S(2)}, u32[]{:S(2)}) collective-permute-start(f32[8,128]{1,0:T(8,128)S(1)} %shard_map.204.correction), channel_id=1, source_target_pairs={{1,0},{2,1},{3,2},{4,3},{5,4},{6,5},{7,6},{8,7},{9,8},{10,9},{11,1... | collective-permute-start | bytes 12296 | tf_op jit(solution)/shard_map/ppermute | solution.py:491
  62.0 1.3 %collective-permute-done.2.right = f32[8,128]{1,0:T(8,128)S(1)} collective-permute-done((f32[8,128]{1,0:T(8,128)S(1)}, f32[8,128]{1,0:T(8,128)S(1)}, u32[]{:S(2)}, u32[]{:S(2)}) %collective-permute-start.2) | collective-permute-done | bytes 4128 | tf_op jit(solution)/shard_map/ppermute | solution.py:491
  63.3 2.3 %shard_map.205 = (f32[3,4,16,128]{3,2,1,0:T(8,128)S(1)}, f32[3,4,16,128]{3,2,1,0:T(8,128)S(1)}, f32[72,128]{1,0:T(8,128)S(1)}, f32[3,4,32]{2,1,0:T(4,128)S(1)}) custom-call(f32[8,128]{1,0:T(8,128)S(1)} %shard_map.204.correction, f32[8,128]{1,0:T(8,128)S(1)} %collective-permute-done.2.right, f32[336,768]{1,0:T(8,128)S(1)} %get-tuple-element.53.state_grad, ...), custom_call_target="tpu_custom_call" | custom-call | tf_op jit(solution)/shard_map/pallas_call | solution.py:157
  65.7 1.9 %collective-permute-start.3 = (f32[72,128]{1,0:T(8,128)S(1)}, f32[72,128]{1,0:T(8,128)S(1)}, u32[]{:S(2)}, u32[]{:S(2)}) collective-permute-start(f32[72,128]{1,0:T(8,128)S(1)} %get-tuple-element.57), channel_id=1, source_target_pairs={{0,1},{1,2},{2,3},{3,4},{4,5},{5,6},{6,7},{7,8},{8,9},{9,10},{10,1... | collective-permute-start | bytes 110600 | tf_op jit(solution)/shard_map/ppermute | solution.py:491
  67.6 0.6 copy.25
  68.2 6.9 %collective-permute-done.3.arrived = f32[72,128]{1,0:T(8,128)S(1)} collective-permute-done((f32[72,128]{1,0:T(8,128)S(1)}, f32[72,128]{1,0:T(8,128)S(1)}, u32[]{:S(2)}, u32[]{:S(2)}) %collective-permute-start.3) | collective-permute-done | bytes 36896 | tf_op jit(solution)/shard_map/ppermute | solution.py:491
  75.2 0.7 shard_map.206
  (2 shorter events, 0.0 us)
Async XLA Ops:
  2.8 26.6 %collective-permute-start = (f32[120,128]{1,0:T(8,128)S(1)}, f32[120,128]{1,0:T(8,128)S(1)}, u32[]{:S(2)}, u32[]{:S(2)}) collective-permute-start(f32[120,128]{1,0:T(8,128)S(1)} %get-tuple-element.36), channel_id=1, source_target_pairs={{1,0},{2,1},{3,2},{4,3},{5,4},{6,5},{7,6},{8,7},{9,8},{10,9},{11,1... | collective-permute-start | bytes 184328 | tf_op jit(solution)/shard_map/ppermute | solution.py:491
  8.9 33.3 %all-to-all-start = ((f32[576,1,128]{2,1,0:T(1,128)}), f32[576,1,128]{2,1,0:T(1,128)S(1)}, u32[]{:S(2)}, u32[]{:S(2)}) async-start(f32[576,1,128]{2,1,0:T(1,128)} %bitcast.4), calls=%async_computation | async-start | bytes 589824 | tf_op jit(solution)/shard_map/all_to_all | solution.py:505
  32.1 9.2 %collective-permute-start.1 = (f32[8,128]{1,0:T(8,128)S(1)}, f32[8,128]{1,0:T(8,128)S(1)}, u32[]{:S(2)}, u32[]{:S(2)}) collective-permute-start(f32[8,128]{1,0:T(8,128)S(1)} %get-tuple-element.49), channel_id=1, source_target_pairs={{0,1},{1,2},{2,3},{3,4},{4,5},{5,6},{6,7},{7,8},{8,9},{9,10},{10,1... | collective-permute-start | bytes 12296 | tf_op jit(solution)/shard_map/ppermute | solution.py:491
  60.1 3.2 %collective-permute-start.2 = (f32[8,128]{1,0:T(8,128)S(1)}, f32[8,128]{1,0:T(8,128)S(1)}, u32[]{:S(2)}, u32[]{:S(2)}) collective-permute-start(f32[8,128]{1,0:T(8,128)S(1)} %shard_map.204.correction), channel_id=1, source_target_pairs={{1,0},{2,1},{3,2},{4,3},{5,4},{6,5},{7,6},{8,7},{9,8},{10,9},{11,1... | collective-permute-start | bytes 12296 | tf_op jit(solution)/shard_map/ppermute | solution.py:491
  65.7 9.5 %collective-permute-start.3 = (f32[72,128]{1,0:T(8,128)S(1)}, f32[72,128]{1,0:T(8,128)S(1)}, u32[]{:S(2)}, u32[]{:S(2)}) collective-permute-start(f32[72,128]{1,0:T(8,128)S(1)} %get-tuple-element.57), channel_id=1, source_target_pairs={{0,1},{1,2},{2,3},{3,4},{4,5},{5,6},{6,7},{7,8},{8,9},{9,10},{10,1... | collective-permute-start | bytes 110600 | tf_op jit(solution)/shard_map/ppermute | solution.py:491

commit v9 on v6

--- a/solution.py
+++ b/solution.py
@@ -526,7 +526,7 @@
         first_body,
         [big, (6, LIVE, WIDE), (8, 128)],
         state, direction, rhs, keep_rows, halo, weighting, *shared, owner,
-        scratch=scratch, cost=pl.CostEstimate(flops=20000000000, bytes_accessed=4 * 10**6, transcendentals=0),
+        scratch=scratch, cost=None,
     )
     arrived = lax.ppermute(sums, ("grp", "mem"), ring())[4:8]
     wraps = lax.axis_index("mem") == 0

time: 74.6 us -> 75.9 us (1.017)
  blocking collectives: 15.5 us -> 16.5 us
  waiting for transfers between devices: 14.7 us -> 13.8 us
    all_to_all x1, blocking collectives: 15.5 us -> 16.5 us  [shards(): lax.all_to_all(total, 'grp', split_axis=0, concat_axis=0, tiled=True, axi...]
    all_to_all x1, waiting for transfers between devices: 4.34 us -> 3.51 us  [shards(): lax.all_to_all(rows.reshape(576, 1, 128), 'grp', split_axis=0, concat_axi...]
  transfers between devices with their start and end apart: 5 -> 5, of which waited for: 4 -> 4; matrix products, arithmetic and copies ran while one was open for 1% -> 2% of each run, Pallas kernels for 4% -> 4%
where the time goes in v9:
time: 75.9 us; the launch traced here: 75.5 us
  starting transfers between devices  34.1 us (45%)
  blocking collectives  16.5 us (22%)
  waiting for transfers between devices  13.8 us (18%)
  Pallas kernels  9 us (12%)
  local copies, waits for them, and re-layouts  1.32 us (2%)
    all_to_all x1, starting transfers between devices, shards(): lax.all_to_all(rows.reshape(576, 1, 128), 'grp', split_axis=0, concat_axi...  22.7 us
    all_to_all x1, blocking collectives, shards(): lax.all_to_all(total, 'grp', split_axis=0, concat_axis=0, tiled=True, axi...  16.5 us
    ppermute x3, starting transfers between devices, shifted(): return lax.ppermute(block, axes, route)  9.44 us
    pallas_call x3, Pallas kernels, call(): pl.pallas_call(body, out_shape=[pltpu.VMEM(s, F32) for s in outs], in_spe...  6.23 us
    ppermute x3, waiting for transfers between devices, shifted(): return lax.ppermute(block, axes, route)  6.12 us
    ppermute x1, waiting for transfers between devices, shards(): arrived = lax.ppermute(sums, ('grp', 'mem'), ring())[4:8]  4.2 us
    all_to_all x1, waiting for transfers between devices, shards(): lax.all_to_all(rows.reshape(576, 1, 128), 'grp', split_axis=0, concat_axi...  3.51 us
    pallas_call x1, Pallas kernels, prepare(): pl.pallas_call(functools.partial(prepare_body, len(operands)), out_shape=...  2.13 us
  transfers between devices with their start and end apart: 5, of which 4 were waited for; matrix products, arithmetic and copies ran while one was open for 2% of the time, Pallas kernels for 4%

profile of v9, /device:TPU:2, one launch (start us, length us, event | category | flops | bytes accessed | tf_op | source)
XLA Modules:
  0.0 75.5 jit_solution(17451771752987684796)
XLA Ops:
  0.6 2.1 %shard_map.202 = (f32[120,128]{1,0:T(8,128)S(1)}, f32[64,128]{1,0:T(8,128)S(1)}, f32[576,128]{1,0:T(8,128)}, f32[112,256]{1,0:T(8,128)S(1)}, f32[3,4,16,128]{3,2...) custom-call(f32[3,4,16,128]{3,2,1,0:T(8,128)} %refs_0_.1, ...), custom_call_target="tpu_custom_call" | custom-call | tf_op jit(solution)/shard_map/pallas_call | solution.py:237
  2.8 5.6 %collective-permute-start = (f32[120,128]{1,0:T(8,128)S(1)}, f32[120,128]{1,0:T(8,128)S(1)}, u32[]{:S(2)}, u32[]{:S(2)}) collective-permute-start(f32[120,128]{1,0:T(8,128)S(1)} %get-tuple-element.36), channel_id=1, source_target_pairs={{1,0},{2,1},{3,2},{4,3},{5,4},{6,5},{7,6},{8,7},{9,8},{10,9},{11,1... | collective-permute-start | bytes 184328 | tf_op jit(solution)/shard_map/ppermute | solution.py:494
  8.4 22.7 %all-to-all-start = ((f32[576,1,128]{2,1,0:T(1,128)}), f32[576,1,128]{2,1,0:T(1,128)S(1)}, u32[]{:S(2)}, u32[]{:S(2)}) async-start(f32[576,1,128]{2,1,0:T(1,128)} %bitcast.4), calls=%async_computation | async-start | bytes 589824 | tf_op jit(solution)/shard_map/all_to_all | solution.py:520
  31.1 0.0 collective-permute-done.halo
  31.1 2.9 %shard_map.203 = (f32[336,768]{1,0:T(8,128)S(1)}, f32[6,104,256]{2,1,0:T(8,128)S(1)}, f32[8,128]{1,0:T(8,128)S(1)}) custom-call(f32[3,4,16,128]{3,2,1,0:T(8,128)S(1)} %get-tuple-element.32.state, f32[3,4,16,128]{3,2,1,0:T(8,128)S(1)} %get-tuple-element.33.direction, f32[3,4,16,128]{3,2,1,0:T(8,128)S(1)} %get-tuple-element.34.rhs, ...), custom_call_target="tpu_custom_call" | custom-call | tf_op jit(solution)/shard_map/pallas_call | solution.py:157
  34.1 1.9 %collective-permute-start.1 = (f32[8,128]{1,0:T(8,128)S(1)}, f32[8,128]{1,0:T(8,128)S(1)}, u32[]{:S(2)}, u32[]{:S(2)}) collective-permute-start(f32[8,128]{1,0:T(8,128)S(1)} %get-tuple-element.49), channel_id=1, source_target_pairs={{0,1},{1,2},{2,3},{3,4},{4,5},{5,6},{6,7},{7,8},{8,9},{9,10},{10,1... | collective-permute-start | bytes 12296 | tf_op jit(solution)/shard_map/ppermute | solution.py:531
  36.0 4.2 %collective-permute-done.1 = f32[8,128]{1,0:T(8,128)S(1)} collective-permute-done((f32[8,128]{1,0:T(8,128)S(1)}, f32[8,128]{1,0:T(8,128)S(1)}, u32[]{:S(2)}, u32[]{:S(2)}) %collective-permute-start.1) | collective-permute-done | bytes 4128 | tf_op jit(solution)/shard_map/ppermute | solution.py:531
  40.2 0.7 broadcast_bitcast_fusion
  40.9 3.5 %all-to-all-done = f32[576,1,128]{2,1,0:T(1,128)S(1)} async-done(((f32[576,1,128]{2,1,0:T(1,128)}), f32[576,1,128]{2,1,0:T(1,128)S(1)}, u32[]{:S(2)}, u32[]{:S(2)}) %all-to-all-start) | async-done | bytes 294944 | tf_op jit(solution)/shard_map/all_to_all | solution.py:520
  44.4 16.5 %all_to_all.16 = f32[32,8,128]{2,1,0:T(8,128)S(1)} all-to-all(f32[32,8,128]{2,1,0:T(8,128)} %bitcast.15), channel_id=1, replica_groups={{0,16,32,48,64,80,96,112,128,144,160,176,192,208,224,240,256,272,288,30..., dimensions={0} | all-to-all | bytes 262144 | tf_op jit(solution)/shard_map/all_to_all | solution.py:539
  60.9 0.7 shard_map.204.correction
  61.7 1.9 %collective-permute-start.2 = (f32[8,128]{1,0:T(8,128)S(1)}, f32[8,128]{1,0:T(8,128)S(1)}, u32[]{:S(2)}, u32[]{:S(2)}) collective-permute-start(f32[8,128]{1,0:T(8,128)S(1)} %shard_map.204.correction), channel_id=1, source_target_pairs={{1,0},{2,1},{3,2},{4,3},{5,4},{6,5},{7,6},{8,7},{9,8},{10,9},{11,1... | collective-permute-start | bytes 12296 | tf_op jit(solution)/shard_map/ppermute | solution.py:494
  63.6 1.3 %collective-permute-done.2.right = f32[8,128]{1,0:T(8,128)S(1)} collective-permute-done((f32[8,128]{1,0:T(8,128)S(1)}, f32[8,128]{1,0:T(8,128)S(1)}, u32[]{:S(2)}, u32[]{:S(2)}) %collective-permute-start.2) | collective-permute-done | bytes 4128 | tf_op jit(solution)/shard_map/ppermute | solution.py:494
  64.9 2.6 %shard_map.205 = (f32[3,4,16,128]{3,2,1,0:T(8,128)S(1)}, f32[3,4,16,128]{3,2,1,0:T(8,128)S(1)}, f32[72,128]{1,0:T(8,128)S(1)}, f32[3,4,32]{2,1,0:T(4,128)S(1)}) custom-call(f32[8,128]{1,0:T(8,128)S(1)} %shard_map.204.correction, f32[8,128]{1,0:T(8,128)S(1)} %collective-permute-done.2.right, f32[336,768]{1,0:T(8,128)S(1)} %get-tuple-element.53.state_grad, ...), custom_call_target="tpu_custom_call" | custom-call | tf_op jit(solution)/shard_map/pallas_call | solution.py:157
  67.5 1.9 %collective-permute-start.3 = (f32[72,128]{1,0:T(8,128)S(1)}, f32[72,128]{1,0:T(8,128)S(1)}, u32[]{:S(2)}, u32[]{:S(2)}) collective-permute-start(f32[72,128]{1,0:T(8,128)S(1)} %get-tuple-element.57), channel_id=1, source_target_pairs={{0,1},{1,2},{2,3},{3,4},{4,5},{5,6},{6,7},{7,8},{8,9},{9,10},{10,1... | collective-permute-start | bytes 110600 | tf_op jit(solution)/shard_map/ppermute | solution.py:494
  69.4 0.6 copy.25
  70.0 4.8 %collective-permute-done.3.arrived = f32[72,128]{1,0:T(8,128)S(1)} collective-permute-done((f32[72,128]{1,0:T(8,128)S(1)}, f32[72,128]{1,0:T(8,128)S(1)}, u32[]{:S(2)}, u32[]{:S(2)}) %collective-permute-start.3) | collective-permute-done | bytes 36896 | tf_op jit(solution)/shard_map/ppermute | solution.py:494
  74.9 0.7 shard_map.206
  (2 shorter events, 0.0 us)
Async XLA Ops:
  2.8 28.3 %collective-permute-start = (f32[120,128]{1,0:T(8,128)S(1)}, f32[120,128]{1,0:T(8,128)S(1)}, u32[]{:S(2)}, u32[]{:S(2)}) collective-permute-start(f32[120,128]{1,0:T(8,128)S(1)} %get-tuple-element.36), channel_id=1, source_target_pairs={{1,0},{2,1},{3,2},{4,3},{5,4},{6,5},{7,6},{8,7},{9,8},{10,9},{11,1... | collective-permute-start | bytes 184328 | tf_op jit(solution)/shard_map/ppermute | solution.py:494
  8.4 36.1 %all-to-all-start = ((f32[576,1,128]{2,1,0:T(1,128)}), f32[576,1,128]{2,1,0:T(1,128)S(1)}, u32[]{:S(2)}, u32[]{:S(2)}) async-start(f32[576,1,128]{2,1,0:T(1,128)} %bitcast.4), calls=%async_computation | async-start | bytes 589824 | tf_op jit(solution)/shard_map/all_to_all | solution.py:520
  34.1 6.2 %collective-permute-start.1 = (f32[8,128]{1,0:T(8,128)S(1)}, f32[8,128]{1,0:T(8,128)S(1)}, u32[]{:S(2)}, u32[]{:S(2)}) collective-permute-start(f32[8,128]{1,0:T(8,128)S(1)} %get-tuple-element.49), channel_id=1, source_target_pairs={{0,1},{1,2},{2,3},{3,4},{4,5},{5,6},{6,7},{7,8},{8,9},{9,10},{10,1... | collective-permute-start | bytes 12296 | tf_op jit(solution)/shard_map/ppermute | solution.py:531
  61.7 3.2 %collective-permute-start.2 = (f32[8,128]{1,0:T(8,128)S(1)}, f32[8,128]{1,0:T(8,128)S(1)}, u32[]{:S(2)}, u32[]{:S(2)}) collective-permute-start(f32[8,128]{1,0:T(8,128)S(1)} %shard_map.204.correction), channel_id=1, source_target_pairs={{1,0},{2,1},{3,2},{4,3},{5,4},{6,5},{7,6},{8,7},{9,8},{10,9},{11,1... | collective-permute-start | bytes 12296 | tf_op jit(solution)/shard_map/ppermute | solution.py:494
  67.5 7.4 %collective-permute-start.3 = (f32[72,128]{1,0:T(8,128)S(1)}, f32[72,128]{1,0:T(8,128)S(1)}, u32[]{:S(2)}, u32[]{:S(2)}) collective-permute-start(f32[72,128]{1,0:T(8,128)S(1)} %get-tuple-element.57), channel_id=1, source_target_pairs={{0,1},{1,2},{2,3},{3,4},{4,5},{5,6},{6,7},{7,8},{8,9},{9,10},{10,1... | collective-permute-start | bytes 110600 | tf_op jit(solution)/shard_map/ppermute | solution.py:494
